TPU v7x, 32 devices: a whole 2x2x4 slice. The times are simulated.
32 devices in a mesh: task: 2 (over y), fsdp: 8 (over z, x), view: 2 (over core).
Axes of the slice: x: 2, y: 2, z: 4, core: 2. Of those that a mesh axis runs over, the one named last changes fastest.
Arguments:
- train_input: bfloat16 [4, 2048, 8192], P(('task', 'view'), 'fsdp'), parts along dimension 0, may hold values from -6 to 6
- train_query: bfloat16 [4, 2048, 4096], P(('task', 'view'), 'fsdp'), parts along dimension 0, may hold values from -120 to 120, as said below
- train_keys: bfloat16 [4, 2048, 512], P(('task', 'view'), 'fsdp'), parts along dimension 0, may hold values from -6 to 6, as said below
- train_target: bfloat16 [4, 2048, 4096], P(('task', 'view'), 'fsdp'), parts along dimension 0, may hold values from -6 to 6
- train_segments: int32 [4, 8, 256], P(('task', 'view'), 'fsdp'), parts along dimension 0, may hold values from 0 to 7, never falling along the last dimension, each value on 1 to 64 neighbouring positions
- value_weight: bfloat16 [8192, 512], P('fsdp'), may hold values from -0.0625 to 0.0625
- adapter_down: float32 [16384, 64], P(('task', 'fsdp')), parts along dimension 0, may hold values from -0.0625 to 0.0625
- adapter_up: float32 [128, 512], P('task'), parts along dimension 0, may hold values from -0.75 to 0.75
- score_input: bfloat16 [4, 512, 8192], P(('task', 'view'), 'fsdp'), parts along dimension 0, may hold values from -6 to 6
- score_query: bfloat16 [4, 512, 4096], P(('task', 'view'), 'fsdp'), parts along dimension 0, may hold values from -120 to 120, as said below
- score_keys: bfloat16 [4, 512, 512], P(('task', 'view'), 'fsdp'), parts along dimension 0, may hold values from -6 to 6, as said below
- score_segments: int32 [4, 8, 64], P(('task', 'view'), 'fsdp'), parts along dimension 0, may hold values from 0 to 3, never falling along the last dimension, each value on 1 to 32 neighbouring positions
Outputs:
- new_down: float32 [16384, 64], P(('task', 'fsdp')), parts along dimension 0
- new_up: float32 [128, 512], P('task'), parts along dimension 0
- scored: bfloat16 [4, 512, 4096], P(('task', 'view'), 'fsdp'), parts along dimension 0
There are 2 independent parts, one for each index of `task`. A program takes and returns all parts, laid end to end along the dimension named above; an argument that names none is the same for every part. Nothing has to cross between parts.
Inputs may be any that keep to these rules, and one draw needn't show every extreme that they name: `train_query`: query features of each token. `train_keys`: key features of each token. `score_query`: query features of each token. `score_keys`: key features of each token. `train_segments`: ids never decrease along a packed row. `score_segments`: ids never decrease along a packed row.
All inputs are finite; a program needn't handle non-finite values.
Results may differ from a plain program's by a relative error of at most 0.01.
Values may be sent and summed in bfloat16 or wider, within the bound.
No kernel may reach another device: no remote copies, remote signals or barrier semaphores. Data moves between devices by JAX's collectives and lax.ppermute only.
A program may use at most 128 MiB of HBM per device.

v0:
```python
import functools

import jax
import jax.numpy as jnp
from jax import lax
from jax.experimental import pallas as pl
from jax.experimental.pallas import tpu as pltpu
from jax.sharding import PartitionSpec as P


Q_HEADS = 32
KV_HEADS = 4
HEAD_DIM = 128
GROUP = 8
VALUE_WIDTH = 512
RANK = 64
UP_ROWS = 8

adapter_scale_factor = 0.5
rate_down = 2e-05
rate_up = 0.001


F32 = jnp.float32
BF16 = jnp.bfloat16
VM = pl.BlockSpec(memory_space=pltpu.VMEM)
SM = pl.BlockSpec(memory_space=pltpu.SMEM)
ANY = pl.BlockSpec(memory_space=pl.ANY)
VMEM_GRANT = 16 * 2**20


def dot_nn(a, b):
    return lax.dot_general(a, b, (((1,), (0,)), ((), ())), preferred_element_type=F32)


def dot_nt(a, b):
    return lax.dot_general(a, b, (((1,), (1,)), ((), ())), preferred_element_type=F32)


def cost(flops, nbytes):
    return pl.CostEstimate(flops=int(flops), bytes_accessed=int(nbytes), transcendentals=0)


def near(array):
    return pltpu.with_memory_space_constraint(array, pltpu.VMEM)


def call(kernel, outs, scalars, operands, scratch=(), flops=1e6, final=(), deps=()):
    n, d = len(operands), len(deps)

    def whole(scalar_ref, *refs):
        kernel(scalar_ref, refs[:n], refs[n + d : n + d + len(outs)], refs[n + d + len(outs) :])

    return pl.pallas_call(
        whole,
        out_shape=[jax.ShapeDtypeStruct(*o) if i in final else pltpu.VMEM(*o) for i, o in enumerate(outs)],
        in_specs=[SM] + [VM] * n + [ANY] * d,
        out_specs=[VM] * len(outs),
        scratch_shapes=list(scratch),
        cost_estimate=cost(flops, 2**20),
        compiler_params=pltpu.CompilerParams(vmem_limit_bytes=VMEM_GRANT),
    )(scalars, *[near(a) for a in operands], *deps)


def lanes_at(start, size):
    return pl.ds(pl.multiple_of(start, 128), size)


def train_head_kernel(g, s, refs, outs, scratch):
    seg_row, seg_col, q_ref, k_ref, t_ref = refs
    high_out, rest_out, aimed_out = outs
    length = k_ref.shape[0]
    keys = k_ref[:, g * HEAD_DIM : (g + 1) * HEAD_DIM]
    row = lax.broadcasted_iota(jnp.int32, (length, length), 0)
    col = lax.broadcasted_iota(jnp.int32, (length, length), 1)
    allowed = (row <= col) & (seg_col[...] == seg_row[...])
    lanes = [slice(h * HEAD_DIM, (h + 1) * HEAD_DIM) for h in range(g * GROUP, (g + 1) * GROUP)]
    every = []
    for j in range(GROUP):
        logits = dot_nt(keys, q_ref[:, lanes[j]]) * HEAD_DIM ** (-0.5)
        logits = jnp.where(allowed, logits, -1e30)
        peak = jnp.max(logits, axis=0, keepdims=True)
        weights = jnp.exp(logits - peak)
        every.append((weights / jnp.sum(weights, axis=0, keepdims=True)).astype(BF16))
    gram = sum(dot_nt(probs, probs) for probs in every)
    high = gram.astype(BF16)
    high_out[...] = high
    rest_out[...] = (gram - high.astype(F32)).astype(BF16)
    aimed_out[...] = sum(dot_nn(probs, t_ref[:, lanes[j]]) for j, probs in enumerate(every))


def train_head(s, g, seg_row, seg_col, query, keyset, target, deps):
    length = query.shape[0]
    return call(
        functools.partial(train_head_kernel, g),
        [((length, length), BF16), ((length, length), BF16), ((length, HEAD_DIM), F32)],
        s, [seg_row, seg_col, query, keyset, target], flops=2e9, deps=deps,
    )


def score_probs_kernel(s, refs, outs, scratch):
    seg_row, seg_col, q_ref, k_ref = refs
    (p_ref,) = outs
    length = k_ref.shape[0]
    row = lax.broadcasted_iota(jnp.int32, (length, length), 0)
    col = lax.broadcasted_iota(jnp.int32, (length, length), 1)
    allowed = (col <= row) & (seg_col[...] == seg_row[...])
    for g in range(KV_HEADS):
        keys = k_ref[:, g * HEAD_DIM : (g + 1) * HEAD_DIM]
        for j in range(GROUP):
            h = g * GROUP + j
            logits = dot_nt(q_ref[:, h * HEAD_DIM : (h + 1) * HEAD_DIM], keys) * HEAD_DIM ** (-0.5)
            logits = jnp.where(allowed, logits, -1e30)
            weights = jnp.exp(logits - jnp.max(logits, axis=1, keepdims=True))
            probs = weights / jnp.sum(weights, axis=1, keepdims=True)
            p_ref[g, j * length : (j + 1) * length, :] = probs.astype(BF16)


def score_probs(s, seg_row, seg_col, query, keyset, deps):
    length = query.shape[0]
    return call(
        score_probs_kernel, [((KV_HEADS, GROUP * length, length), BF16)],
        s, [seg_row, seg_col, query, keyset], flops=1e9, deps=deps,
    )[0]


def unpack_down(packed, half):
    parts = VALUE_WIDTH // half
    if parts == 1:
        return packed
    return jnp.concatenate([packed[:, i * half : (i + 1) * half] for i in range(parts)], axis=0)


def pack_down(block, half):
    parts = VALUE_WIDTH // half
    if parts == 1:
        return block
    rows = block.shape[0] // parts
    return jnp.concatenate([block[i * rows : (i + 1) * rows] for i in range(parts)], axis=1)


def low_of(pieces, half):
    return jnp.concatenate([unpack_down(p[half // 2 :, :], half) for p in pieces], axis=0)


def features_of(position, n, shard, half, core):
    position = lax.rem(position, n)
    owner = jnp.where(position < n // 2, 2 * position, 2 * (n - 1 - position) + 1)
    return owner * shard + core * half


def project_kernel(n, offsets, half, s, refs, outs, scratch):
    x, xo, xs, xso = refs[:4]
    refs = refs[4:]
    (xb,) = scratch
    t, u = x.shape[0], xs.shape[0]
    rows = half // 2
    total = low = None
    for i, offset in enumerate(offsets):
        here = lanes_at(features_of(s[2] + offset, n, 2 * half, half, s[1]), half)
        for at, a in ((0, x), (t, xo), (2 * t, xs), (2 * t + u, xso)):
            xb[i, at : at + a.shape[0], :] = a[:, here]
        pieces = [refs[2 * i][...], refs[2 * i + 1][...]]
        weight = jnp.concatenate([p[:rows, :] for p in pieces], axis=0)
        part = dot_nn(xb[i], weight)
        total = part if total is None else total + part
        part = dot_nt(low_of(pieces, half), xb[i, : 2 * t, :])
        low = part if low is None else low + part
    before = refs[2 * len(offsets) :]
    if before:
        total = total + before[0][...]
        low = low + before[1][...]
    if outs[0].shape[0] == total.shape[0]:
        outs[0][...] = total
        outs[1][...] = low
        return
    for i, out in enumerate(outs):
        out[:t, :] = total[i * t : (i + 1) * t, :]
        out[t : t + u, :] = total[2 * t + i * u : 2 * t + (i + 1) * u, :]
        part = low[:, i * t : (i + 1) * t]
        out[t + u :, :t] = part[: RANK // 2, :]
        out[t + u :, t : 2 * t] = part[RANK // 2 :, :]


def project(s, n, offsets, half, pieces, before, raw, final):
    t, u = raw[0].shape[0], raw[2].shape[0]
    if final:
        outs = [((t + u + RANK // 2, VALUE_WIDTH), F32)] * 2
    else:
        outs = [((2 * t + 2 * u, VALUE_WIDTH), F32), ((RANK, 2 * t), F32)]
    return call(
        functools.partial(project_kernel, n, offsets, half),
        outs, s, [*raw, *pieces, *before],
        scratch=[pltpu.VMEM((len(offsets), 2 * t + 2 * u, half), BF16)],
        flops=len(offsets) * 3.4e8,
    )


def grad_kernel(n, offset, half, s, refs, outs, scratch):
    x, xs = refs[:2]
    pieces, (mine, got, up_ref), heads = refs[2:6], refs[6:9], refs[9:]
    base, d_low_out, up_grad = outs
    t, u = x.shape[0], xs.shape[0]
    rows = half // 2
    total = mine[:t, :] + got[:t, :]
    base_total = mine[t : t + u, :] + got[t : t + u, :]
    packed = mine[t + u :, :] + got[t + u :, :]
    low = jnp.concatenate([packed[:, :t], packed[:, t : 2 * t]], axis=0)
    for i in range(2):
        core = s[1] if i == 0 else 1 - s[1]
        here = lanes_at(features_of(s[2] + offset, n, 2 * half, half, core), half)
        pair = [pieces[2 * i][...], pieces[2 * i + 1][...]]
        weight = jnp.concatenate([p[:rows, :] for p in pair], axis=0)
        total = total + dot_nn(x[:, here], weight)
        base_total = base_total + dot_nn(xs[:, here], weight)
        low = low + dot_nt(low_of(pair, half), x[:, here])
    base[...] = base_total
    low = low.astype(BF16)
    up_half = up_ref[...].astype(BF16)
    low_rows = low.astype(F32).T.astype(BF16)
    values = (total + adapter_scale_factor * dot_nn(low_rows, up_half)).astype(BF16)
    grads = []
    for g in range(KV_HEADS):
        head = values[:, g * HEAD_DIM : (g + 1) * HEAD_DIM]
        high, rest, aimed = heads[3 * g : 3 * g + 3]
        d_head = dot_nn(high[...], head) + dot_nn(rest[...], head) - aimed[...]
        grads.append(d_head.astype(BF16))
    d_values = jnp.concatenate(grads, axis=1)
    d_low_out[...] = (adapter_scale_factor * dot_nt(up_half, d_values)).astype(BF16)
    up_grad[...] = adapter_scale_factor * dot_nn(low, d_values)


def value_grads(s, n, offset, half, pieces, mine, got, up, heads, raw):
    t, u = raw[0].shape[0], raw[1].shape[0]
    return call(
        functools.partial(grad_kernel, n, offset, half),
        [((u, VALUE_WIDTH), F32), ((RANK, t), BF16), ((RANK, VALUE_WIDTH), F32)],
        s, [*raw, *pieces, mine, got, up, *[a for h in heads for a in h]],
        flops=1e9,
    )


def up_place(device, half):
    columns = VALUE_WIDTH // half
    row = pl.multiple_of(lax.div(device, columns) * UP_ROWS, UP_ROWS)
    col = lax.rem(device, columns) * half
    return pl.ds(row, UP_ROWS), lanes_at(col, half)


def down_kernel(n, half, s, refs, outs, scratch):
    x, xo, d_low, d_low_got, up_grad, up_got = refs
    (up_sum,) = scratch
    keep, keep_up, *out = outs
    up_sum[...] = up_grad[...] + up_got[...]
    for k in [*range(n - 1, 0, -1), 0]:
        here = lanes_at((s[0] ^ k) * 2 * half + s[1] * half, half)
        part = dot_nn(d_low[...], x[:, here]) + dot_nn(d_low_got[...], xo[:, here])
        up_piece = up_sum[up_place(s[0] ^ k, half)]
        if k == 0:
            keep[...] = part
            keep_up[...] = up_piece
        else:
            out[k - 1][:RANK, :] = part.astype(BF16)
            out[k - 1][RANK:, :] = up_piece.astype(BF16)


def down_pieces(s, n, half, d_low, d_low_got, up_grad, up_got, raw):
    return call(
        functools.partial(down_kernel, n, half),
        [((RANK, half), F32), ((UP_ROWS, half), F32)] + [((RANK + UP_ROWS, half), BF16)] * (n - 1),
        s, [*raw, d_low, d_low_got, up_grad, up_got],
        scratch=[pltpu.VMEM((RANK, VALUE_WIDTH), F32)], flops=1e9,
    )


def update_kernel(s, refs, outs, scratch):
    keep, keep_up, down_ref, up_ref, *got = refs
    fresh, message = outs
    half = fresh.shape[1]
    old_down = down_ref[:, lanes_at(s[1] * half, half)]
    old_up = up_ref[up_place(s[0], half)]
    total, total_up = keep[...], keep_up[...]
    for piece in got:
        total += piece[:RANK, :].astype(F32)
        total_up += piece[RANK:, :].astype(F32)
    new_down = old_down - rate_down * total
    new_up = old_up - rate_up * total_up
    high = new_up.astype(BF16)
    fresh[...] = new_down
    message[:RANK, :] = new_down.astype(BF16)
    message[RANK : RANK + UP_ROWS, :] = high
    message[RANK + UP_ROWS :, :] = (new_up - high.astype(F32)).astype(BF16)


def update(s, keep, keep_up, down_t, up, got):
    half = keep.shape[1]
    return call(
        update_kernel,
        [((RANK, half), F32), ((RANK + 2 * UP_ROWS, half), BF16)],
        s, [keep, keep_up, down_t, up, *got],
    )


def score_low_kernel(n, half, s, refs, outs, scratch):
    xs, xso, *messages = refs
    mine, other, up = outs
    low_mine = low_other = None
    for k in range(n):
        here = lanes_at((s[0] ^ k) * 2 * half + s[1] * half, half)
        message = messages[k]
        part = dot_nt(xs[:, here], message[:RANK, :])
        low_mine = part if low_mine is None else low_mine + part
        part = dot_nt(xso[:, here], message[:RANK, :])
        low_other = part if low_other is None else low_other + part
        high = message[RANK : RANK + UP_ROWS, :].astype(F32)
        up[up_place(s[0] ^ k, half)] = high + message[RANK + UP_ROWS :, :].astype(F32)
    mine[...] = low_mine
    other[...] = low_other


def score_low(s, half, messages, raw):
    n, u = len(messages), raw[0].shape[0]
    return call(
        functools.partial(score_low_kernel, n, half),
        [((u, RANK), F32), ((u, RANK), F32), ((RANK, VALUE_WIDTH), F32)],
        s, [*raw, *messages], flops=2e8,
    )


def score_kernel(s, refs, outs, scratch):
    base, mine, got, up, probs, fresh, fresh_got = refs
    out, new_down, new_up = outs
    half = new_down.shape[1] // 2
    low = (mine[...] + got[...]).astype(BF16)
    u = low.shape[0]
    values = base[...] + adapter_scale_factor * dot_nn(low, up[...].astype(BF16))
    values = values.astype(BF16)
    for g in range(KV_HEADS):
        attended = dot_nn(probs[g], values[:, g * HEAD_DIM : (g + 1) * HEAD_DIM]).astype(BF16)
        for j in range(GROUP):
            h = g * GROUP + j
            out[:, h * HEAD_DIM : (h + 1) * HEAD_DIM] = attended[j * u : (j + 1) * u, :]
    new_down[:, lanes_at(s[1] * half, half)] = fresh[...]
    new_down[:, lanes_at((1 - s[1]) * half, half)] = fresh_got[...]
    new_up[...] = up[...]


def score(s, base, mine, got, up, probs, fresh, fresh_got):
    u, half = base.shape[0], fresh.shape[1]
    return call(
        score_kernel,
        [((u, Q_HEADS * HEAD_DIM), BF16), ((RANK, 2 * half), F32), (up.shape, F32)],
        s, [base, mine, got, up, probs, fresh, fresh_got], flops=2e8, final=(0, 1, 2),
    )


def reduce_order(n):
    return [*range(n - 2, 0, -2), *range(n - 1, 0, -2)]


def solution(mesh):
    n_fsdp, n_view = mesh.shape["fsdp"], mesh.shape["view"]
    line = n_fsdp // 2

    def ring_device(place):
        place = place % n_fsdp
        return 2 * place if place < line else 2 * (n_fsdp - 1 - place) + 1

    forward = [(ring_device(i), ring_device(i + 1)) for i in range(n_fsdp)]
    backward = [(b, a) for a, b in forward]

    def over_view(array, bit):
        return lax.ppermute(array, "view", [(i, i ^ bit) for i in range(n_view)])

    def swap(array):
        return lax.ppermute(array, "view", [(i, i ^ 1) for i in range(n_view)])

    def exchange(array, k):
        return lax.ppermute(array, "fsdp", [(i, i ^ k) for i in range(n_fsdp)])

    def body(
        train_input,
        train_query,
        train_keys,
        train_target,
        train_segments,
        value_weight,
        adapter_down,
        adapter_up,
        score_input,
        score_query,
        score_keys,
        score_segments,
    ):
        width = train_input.shape[-1]
        x = train_input.reshape(-1, width)
        xs = score_input.reshape(-1, width)
        query, keyset, target = (a.reshape(x.shape[0], -1) for a in (train_query, train_keys, train_target))
        squery, skeyset = (a.reshape(xs.shape[0], -1) for a in (score_query, score_keys))
        shard = value_weight.shape[0]
        half = shard // 2
        me = lax.axis_index("fsdp")
        core = lax.axis_index("view") % 2
        place = jnp.where(me % 2 == 0, me // 2, n_fsdp - 1 - me // 2)
        s = jnp.stack([me, core, place]).astype(jnp.int32)

        down_t = adapter_down.T
        down_half = down_t.astype(BF16)
        my_down = lax.dynamic_slice_in_dim(down_half, core * half, half, 1)
        my_weight = lax.dynamic_slice_in_dim(value_weight, core * half, half, 0)
        pieces = [
            jnp.concatenate(
                [
                    my_weight[q * half // 2 : (q + 1) * half // 2],
                    pack_down(my_down[q * RANK // 2 : (q + 1) * RANK // 2], half),
                ],
                axis=0,
            )
            for q in range(2)
        ]

        seg_row, seg_col = train_segments.reshape(1, -1), train_segments.reshape(-1, 1)
        sseg_row, sseg_col = score_segments.reshape(1, -1), score_segments.reshape(-1, 1)
        near_query, near_keys, near_target = near(query), near(keyset), near(target)

        def head(g, deps):
            return train_head(s, g, seg_row, seg_col, near_query, near_keys, near_target, deps)

        def onward(array, ahead):
            return lax.ppermute(array, "fsdp", forward if ahead else backward)

        steps = n_fsdp // 2
        arrived, offsets = list(pieces), [0]
        ahead, back = list(pieces), list(pieces)
        heads = [None] * KV_HEADS
        for k in range(1, steps + 1):
            if k < steps:
                for q in range(2):
                    ahead[q] = onward(ahead[q], True)
                    back[q] = onward(back[q], False)
            else:
                last = [onward(ahead[0], True), onward(back[1], False)]
            if k == 1:
                xo, xso = swap(x), swap(xs)
                raw = tuple(near(a) for a in (x, xo, xs, xso))
                heads[0] = head(0, ())
                probs = score_probs(s, sseg_row, sseg_col, squery, skeyset, ())
            elif k == 2:
                heads[1] = head(1, ())
                heads[2] = head(2, ())
            elif k == 3:
                partial = project(s, n_fsdp, offsets, half, arrived, (), raw, False)
                cut = len(offsets)
            if k < steps:
                arrived += [*ahead, *back]
                offsets += [n_fsdp - k, k]
        sums, sums_out = project(s, n_fsdp, offsets[cut:], half, arrived[2 * cut :], partial, raw, True)
        sums_got = swap(sums_out)
        heads[3] = head(3, ())
        last += [swap(a) for a in last]
        base, d_low, up_grad = value_grads(
            s, n_fsdp, steps, half, last, sums, sums_got, adapter_up, heads, (raw[0], raw[2])
        )
        d_low_got, up_got = swap(d_low), swap(up_grad)
        keep, keep_up, *out = down_pieces(s, n_fsdp, half, d_low, d_low_got, up_grad, up_got, raw[:2])
        bit = 2
        while bit < n_view:
            keep, keep_up = (a + over_view(a, bit) for a in (keep, keep_up))
            out = [(a.astype(F32) + over_view(a, bit).astype(F32)).astype(BF16) for a in out]
            bit *= 2

        got = [None] * len(out)
        for k in reduce_order(n_fsdp):
            got[k - 1] = exchange(out[k - 1], k)
        fresh, message = update(s, keep, keep_up, down_t, adapter_up, got)
        messages = [message] + [None] * (n_fsdp - 1)
        for k in range(n_fsdp - 2, 0, -2):
            messages[k] = exchange(message, k)
        for k in range(0, n_fsdp, 2):
            messages[k + 1] = exchange(messages[k], 1)
        fresh_got = swap(fresh)
        mine, other, new_up = score_low(s, half, messages, raw[2:])
        other_got = swap(other)
        scored, new_down, new_up = score(s, base, mine, other_got, new_up, probs, fresh, fresh_got)
        return (new_down.T, new_up, scored.reshape(score_query.shape))

    in_specs = (
        P(("task", "view"), "fsdp", None),
        P(("task", "view"), "fsdp", None),
        P(("task", "view"), "fsdp", None),
        P(("task", "view"), "fsdp", None),
        P(("task", "view"), "fsdp", None),
        P("fsdp", None),
        P(("task", "fsdp"), None),
        P("task", None),
        P(("task", "view"), "fsdp", None),
        P(("task", "view"), "fsdp", None),
        P(("task", "view"), "fsdp", None),
        P(("task", "view"), "fsdp", None),
    )
    out_specs = (P(("task", "fsdp"), None), P("task", None), P(("task", "view"), "fsdp", None))
    return jax.shard_map(body, mesh=mesh, in_specs=in_specs, out_specs=out_specs, check_vma=False)
```

profile of v0, /device:TPU:0, one launch (start us, length us, event | category | flops | bytes accessed | tf_op | source)
XLA Modules:
  0.0 117.5 jit_solution(14995075137515065483)
XLA Ops:
  2.1 1.1 constant_dynamic-slice_fusion.1
  3.2 2.7 %collective-permute-start.12 = (bf16[288,512]{1,0:T(8,128)(2,1)S(1)}, bf16[288,512]{1,0:T(8,128)(2,1)S(1)}, u32[]{:S(2)}, u32[]{:S(2)}) collective-permute-start(bf16[288,512]{1,0:T(8,128)(2,1)S(1)} %pad_maximum_fusion.1.refs_5_), channel_id=1, source_target_pairs={{0,4},{4,8},{8,12},{12,14},{14,10},{10,6},{6,2},{2,0},{1,5},{5,9},... | collective-permute-start | bytes 884744 | tf_op jit(solution)/shard_map/ppermute | solution.py:430
  6.1 1.9 %collective-permute-start = (bf16[288,512]{1,0:T(8,128)(2,1)S(1)}, bf16[288,512]{1,0:T(8,128)(2,1)S(1)}, u32[]{:S(2)}, u32[]{:S(2)}) collective-permute-start(bf16[288,512]{1,0:T(8,128)(2,1)S(1)} %pad_maximum_fusion.refs_4_), channel_id=1, source_target_pairs={{0,4},{4,8},{8,12},{12,14},{14,10},{10,6},{6,2},{2,0},{1,5},{5,9},... | collective-permute-start | bytes 884744 | tf_op jit(solution)/shard_map/ppermute | solution.py:430
  8.0 5.7 %collective-permute-done.12.refs_7_ = bf16[288,512]{1,0:T(8,128)(2,1)S(1)} collective-permute-done((bf16[288,512]{1,0:T(8,128)(2,1)S(1)}, bf16[288,512]{1,0:T(8,128)(2,1)S(1)}, u32[]{:S(2)}, u32[]{:S(2)}) %collective-permute-start.12) | collective-permute-done | bytes 294944 | tf_op jit(solution)/shard_map/ppermute | solution.py:430
  13.7 2.0 %collective-permute-start.15 = (bf16[288,512]{1,0:T(8,128)(2,1)S(1)}, bf16[288,512]{1,0:T(8,128)(2,1)S(1)}, u32[]{:S(2)}, u32[]{:S(2)}) collective-permute-start(bf16[288,512]{1,0:T(8,128)(2,1)S(1)} %pad_maximum_fusion.refs_4_), channel_id=1, source_target_pairs={{4,0},{8,4},{12,8},{14,12},{10,14},{6,10},{2,6},{0,2},{5,1},{9,5},... | collective-permute-start | bytes 884744 | tf_op jit(solution)/shard_map/ppermute | solution.py:430
  17.3 2.7 %collective-permute-done.refs_6_ = bf16[288,512]{1,0:T(8,128)(2,1)S(1)} collective-permute-done((bf16[288,512]{1,0:T(8,128)(2,1)S(1)}, bf16[288,512]{1,0:T(8,128)(2,1)S(1)}, u32[]{:S(2)}, u32[]{:S(2)}) %collective-permute-start) | collective-permute-done | bytes 294944 | tf_op jit(solution)/shard_map/ppermute | solution.py:430
  20.0 2.0 %collective-permute-start.5 = (bf16[288,512]{1,0:T(8,128)(2,1)S(1)}, bf16[288,512]{1,0:T(8,128)(2,1)S(1)}, u32[]{:S(2)}, u32[]{:S(2)}) collective-permute-start(bf16[288,512]{1,0:T(8,128)(2,1)S(1)} %collective-permute-done.4.refs_9_), channel_id=1, source_target_pairs={{4,0},{8,4},{12,8},{14,12},{10,14},{6,10},{2,6},{0,2},{5,1},{9,5},... | collective-permute-start | bytes 884744 | tf_op jit(solution)/shard_map/ppermute | solution.py:430
  22.7 1.1 collective-permute-start.1
  24.5 1.9 %collective-permute-done.13.refs_11_ = bf16[288,512]{1,0:T(8,128)(2,1)} collective-permute-done((bf16[288,512]{1,0:T(8,128)(2,1)S(1)}, bf16[288,512]{1,0:T(8,128)(2,1)}, u32[]{:S(2)}, u32[]{:S(2)}) %collective-permute-start.13) | collective-permute-done | bytes 294944 | tf_op jit(solution)/shard_map/ppermute | solution.py:430
  26.4 2.0 %collective-permute-start.16 = (bf16[288,512]{1,0:T(8,128)(2,1)S(1)}, bf16[288,512]{1,0:T(8,128)(2,1)}, u32[]{:S(2)}, u32[]{:S(2)}) collective-permute-start(bf16[288,512]{1,0:T(8,128)(2,1)S(1)} %collective-permute-done.15.refs_8_), channel_id=1, source_target_pairs={{4,0},{8,4},{12,8},{14,12},{10,14},{6,10},{2,6},{0,2},{5,1},{9,5},... | collective-permute-start | bytes 884744 | tf_op jit(solution)/shard_map/ppermute | solution.py:430
  29.1 1.6 %collective-permute-start.6 = (bf16[288,512]{1,0:T(8,128)(2,1)S(1)}, bf16[288,512]{1,0:T(8,128)(2,1)S(1)}, u32[]{:S(2)}, u32[]{:S(2)}) collective-permute-start(bf16[288,512]{1,0:T(8,128)(2,1)S(1)} %collective-permute-done.5.refs_13_), channel_id=1, source_target_pairs={{4,0},{8,4},{12,8},{14,12},{10,14},{6,10},{2,6},{0,2},{5,1},{9,5},... | collective-permute-start | bytes 884744 | tf_op jit(solution)/shard_map/ppermute | solution.py:430
  31.4 1.1 collective-permute-done.1.refs_10_
  32.5 1.8 %collective-permute-start.2 = (bf16[288,512]{1,0:T(8,128)(2,1)}, bf16[288,512]{1,0:T(8,128)(2,1)S(1)}, u32[]{:S(2)}, u32[]{:S(2)}) collective-permute-start(bf16[288,512]{1,0:T(8,128)(2,1)} %collective-permute-done.1.refs_10_), channel_id=1, source_target_pairs={{0,4},{4,8},{8,12},{12,14},{14,10},{10,6},{6,2},{2,0},{1,5},{5,9},... | collective-permute-start | bytes 884744 | tf_op jit(solution)/shard_map/ppermute | solution.py:430
  34.3 2.1 %collective-permute-done.16.refs_12_ = bf16[288,512]{1,0:T(8,128)(2,1)} collective-permute-done((bf16[288,512]{1,0:T(8,128)(2,1)S(1)}, bf16[288,512]{1,0:T(8,128)(2,1)}, u32[]{:S(2)}, u32[]{:S(2)}) %collective-permute-start.16) | collective-permute-done | bytes 294944 | tf_op jit(solution)/shard_map/ppermute | solution.py:430
  36.5 2.0 %collective-permute-start.14 = (bf16[288,512]{1,0:T(8,128)(2,1)}, bf16[288,512]{1,0:T(8,128)(2,1)}, u32[]{:S(2)}, u32[]{:S(2)}) collective-permute-start(bf16[288,512]{1,0:T(8,128)(2,1)} %collective-permute-done.13.refs_11_), channel_id=1, source_target_pairs={{0,4},{4,8},{8,12},{12,14},{14,10},{10,6},{6,2},{2,0},{1,5},{5,9},... | collective-permute-start | bytes 884744 | tf_op jit(solution)/shard_map/ppermute | solution.py:430
  38.5 2.8 %collective-permute-done.6.refs_7_ = bf16[288,512]{1,0:T(8,128)(2,1)S(1)} collective-permute-done((bf16[288,512]{1,0:T(8,128)(2,1)S(1)}, bf16[288,512]{1,0:T(8,128)(2,1)S(1)}, u32[]{:S(2)}, u32[]{:S(2)}) %collective-permute-start.6) | collective-permute-done | bytes 294944 | tf_op jit(solution)/shard_map/ppermute | solution.py:430
  41.3 1.5 %collective-permute-start.17 = (bf16[288,512]{1,0:T(8,128)(2,1)}, bf16[288,512]{1,0:T(8,128)(2,1)}, u32[]{:S(2)}, u32[]{:S(2)}) collective-permute-start(bf16[288,512]{1,0:T(8,128)(2,1)} %collective-permute-done.16.refs_12_), channel_id=1, source_target_pairs={{4,0},{8,4},{12,8},{14,12},{10,14},{6,10},{2,6},{0,2},{5,1},{9,5},... | collective-permute-start | bytes 884744 | tf_op jit(solution)/shard_map/ppermute | solution.py:430
  43.0 1.6 %collective-permute-start.7 = (bf16[288,512]{1,0:T(8,128)(2,1)S(1)}, bf16[288,512]{1,0:T(8,128)(2,1)S(1)}, u32[]{:S(2)}, u32[]{:S(2)}) collective-permute-start(bf16[288,512]{1,0:T(8,128)(2,1)S(1)} %collective-permute-done.6.refs_7_), channel_id=1, source_target_pairs={{4,0},{8,4},{12,8},{14,12},{10,14},{6,10},{2,6},{0,2},{5,1},{9,5},... | collective-permute-start | bytes 884744 | tf_op jit(solution)/shard_map/ppermute | solution.py:430
  45.1 2.2 %copy-done = bf16[1,256,8192]{2,1,0:T(8,128)(2,1)S(1)} copy-done((bf16[1,256,8192]{2,1,0:T(8,128)(2,1)S(1)}, bf16[1,256,8192]{2,1,0:T(8,128)(2,1)}, u32[]{:S(2)}) %copy-start) | copy-done | bytes 4194328
  47.3 1.0 copy-done.6
  48.2 1.0 copy-done.8
  49.2 1.0 copy-done.10
  50.1 1.0 copy-done.12
  51.1 1.0 copy-done.14
  52.1 4.9 %shard_map.139 = (f32[640,512]{1,0:T(8,128)S(1)}, f32[64,512]{1,0:T(8,128)S(1)}) custom-call(s32[3]{0:T(128)S(1)} %pad_add_fusion.scalar_ref, bf16[256,8192]{1,0:T(8,128)(2,1)S(1)} %bitcast.18, bf16[256,8192]{1,0:T(8,128)(2,1)} %collective-permute-done.10.refs_1_, bf16[64,8192]{1,0:T(8,128)(2,1)S(1)} %bitcast.23, ...), custom_call_target="tpu_custom_call" | custom-call | flops 1700000000 | bytes 1048576 | tf_op jit(solution)/shard_map/pallas_call | solution.py:54
  57.0 3.6 %shard_map.140 = (f32[352,512]{1,0:T(8,128)S(1)}, f32[352,512]{1,0:T(8,128)S(1)}) custom-call(s32[3]{0:T(128)S(1)} %pad_add_fusion.scalar_ref, bf16[256,8192]{1,0:T(8,128)(2,1)S(1)} %bitcast.19, bf16[256,8192]{1,0:T(8,128)(2,1)} %collective-permute-done.10.refs_1_, bf16[64,8192]{1,0:T(8,128)(2,1)S(1)} %bitcast.24, ...), custom_call_target="tpu_custom_call" | custom-call | flops 680000000 | bytes 1048576 | tf_op jit(solution)/shard_map/pallas_call | solution.py:54
  60.7 1.8 %shard_map.141 = (bf16[256,256]{1,0:T(8,128)(2,1)S(1)}, bf16[256,256]{1,0:T(8,128)(2,1)S(1)}, f32[256,128]{1,0:T(8,128)S(1)}) custom-call(s32[3]{0:T(128)S(1)} %pad_add_fusion.scalar_ref, s32[1,256]{1,0:T(1,128)S(1)} %bitcast.30, s32[256,1]{1,0:T(8,128)S(1)} %copy.16.refs_1_, bf16[256,4096]{1,0:T(8,128)(2,1)S(1)} %bitcast.36, bf16[256,512]{1,0:T(8,128)(2,1)S(1)} %bitcast.45, ...), custom_call_target="tpu_custom_call" | custom-call | flops 2000000000 | bytes 1048576 | tf_op jit(solution)/shard_map/pallas_call | solution.py:54
  62.5 1.8 %shard_map.142 = (bf16[256,256]{1,0:T(8,128)(2,1)S(1)}, bf16[256,256]{1,0:T(8,128)(2,1)S(1)}, f32[256,128]{1,0:T(8,128)S(1)}) custom-call(s32[3]{0:T(128)S(1)} %pad_add_fusion.scalar_ref, s32[1,256]{1,0:T(1,128)S(1)} %bitcast.31, s32[256,1]{1,0:T(8,128)S(1)} %copy.16.refs_1_, bf16[256,4096]{1,0:T(8,128)(2,1)S(1)} %bitcast.37, bf16[256,512]{1,0:T(8,128)(2,1)S(1)} %bitcast.46, ...), custom_call_target="tpu_custom_call" | custom-call | flops 2000000000 | bytes 1048576 | tf_op jit(solution)/shard_map/pallas_call | solution.py:54
  65.0 1.8 %shard_map.143 = (bf16[256,256]{1,0:T(8,128)(2,1)S(1)}, bf16[256,256]{1,0:T(8,128)(2,1)S(1)}, f32[256,128]{1,0:T(8,128)S(1)}) custom-call(s32[3]{0:T(128)S(1)} %pad_add_fusion.scalar_ref, s32[1,256]{1,0:T(1,128)S(1)} %bitcast.32, s32[256,1]{1,0:T(8,128)S(1)} %copy.16.refs_1_, bf16[256,4096]{1,0:T(8,128)(2,1)S(1)} %bitcast.38, bf16[256,512]{1,0:T(8,128)(2,1)S(1)} %bitcast.47, ...), custom_call_target="tpu_custom_call" | custom-call | flops 2000000000 | bytes 1048576 | tf_op jit(solution)/shard_map/pallas_call | solution.py:54
  66.8 1.8 %shard_map.144 = (bf16[256,256]{1,0:T(8,128)(2,1)S(1)}, bf16[256,256]{1,0:T(8,128)(2,1)S(1)}, f32[256,128]{1,0:T(8,128)S(1)}) custom-call(s32[3]{0:T(128)S(1)} %pad_add_fusion.scalar_ref, s32[1,256]{1,0:T(1,128)S(1)} %bitcast.33, s32[256,1]{1,0:T(8,128)S(1)} %copy.16.refs_1_, bf16[256,4096]{1,0:T(8,128)(2,1)S(1)} %bitcast.39, bf16[256,512]{1,0:T(8,128)(2,1)S(1)} %bitcast.48, ...), custom_call_target="tpu_custom_call" | custom-call | flops 2000000000 | bytes 1048576 | tf_op jit(solution)/shard_map/pallas_call | solution.py:54
  68.9 2.3 %shard_map.145 = (f32[64,512]{1,0:T(8,128)S(1)}, bf16[64,256]{1,0:T(8,128)(2,1)S(1)}, f32[64,512]{1,0:T(8,128)S(1)}) custom-call(s32[3]{0:T(128)S(1)} %pad_add_fusion.scalar_ref, bf16[256,8192]{1,0:T(8,128)(2,1)S(1)} %bitcast.20, bf16[64,8192]{1,0:T(8,128)(2,1)S(1)} %bitcast.25, bf16[288,512]{1,0:T(8,128)(2,1)S(1)} %collective-permute-done.3.refs_2_, ...), custom_call_target="tpu_custom_call" | custom-call | flops 1000000000 | bytes 1048576 | tf_op jit(solution)/shard_map/pallas_call | solution.py:54
  71.9 1.1 collective-permute-done.19.refs_3_
  73.0 3.1 %shard_map.146 = (f32[64,512]{1,0:T(8,128)S(1)}, f32[8,512]{1,0:T(8,128)S(1)}, bf16[72,512]{1,0:T(8,128)(2,1)S(1)}, bf16[72,512]{1,0:T(8,128)(2,1)S(1)}, bf16[72...) custom-call(s32[3]{0:T(128)S(1)} %pad_add_fusion.scalar_ref, ...), custom_call_target="tpu_custom_call" | custom-call | flops 1000000000 | bytes 1048576 | tf_op jit(solution)/shard_map/pallas_call | solution.py:54
  76.0 1.6 %collective-permute-start.21 = (bf16[72,512]{1,0:T(8,128)(2,1)S(1)}, bf16[72,512]{1,0:T(8,128)(2,1)S(1)}, u32[]{:S(2)}, u32[]{:S(2)}) collective-permute-start(bf16[72,512]{1,0:T(8,128)(2,1)S(1)} %get-tuple-element.60), channel_id=1, source_target_pairs={{0,2},{2,0},{4,6},{6,4},{8,10},{10,8},{12,14},{14,12},{1,3},{3,1},... | collective-permute-start | bytes 221192 | tf_op jit(solution)/shard_map/ppermute | solution.py:379
  77.7 1.6 %collective-permute-start.22 = (bf16[72,512]{1,0:T(8,128)(2,1)S(1)}, bf16[72,512]{1,0:T(8,128)(2,1)S(1)}, u32[]{:S(2)}, u32[]{:S(2)}) collective-permute-start(bf16[72,512]{1,0:T(8,128)(2,1)S(1)} %get-tuple-element.61), channel_id=1, source_target_pairs={{0,4},{2,6},{4,0},{6,2},{8,12},{10,14},{12,8},{14,10},{1,5},{3,7},... | collective-permute-start | bytes 221192 | tf_op jit(solution)/shard_map/ppermute | solution.py:379
  79.6 2.4 %collective-permute-start.24 = (bf16[72,512]{1,0:T(8,128)(2,1)S(1)}, bf16[72,512]{1,0:T(8,128)(2,1)S(1)}, u32[]{:S(2)}, u32[]{:S(2)}) collective-permute-start(bf16[72,512]{1,0:T(8,128)(2,1)S(1)} %get-tuple-element.63), channel_id=1, source_target_pairs={{0,8},{2,10},{4,12},{6,14},{8,0},{10,2},{12,4},{14,6},{1,9},{3,11}... | collective-permute-start | bytes 221192 | tf_op jit(solution)/shard_map/ppermute | solution.py:379
  82.0 1.5 %collective-permute-start.25 = (bf16[72,512]{1,0:T(8,128)(2,1)S(1)}, bf16[72,512]{1,0:T(8,128)(2,1)S(1)}, u32[]{:S(2)}, u32[]{:S(2)}) collective-permute-start(bf16[72,512]{1,0:T(8,128)(2,1)S(1)} %get-tuple-element.64), channel_id=1, source_target_pairs={{0,10},{2,8},{4,14},{6,12},{8,2},{10,0},{12,6},{14,4},{1,11},{3,9}... | collective-permute-start | bytes 221192 | tf_op jit(solution)/shard_map/ppermute | solution.py:379
  83.5 3.4 %collective-permute-start.26 = (bf16[72,512]{1,0:T(8,128)(2,1)S(1)}, bf16[72,512]{1,0:T(8,128)(2,1)S(1)}, u32[]{:S(2)}, u32[]{:S(2)}) collective-permute-start(bf16[72,512]{1,0:T(8,128)(2,1)S(1)} %get-tuple-element.65), channel_id=1, source_target_pairs={{0,12},{2,14},{4,8},{6,10},{8,4},{10,6},{12,0},{14,2},{1,13},{3,15... | collective-permute-start | bytes 221192 | tf_op jit(solution)/shard_map/ppermute | solution.py:379
  87.3 7.1 %collective-permute-done.25.refs_8_ = bf16[72,512]{1,0:T(8,128)(2,1)S(1)} collective-permute-done((bf16[72,512]{1,0:T(8,128)(2,1)S(1)}, bf16[72,512]{1,0:T(8,128)(2,1)S(1)}, u32[]{:S(2)}, u32[]{:S(2)}) %collective-permute-start.25) | collective-permute-done | bytes 73760 | tf_op jit(solution)/shard_map/ppermute | solution.py:379
  95.1 3.0 %collective-permute-start.29 = (bf16[80,512]{1,0:T(8,128)(2,1)S(1)}, bf16[80,512]{1,0:T(8,128)(2,1)S(1)}, u32[]{:S(2)}, u32[]{:S(2)}) collective-permute-start(bf16[80,512]{1,0:T(8,128)(2,1)S(1)} %get-tuple-element.67.refs_2_), channel_id=1, source_target_pairs={{0,4},{2,6},{4,0},{6,2},{8,12},{10,14},{12,8},{14,10},{1,5},{3,7},... | collective-permute-start | bytes 245768 | tf_op jit(solution)/shard_map/ppermute | solution.py:379
  98.1 1.3 %collective-permute-start.31 = (bf16[80,512]{1,0:T(8,128)(2,1)S(1)}, bf16[80,512]{1,0:T(8,128)(2,1)S(1)}, u32[]{:S(2)}, u32[]{:S(2)}) collective-permute-start(bf16[80,512]{1,0:T(8,128)(2,1)S(1)} %get-tuple-element.67.refs_2_), channel_id=1, source_target_pairs={{0,8},{2,10},{4,12},{6,14},{8,0},{10,2},{12,4},{14,6},{1,9},{3,11}... | collective-permute-start | bytes 245768 | tf_op jit(solution)/shard_map/ppermute | solution.py:379
  99.3 1.4 %collective-permute-start.33 = (bf16[80,512]{1,0:T(8,128)(2,1)S(1)}, bf16[80,512]{1,0:T(8,128)(2,1)S(1)}, u32[]{:S(2)}, u32[]{:S(2)}) collective-permute-start(bf16[80,512]{1,0:T(8,128)(2,1)S(1)} %get-tuple-element.67.refs_2_), channel_id=1, source_target_pairs={{0,12},{2,14},{4,8},{6,10},{8,4},{10,6},{12,0},{14,2},{1,13},{3,15... | collective-permute-start | bytes 245768 | tf_op jit(solution)/shard_map/ppermute | solution.py:379
  101.5 1.3 %collective-permute-start.30 = (bf16[80,512]{1,0:T(8,128)(2,1)S(1)}, bf16[80,512]{1,0:T(8,128)(2,1)S(1)}, u32[]{:S(2)}, u32[]{:S(2)}) collective-permute-start(bf16[80,512]{1,0:T(8,128)(2,1)S(1)} %collective-permute-done.29.refs_4_), channel_id=1, source_target_pairs={{0,2},{2,0},{4,6},{6,4},{8,10},{10,8},{12,14},{14,12},{1,3},{3,1},... | collective-permute-start | bytes 245768 | tf_op jit(solution)/shard_map/ppermute | solution.py:379
  102.8 4.7 %collective-permute-done.31.refs_6_ = bf16[80,512]{1,0:T(8,128)(2,1)S(1)} collective-permute-done((bf16[80,512]{1,0:T(8,128)(2,1)S(1)}, bf16[80,512]{1,0:T(8,128)(2,1)S(1)}, u32[]{:S(2)}, u32[]{:S(2)}) %collective-permute-start.31) | collective-permute-done | bytes 81952 | tf_op jit(solution)/shard_map/ppermute | solution.py:379
  107.6 1.8 %collective-permute-start.34 = (bf16[80,512]{1,0:T(8,128)(2,1)S(1)}, bf16[80,512]{1,0:T(8,128)(2,1)S(1)}, u32[]{:S(2)}, u32[]{:S(2)}) collective-permute-start(bf16[80,512]{1,0:T(8,128)(2,1)S(1)} %collective-permute-done.33.refs_8_), channel_id=1, source_target_pairs={{0,2},{2,0},{4,6},{6,4},{8,10},{10,8},{12,14},{14,12},{1,3},{3,1},... | collective-permute-start | bytes 245768 | tf_op jit(solution)/shard_map/ppermute | solution.py:379
  109.6 2.3 %collective-permute-done.32.refs_7_ = bf16[80,512]{1,0:T(8,128)(2,1)S(1)} collective-permute-done((bf16[80,512]{1,0:T(8,128)(2,1)S(1)}, bf16[80,512]{1,0:T(8,128)(2,1)S(1)}, u32[]{:S(2)}, u32[]{:S(2)}) %collective-permute-start.32) | collective-permute-done | bytes 81952 | tf_op jit(solution)/shard_map/ppermute | solution.py:379
  113.8 1.8 %shard_map.149.refs_4_ = bf16[4,512,64]{2,1,0:T(8,128)(2,1)S(1)} custom-call(s32[3]{0:T(128)S(1)} %pad_add_fusion.scalar_ref, s32[1,64]{1,0:T(1,128)S(1)} %bitcast.35, s32[64,1]{1,0:T(8,128)S(1)} %copy.20.refs_1_, bf16[64,4096]{1,0:T(8,128)(2,1)S(1)} %bitcast.44, bf16[64,512]{1,0:T(8,128)(2,1)S(1)} %bitcast.49), custom_call_target="tpu_custom_call" | custom-call | flops 1000000000 | bytes 1048576 | tf_op jit(solution)/shard_map/pallas_call | solution.py:54
  115.6 1.9 %shard_map.150 = (bf16[64,4096]{1,0:T(8,128)(2,1)}, f32[64,1024]{1,0:T(8,128)}, f32[64,512]{1,0:T(8,128)}) custom-call(s32[3]{0:T(128)S(1)} %pad_add_fusion.scalar_ref, f32[64,512]{1,0:T(8,128)S(1)} %get-tuple-element.55.refs_0_, f32[64,64]{1,0:T(8,128)S(1)} %get-tuple-element.68.refs_1_, f32[64,64]{1,0:T(8,128)S(1)} %collective-permute-done.35.refs_2_, ...), custom_call_target="tpu_custom_call" | custom-call | flops 200000000 | bytes 1048576 | tf_op jit(solution)/shard_map/pallas_call | solution.py:54
  (90 shorter events, 12.8 us)
Async XLA Ops:
  0.6 44.4 %copy-start.2 = (bf16[1,64,8192]{2,1,0:T(8,128)(2,1)S(1)}, bf16[1,64,8192]{2,1,0:T(8,128)(2,1)}, u32[]{:S(2)}) copy-start(bf16[1,64,8192]{2,1,0:T(8,128)(2,1)} %param.20) | copy-start | bytes 3145732
  0.6 42.1 %copy-start.15 = (s32[1,1,256]{2,1,0:T(1,128)S(1)}, s32[1,1,256]{2,1,0:T(1,128)}, u32[]{:S(2)}) copy-start(s32[1,1,256]{2,1,0:T(1,128)} %param.16) | copy-start | bytes 3076
  0.7 44.4 %collective-permute-start.10 = (bf16[256,8192]{1,0:T(8,128)(2,1)}, bf16[256,8192]{1,0:T(8,128)(2,1)}, u32[]{:S(2)}, u32[]{:S(2)}) collective-permute-start(bf16[256,8192]{1,0:T(8,128)(2,1)} %bitcast.17), channel_id=1, source_target_pairs={{0,1},{1,0},{2,3},{3,2},{4,5},{5,4},{6,7},{7,6},{8,9},{9,8},{10,11... | collective-permute-start | bytes 12582920 | tf_op jit(solution)/shard_map/ppermute | solution.py:376
  3.2 10.4 %collective-permute-start.12 = (bf16[288,512]{1,0:T(8,128)(2,1)S(1)}, bf16[288,512]{1,0:T(8,128)(2,1)S(1)}, u32[]{:S(2)}, u32[]{:S(2)}) collective-permute-start(bf16[288,512]{1,0:T(8,128)(2,1)S(1)} %pad_maximum_fusion.1.refs_5_), channel_id=1, source_target_pairs={{0,4},{4,8},{8,12},{12,14},{14,10},{10,6},{6,2},{2,0},{1,5},{5,9},... | collective-permute-start | bytes 884744 | tf_op jit(solution)/shard_map/ppermute | solution.py:430
  5.9 9.8 %collective-permute-start.4 = (bf16[288,512]{1,0:T(8,128)(2,1)S(1)}, bf16[288,512]{1,0:T(8,128)(2,1)S(1)}, u32[]{:S(2)}, u32[]{:S(2)}) collective-permute-start(bf16[288,512]{1,0:T(8,128)(2,1)S(1)} %pad_maximum_fusion.1.refs_5_), channel_id=1, source_target_pairs={{4,0},{8,4},{12,8},{14,12},{10,14},{6,10},{2,6},{0,2},{5,1},{9,5},... | collective-permute-start | bytes 884744 | tf_op jit(solution)/shard_map/ppermute | solution.py:430
  5.9 38.7 %collective-permute-start.11 = (bf16[64,8192]{1,0:T(8,128)(2,1)}, bf16[64,8192]{1,0:T(8,128)(2,1)S(1)}, u32[]{:S(2)}, u32[]{:S(2)}) collective-permute-start(bf16[64,8192]{1,0:T(8,128)(2,1)} %bitcast.22), channel_id=1, source_target_pairs={{0,1},{1,0},{2,3},{3,2},{4,5},{5,4},{6,7},{7,6},{8,9},{9,8},{10,11... | collective-permute-start | bytes 3145736 | tf_op jit(solution)/shard_map/ppermute | solution.py:376
  6.1 13.9 %collective-permute-start = (bf16[288,512]{1,0:T(8,128)(2,1)S(1)}, bf16[288,512]{1,0:T(8,128)(2,1)S(1)}, u32[]{:S(2)}, u32[]{:S(2)}) collective-permute-start(bf16[288,512]{1,0:T(8,128)(2,1)S(1)} %pad_maximum_fusion.refs_4_), channel_id=1, source_target_pairs={{0,4},{4,8},{8,12},{12,14},{14,10},{10,6},{6,2},{2,0},{1,5},{5,9},... | collective-permute-start | bytes 884744 | tf_op jit(solution)/shard_map/ppermute | solution.py:430
  13.7 9.1 %collective-permute-start.15 = (bf16[288,512]{1,0:T(8,128)(2,1)S(1)}, bf16[288,512]{1,0:T(8,128)(2,1)S(1)}, u32[]{:S(2)}, u32[]{:S(2)}) collective-permute-start(bf16[288,512]{1,0:T(8,128)(2,1)S(1)} %pad_maximum_fusion.refs_4_), channel_id=1, source_target_pairs={{4,0},{8,4},{12,8},{14,12},{10,14},{6,10},{2,6},{0,2},{5,1},{9,5},... | collective-permute-start | bytes 884744 | tf_op jit(solution)/shard_map/ppermute | solution.py:430
  15.7 10.7 %collective-permute-start.13 = (bf16[288,512]{1,0:T(8,128)(2,1)S(1)}, bf16[288,512]{1,0:T(8,128)(2,1)}, u32[]{:S(2)}, u32[]{:S(2)}) collective-permute-start(bf16[288,512]{1,0:T(8,128)(2,1)S(1)} %collective-permute-done.12.refs_7_), channel_id=1, source_target_pairs={{0,4},{4,8},{8,12},{12,14},{14,10},{10,6},{6,2},{2,0},{1,5},{5,9},... | collective-permute-start | bytes 884744 | tf_op jit(solution)/shard_map/ppermute | solution.py:430
  20.0 9.1 %collective-permute-start.5 = (bf16[288,512]{1,0:T(8,128)(2,1)S(1)}, bf16[288,512]{1,0:T(8,128)(2,1)S(1)}, u32[]{:S(2)}, u32[]{:S(2)}) collective-permute-start(bf16[288,512]{1,0:T(8,128)(2,1)S(1)} %collective-permute-done.4.refs_9_), channel_id=1, source_target_pairs={{4,0},{8,4},{12,8},{14,12},{10,14},{6,10},{2,6},{0,2},{5,1},{9,5},... | collective-permute-start | bytes 884744 | tf_op jit(solution)/shard_map/ppermute | solution.py:430
  22.7 9.8 %collective-permute-start.1 = (bf16[288,512]{1,0:T(8,128)(2,1)S(1)}, bf16[288,512]{1,0:T(8,128)(2,1)}, u32[]{:S(2)}, u32[]{:S(2)}) collective-permute-start(bf16[288,512]{1,0:T(8,128)(2,1)S(1)} %collective-permute-done.refs_6_), channel_id=1, source_target_pairs={{0,4},{4,8},{8,12},{12,14},{14,10},{10,6},{6,2},{2,0},{1,5},{5,9},... | collective-permute-start | bytes 884744 | tf_op jit(solution)/shard_map/ppermute | solution.py:430
  26.4 10.1 %collective-permute-start.16 = (bf16[288,512]{1,0:T(8,128)(2,1)S(1)}, bf16[288,512]{1,0:T(8,128)(2,1)}, u32[]{:S(2)}, u32[]{:S(2)}) collective-permute-start(bf16[288,512]{1,0:T(8,128)(2,1)S(1)} %collective-permute-done.15.refs_8_), channel_id=1, source_target_pairs={{4,0},{8,4},{12,8},{14,12},{10,14},{6,10},{2,6},{0,2},{5,1},{9,5},... | collective-permute-start | bytes 884744 | tf_op jit(solution)/shard_map/ppermute | solution.py:430
  29.1 12.2 %collective-permute-start.6 = (bf16[288,512]{1,0:T(8,128)(2,1)S(1)}, bf16[288,512]{1,0:T(8,128)(2,1)S(1)}, u32[]{:S(2)}, u32[]{:S(2)}) collective-permute-start(bf16[288,512]{1,0:T(8,128)(2,1)S(1)} %collective-permute-done.5.refs_13_), channel_id=1, source_target_pairs={{4,0},{8,4},{12,8},{14,12},{10,14},{6,10},{2,6},{0,2},{5,1},{9,5},... | collective-permute-start | bytes 884744 | tf_op jit(solution)/shard_map/ppermute | solution.py:430
  32.5 10.5 %collective-permute-start.2 = (bf16[288,512]{1,0:T(8,128)(2,1)}, bf16[288,512]{1,0:T(8,128)(2,1)S(1)}, u32[]{:S(2)}, u32[]{:S(2)}) collective-permute-start(bf16[288,512]{1,0:T(8,128)(2,1)} %collective-permute-done.1.refs_10_), channel_id=1, source_target_pairs={{0,4},{4,8},{8,12},{12,14},{14,10},{10,6},{6,2},{2,0},{1,5},{5,9},... | collective-permute-start | bytes 884744 | tf_op jit(solution)/shard_map/ppermute | solution.py:430
  36.5 20.5 %collective-permute-start.14 = (bf16[288,512]{1,0:T(8,128)(2,1)}, bf16[288,512]{1,0:T(8,128)(2,1)}, u32[]{:S(2)}, u32[]{:S(2)}) collective-permute-start(bf16[288,512]{1,0:T(8,128)(2,1)} %collective-permute-done.13.refs_11_), channel_id=1, source_target_pairs={{0,4},{4,8},{8,12},{12,14},{14,10},{10,6},{6,2},{2,0},{1,5},{5,9},... | collective-permute-start | bytes 884744 | tf_op jit(solution)/shard_map/ppermute | solution.py:430
  41.3 15.6 %collective-permute-start.17 = (bf16[288,512]{1,0:T(8,128)(2,1)}, bf16[288,512]{1,0:T(8,128)(2,1)}, u32[]{:S(2)}, u32[]{:S(2)}) collective-permute-start(bf16[288,512]{1,0:T(8,128)(2,1)} %collective-permute-done.16.refs_12_), channel_id=1, source_target_pairs={{4,0},{8,4},{12,8},{14,12},{10,14},{6,10},{2,6},{0,2},{5,1},{9,5},... | collective-permute-start | bytes 884744 | tf_op jit(solution)/shard_map/ppermute | solution.py:430
  43.0 21.3 %collective-permute-start.7 = (bf16[288,512]{1,0:T(8,128)(2,1)S(1)}, bf16[288,512]{1,0:T(8,128)(2,1)S(1)}, u32[]{:S(2)}, u32[]{:S(2)}) collective-permute-start(bf16[288,512]{1,0:T(8,128)(2,1)S(1)} %collective-permute-done.6.refs_7_), channel_id=1, source_target_pairs={{4,0},{8,4},{12,8},{14,12},{10,14},{6,10},{2,6},{0,2},{5,1},{9,5},... | collective-permute-start | bytes 884744 | tf_op jit(solution)/shard_map/ppermute | solution.py:430
  44.6 20.3 %collective-permute-start.3 = (bf16[288,512]{1,0:T(8,128)(2,1)S(1)}, bf16[288,512]{1,0:T(8,128)(2,1)S(1)}, u32[]{:S(2)}, u32[]{:S(2)}) collective-permute-start(bf16[288,512]{1,0:T(8,128)(2,1)S(1)} %collective-permute-done.2.refs_4_), channel_id=1, source_target_pairs={{0,4},{4,8},{8,12},{12,14},{14,10},{10,6},{6,2},{2,0},{1,5},{5,9},... | collective-permute-start | bytes 884744 | tf_op jit(solution)/shard_map/ppermute | solution.py:430
  45.1 2.2 %copy-start = (bf16[1,256,8192]{2,1,0:T(8,128)(2,1)S(1)}, bf16[1,256,8192]{2,1,0:T(8,128)(2,1)}, u32[]{:S(2)}) copy-start(bf16[1,256,8192]{2,1,0:T(8,128)(2,1)} %param.12) | copy-start | bytes 12582916
  57.0 3.7 %copy-start.17 = (bf16[1,256,4096]{2,1,0:T(8,128)(2,1)S(1)}, bf16[1,256,4096]{2,1,0:T(8,128)(2,1)}, u32[]{:S(2)}) copy-start(bf16[1,256,4096]{2,1,0:T(8,128)(2,1)} %param.13) | copy-start | bytes 6291460
  57.0 3.7 %copy-start.18 = (bf16[1,256,4096]{2,1,0:T(8,128)(2,1)S(1)}, bf16[1,256,4096]{2,1,0:T(8,128)(2,1)}, u32[]{:S(2)}) copy-start(bf16[1,256,4096]{2,1,0:T(8,128)(2,1)} %param.15) | copy-start | bytes 6291460
  57.0 3.7 %copy-start.20 = (bf16[1,256,512]{2,1,0:T(8,128)(2,1)S(1)}, bf16[1,256,512]{2,1,0:T(8,128)(2,1)}, u32[]{:S(2)}) copy-start(bf16[1,256,512]{2,1,0:T(8,128)(2,1)} %param.14) | copy-start | bytes 786436
  60.6 8.0 %collective-permute-start.18 = (f32[352,512]{1,0:T(8,128)S(1)}, f32[352,512]{1,0:T(8,128)S(1)}, u32[]{:S(2)}, u32[]{:S(2)}) collective-permute-start(f32[352,512]{1,0:T(8,128)S(1)} %get-tuple-element.42), channel_id=1, source_target_pairs={{0,1},{1,0},{2,3},{3,2},{4,5},{5,4},{6,7},{7,6},{8,9},{9,8},{10,11... | collective-permute-start | bytes 2162696 | tf_op jit(solution)/shard_map/ppermute | solution.py:376
  64.3 4.2 %collective-permute-start.9 = (bf16[288,512]{1,0:T(8,128)(2,1)S(1)}, bf16[288,512]{1,0:T(8,128)(2,1)S(1)}, u32[]{:S(2)}, u32[]{:S(2)}) collective-permute-start(bf16[288,512]{1,0:T(8,128)(2,1)S(1)} %collective-permute-done.7.refs_3_), channel_id=1, source_target_pairs={{0,1},{1,0},{2,3},{3,2},{4,5},{5,4},{6,7},{7,6},{8,9},{9,8},{10,11... | collective-permute-start | bytes 884744 | tf_op jit(solution)/shard_map/ppermute | solution.py:376
  64.9 3.7 %collective-permute-start.8 = (bf16[288,512]{1,0:T(8,128)(2,1)S(1)}, bf16[288,512]{1,0:T(8,128)(2,1)S(1)}, u32[]{:S(2)}, u32[]{:S(2)}) collective-permute-start(bf16[288,512]{1,0:T(8,128)(2,1)S(1)} %collective-permute-done.3.refs_2_), channel_id=1, source_target_pairs={{0,1},{1,0},{2,3},{3,2},{4,5},{5,4},{6,7},{7,6},{8,9},{9,8},{10,11... | collective-permute-start | bytes 884744 | tf_op jit(solution)/shard_map/ppermute | solution.py:376
  66.8 2.2 %copy-start.1 = (bf16[1,256,8192]{2,1,0:T(8,128)(2,1)S(1)}, bf16[1,256,8192]{2,1,0:T(8,128)(2,1)}, u32[]{:S(2)}) copy-start(bf16[1,256,8192]{2,1,0:T(8,128)(2,1)} %param.12) | copy-start | bytes 12582916
  71.3 1.7 %collective-permute-start.20 = (f32[64,512]{1,0:T(8,128)S(1)}, f32[64,512]{1,0:T(8,128)S(1)}, u32[]{:S(2)}, u32[]{:S(2)}) collective-permute-start(f32[64,512]{1,0:T(8,128)S(1)} %get-tuple-element.57.refs_4_), channel_id=1, source_target_pairs={{0,1},{1,0},{2,3},{3,2},{4,5},{5,4},{6,7},{7,6},{8,9},{9,8},{10,11... | collective-permute-start | bytes 393224 | tf_op jit(solution)/shard_map/ppermute | solution.py:376
  71.7 22.7 %copy-start.4 = (f32[1024,64]{0,1:T(8,128)S(1)}, f32[1024,64]{0,1:T(8,128)}, u32[]{:S(2)}) copy-start(f32[1024,64]{0,1:T(8,128)} %param.18) | copy-start | bytes 786436
  71.8 37.7 %copy-start.16 = (s32[1,1,64]{2,1,0:T(1,128)S(1)}, s32[1,1,64]{2,1,0:T(1,128)}, u32[]{:S(2)}) copy-start(s32[1,1,64]{2,1,0:T(1,128)} %param.23) | copy-start | bytes 772
  71.8 1.2 %collective-permute-start.19 = (bf16[64,256]{1,0:T(8,128)(2,1)S(1)}, bf16[64,256]{1,0:T(8,128)(2,1)S(1)}, u32[]{:S(2)}, u32[]{:S(2)}) collective-permute-start(bf16[64,256]{1,0:T(8,128)(2,1)S(1)} %get-tuple-element.56.refs_2_), channel_id=1, source_target_pairs={{0,1},{1,0},{2,3},{3,2},{4,5},{5,4},{6,7},{7,6},{8,9},{9,8},{10,11... | collective-permute-start | bytes 98312 | tf_op jit(solution)/shard_map/ppermute | solution.py:376
  76.0 37.7 %copy-start.21 = (bf16[1,64,512]{2,1,0:T(8,128)(2,1)S(1)}, bf16[1,64,512]{2,1,0:T(8,128)(2,1)}, u32[]{:S(2)}) copy-start(bf16[1,64,512]{2,1,0:T(8,128)(2,1)} %param.22) | copy-start | bytes 196612
  76.0 7.5 %collective-permute-start.21 = (bf16[72,512]{1,0:T(8,128)(2,1)S(1)}, bf16[72,512]{1,0:T(8,128)(2,1)S(1)}, u32[]{:S(2)}, u32[]{:S(2)}) collective-permute-start(bf16[72,512]{1,0:T(8,128)(2,1)S(1)} %get-tuple-element.60), channel_id=1, source_target_pairs={{0,2},{2,0},{4,6},{6,4},{8,10},{10,8},{12,14},{14,12},{1,3},{3,1},... | collective-permute-start | bytes 221192 | tf_op jit(solution)/shard_map/ppermute | solution.py:379
  77.7 9.2 %collective-permute-start.22 = (bf16[72,512]{1,0:T(8,128)(2,1)S(1)}, bf16[72,512]{1,0:T(8,128)(2,1)S(1)}, u32[]{:S(2)}, u32[]{:S(2)}) collective-permute-start(bf16[72,512]{1,0:T(8,128)(2,1)S(1)} %get-tuple-element.61), channel_id=1, source_target_pairs={{0,4},{2,6},{4,0},{6,2},{8,12},{10,14},{12,8},{14,10},{1,5},{3,7},... | collective-permute-start | bytes 221192 | tf_op jit(solution)/shard_map/ppermute | solution.py:379
  79.3 8.0 %collective-permute-start.23 = (bf16[72,512]{1,0:T(8,128)(2,1)S(1)}, bf16[72,512]{1,0:T(8,128)(2,1)S(1)}, u32[]{:S(2)}, u32[]{:S(2)}) collective-permute-start(bf16[72,512]{1,0:T(8,128)(2,1)S(1)} %get-tuple-element.62), channel_id=1, source_target_pairs={{0,6},{2,4},{4,2},{6,0},{8,14},{10,12},{12,10},{14,8},{1,7},{3,5},... | collective-permute-start | bytes 221192 | tf_op jit(solution)/shard_map/ppermute | solution.py:379
  79.6 7.7 %collective-permute-start.24 = (bf16[72,512]{1,0:T(8,128)(2,1)S(1)}, bf16[72,512]{1,0:T(8,128)(2,1)S(1)}, u32[]{:S(2)}, u32[]{:S(2)}) collective-permute-start(bf16[72,512]{1,0:T(8,128)(2,1)S(1)} %get-tuple-element.63), channel_id=1, source_target_pairs={{0,8},{2,10},{4,12},{6,14},{8,0},{10,2},{12,4},{14,6},{1,9},{3,11}... | collective-permute-start | bytes 221192 | tf_op jit(solution)/shard_map/ppermute | solution.py:379
  82.0 12.4 %collective-permute-start.25 = (bf16[72,512]{1,0:T(8,128)(2,1)S(1)}, bf16[72,512]{1,0:T(8,128)(2,1)S(1)}, u32[]{:S(2)}, u32[]{:S(2)}) collective-permute-start(bf16[72,512]{1,0:T(8,128)(2,1)S(1)} %get-tuple-element.64), channel_id=1, source_target_pairs={{0,10},{2,8},{4,14},{6,12},{8,2},{10,0},{12,6},{14,4},{1,11},{3,9}... | collective-permute-start | bytes 221192 | tf_op jit(solution)/shard_map/ppermute | solution.py:379
  83.5 10.9 %collective-permute-start.26 = (bf16[72,512]{1,0:T(8,128)(2,1)S(1)}, bf16[72,512]{1,0:T(8,128)(2,1)S(1)}, u32[]{:S(2)}, u32[]{:S(2)}) collective-permute-start(bf16[72,512]{1,0:T(8,128)(2,1)S(1)} %get-tuple-element.65), channel_id=1, source_target_pairs={{0,12},{2,14},{4,8},{6,10},{8,4},{10,6},{12,0},{14,2},{1,13},{3,15... | collective-permute-start | bytes 221192 | tf_op jit(solution)/shard_map/ppermute | solution.py:379
  86.9 7.5 %collective-permute-start.27 = (bf16[72,512]{1,0:T(8,128)(2,1)S(1)}, bf16[72,512]{1,0:T(8,128)(2,1)S(1)}, u32[]{:S(2)}, u32[]{:S(2)}) collective-permute-start(bf16[72,512]{1,0:T(8,128)(2,1)S(1)} %get-tuple-element.66), channel_id=1, source_target_pairs={{0,14},{2,12},{4,10},{6,8},{8,6},{10,4},{12,2},{14,0},{1,15},{3,13... | collective-permute-start | bytes 221192 | tf_op jit(solution)/shard_map/ppermute | solution.py:379
  95.1 6.4 %collective-permute-start.29 = (bf16[80,512]{1,0:T(8,128)(2,1)S(1)}, bf16[80,512]{1,0:T(8,128)(2,1)S(1)}, u32[]{:S(2)}, u32[]{:S(2)}) collective-permute-start(bf16[80,512]{1,0:T(8,128)(2,1)S(1)} %get-tuple-element.67.refs_2_), channel_id=1, source_target_pairs={{0,4},{2,6},{4,0},{6,2},{8,12},{10,14},{12,8},{14,10},{1,5},{3,7},... | collective-permute-start | bytes 245768 | tf_op jit(solution)/shard_map/ppermute | solution.py:379
  98.1 9.3 %collective-permute-start.31 = (bf16[80,512]{1,0:T(8,128)(2,1)S(1)}, bf16[80,512]{1,0:T(8,128)(2,1)S(1)}, u32[]{:S(2)}, u32[]{:S(2)}) collective-permute-start(bf16[80,512]{1,0:T(8,128)(2,1)S(1)} %get-tuple-element.67.refs_2_), channel_id=1, source_target_pairs={{0,8},{2,10},{4,12},{6,14},{8,0},{10,2},{12,4},{14,6},{1,9},{3,11}... | collective-permute-start | bytes 245768 | tf_op jit(solution)/shard_map/ppermute | solution.py:379
  99.3 8.3 %collective-permute-start.33 = (bf16[80,512]{1,0:T(8,128)(2,1)S(1)}, bf16[80,512]{1,0:T(8,128)(2,1)S(1)}, u32[]{:S(2)}, u32[]{:S(2)}) collective-permute-start(bf16[80,512]{1,0:T(8,128)(2,1)S(1)} %get-tuple-element.67.refs_2_), channel_id=1, source_target_pairs={{0,12},{2,14},{4,8},{6,10},{8,4},{10,6},{12,0},{14,2},{1,13},{3,15... | collective-permute-start | bytes 245768 | tf_op jit(solution)/shard_map/ppermute | solution.py:379
  100.7 8.8 %collective-permute-start.28 = (bf16[80,512]{1,0:T(8,128)(2,1)S(1)}, bf16[80,512]{1,0:T(8,128)(2,1)S(1)}, u32[]{:S(2)}, u32[]{:S(2)}) collective-permute-start(bf16[80,512]{1,0:T(8,128)(2,1)S(1)} %get-tuple-element.67.refs_2_), channel_id=1, source_target_pairs={{0,2},{2,0},{4,6},{6,4},{8,10},{10,8},{12,14},{14,12},{1,3},{3,1},... | collective-permute-start | bytes 245768 | tf_op jit(solution)/shard_map/ppermute | solution.py:379
  101.5 8.1 %collective-permute-start.30 = (bf16[80,512]{1,0:T(8,128)(2,1)S(1)}, bf16[80,512]{1,0:T(8,128)(2,1)S(1)}, u32[]{:S(2)}, u32[]{:S(2)}) collective-permute-start(bf16[80,512]{1,0:T(8,128)(2,1)S(1)} %collective-permute-done.29.refs_4_), channel_id=1, source_target_pairs={{0,2},{2,0},{4,6},{6,4},{8,10},{10,8},{12,14},{14,12},{1,3},{3,1},... | collective-permute-start | bytes 245768 | tf_op jit(solution)/shard_map/ppermute | solution.py:379
  107.4 4.4 %collective-permute-start.32 = (bf16[80,512]{1,0:T(8,128)(2,1)S(1)}, bf16[80,512]{1,0:T(8,128)(2,1)S(1)}, u32[]{:S(2)}, u32[]{:S(2)}) collective-permute-start(bf16[80,512]{1,0:T(8,128)(2,1)S(1)} %collective-permute-done.31.refs_6_), channel_id=1, source_target_pairs={{0,2},{2,0},{4,6},{6,4},{8,10},{10,8},{12,14},{14,12},{1,3},{3,1},... | collective-permute-start | bytes 245768 | tf_op jit(solution)/shard_map/ppermute | solution.py:379
  107.6 5.1 %collective-permute-start.34 = (bf16[80,512]{1,0:T(8,128)(2,1)S(1)}, bf16[80,512]{1,0:T(8,128)(2,1)S(1)}, u32[]{:S(2)}, u32[]{:S(2)}) collective-permute-start(bf16[80,512]{1,0:T(8,128)(2,1)S(1)} %collective-permute-done.33.refs_8_), channel_id=1, source_target_pairs={{0,2},{2,0},{4,6},{6,4},{8,10},{10,8},{12,14},{14,12},{1,3},{3,1},... | collective-permute-start | bytes 245768 | tf_op jit(solution)/shard_map/ppermute | solution.py:379
  109.4 6.1 %collective-permute-start.36 = (f32[64,512]{1,0:T(8,128)S(1)}, f32[64,512]{1,0:T(8,128)S(1)}, u32[]{:S(2)}, u32[]{:S(2)}) collective-permute-start(f32[64,512]{1,0:T(8,128)S(1)} %get-tuple-element.71.refs_5_), channel_id=1, source_target_pairs={{0,1},{1,0},{2,3},{3,2},{4,5},{5,4},{6,7},{7,6},{8,9},{9,8},{10,11... | collective-permute-start | bytes 393224 | tf_op jit(solution)/shard_map/ppermute | solution.py:376
  109.5 4.2 %copy-start.19 = (bf16[1,64,4096]{2,1,0:T(8,128)(2,1)S(1)}, bf16[1,64,4096]{2,1,0:T(8,128)(2,1)}, u32[]{:S(2)}) copy-start(bf16[1,64,4096]{2,1,0:T(8,128)(2,1)} %param.21) | copy-start | bytes 1572868
  113.7 1.9 %collective-permute-start.35 = (f32[64,64]{1,0:T(8,128)S(1)}, f32[64,64]{1,0:T(8,128)S(1)}, u32[]{:S(2)}, u32[]{:S(2)}) collective-permute-start(f32[64,64]{1,0:T(8,128)S(1)} %get-tuple-element.69), channel_id=1, source_target_pairs={{0,1},{1,0},{2,3},{3,2},{4,5},{5,4},{6,7},{7,6},{8,9},{9,8},{10,11... | collective-permute-start | bytes 49160 | tf_op jit(solution)/shard_map/ppermute | solution.py:376
  (11 other events, 10.5 us)
where the time goes:
time: 118 us; the launch traced here: 117 us
  starting transfers between devices  44.5 us (38%)
  waiting for transfers between devices  32.4 us (27%)
  Pallas kernels  26.3 us (22%)
  local copies, waits for them, and re-layouts  13.2 us (11%)
    pallas_call x12, Pallas kernels, call(): pl.pallas_call(whole, out_shape=[jax.ShapeDtypeStruct(*o) if i in final e...  26.3 us
    ppermute x14, starting transfers between devices, onward(): return lax.ppermute(array, 'fsdp', forward if ahead else backward)  21.5 us
    ppermute x14, starting transfers between devices, exchange(): return lax.ppermute(array, 'fsdp', [(i, i ^ k) for i in range(n_fsdp)])  20.9 us
    ppermute x14, waiting for transfers between devices, onward(): return lax.ppermute(array, 'fsdp', forward if ahead else backward)  16.3 us
    ppermute x14, waiting for transfers between devices, exchange(): return lax.ppermute(array, 'fsdp', [(i, i ^ k) for i in range(n_fsdp)])  15 us
    unnamed x44, local copies, waits for them, and re-layouts  10.9 us
  transfers between devices with their start and end apart: 37, of which 11 were waited for; matrix products, arithmetic and copies ran while one was open for 2% of the time, Pallas kernels for 16%

commit v1 on v0

--- a/solution.py
+++ b/solution.py
@@ -26,6 +26,7 @@
 VM = pl.BlockSpec(memory_space=pltpu.VMEM)
 SM = pl.BlockSpec(memory_space=pltpu.SMEM)
 ANY = pl.BlockSpec(memory_space=pl.ANY)
+HBM = pl.BlockSpec(memory_space=pltpu.MemorySpace.HBM)
 VMEM_GRANT = 16 * 2**20
 
 
@@ -43,6 +44,17 @@
 
 def near(array):
     return pltpu.with_memory_space_constraint(array, pltpu.VMEM)
+
+
+def far_off(array):
+    return pltpu.with_memory_space_constraint(array, pltpu.MemorySpace.HBM)
+
+
+def touch(s, arrays):
+    def kernel(s, refs, outs, scratch):
+        outs[0][...] = jnp.zeros_like(outs[0])
+
+    return call(kernel, [((8, 128), F32)], s, arrays)
 
 
 def call(kernel, outs, scalars, operands, scratch=(), flops=1e6, final=(), deps=()):
@@ -66,14 +78,20 @@
     return pl.ds(pl.multiple_of(start, 128), size)
 
 
+def same_segment(seg_row):
+    length = seg_row.shape[1]
+    across = jnp.broadcast_to(seg_row[...].astype(F32), (length, length))
+    return across == across.T
+
+
 def train_head_kernel(g, s, refs, outs, scratch):
-    seg_row, seg_col, q_ref, k_ref, t_ref = refs
+    seg_row, q_ref, k_ref, t_ref = refs
     high_out, rest_out, aimed_out = outs
     length = k_ref.shape[0]
     keys = k_ref[:, g * HEAD_DIM : (g + 1) * HEAD_DIM]
     row = lax.broadcasted_iota(jnp.int32, (length, length), 0)
     col = lax.broadcasted_iota(jnp.int32, (length, length), 1)
-    allowed = (row <= col) & (seg_col[...] == seg_row[...])
+    allowed = (row <= col) & same_segment(seg_row)
     lanes = [slice(h * HEAD_DIM, (h + 1) * HEAD_DIM) for h in range(g * GROUP, (g + 1) * GROUP)]
     every = []
     for j in range(GROUP):
@@ -89,22 +107,22 @@
     aimed_out[...] = sum(dot_nn(probs, t_ref[:, lanes[j]]) for j, probs in enumerate(every))
 
 
-def train_head(s, g, seg_row, seg_col, query, keyset, target, deps):
+def train_head(s, g, seg_row, query, keyset, target, deps):
     length = query.shape[0]
     return call(
         functools.partial(train_head_kernel, g),
         [((length, length), BF16), ((length, length), BF16), ((length, HEAD_DIM), F32)],
-        s, [seg_row, seg_col, query, keyset, target], flops=2e9, deps=deps,
+        s, [seg_row, query, keyset, target], flops=2e9, deps=deps,
     )
 
 
 def score_probs_kernel(s, refs, outs, scratch):
-    seg_row, seg_col, q_ref, k_ref = refs
+    seg_row, q_ref, k_ref = refs
     (p_ref,) = outs
     length = k_ref.shape[0]
     row = lax.broadcasted_iota(jnp.int32, (length, length), 0)
     col = lax.broadcasted_iota(jnp.int32, (length, length), 1)
-    allowed = (col <= row) & (seg_col[...] == seg_row[...])
+    allowed = (col <= row) & same_segment(seg_row)
     for g in range(KV_HEADS):
         keys = k_ref[:, g * HEAD_DIM : (g + 1) * HEAD_DIM]
         for j in range(GROUP):
@@ -116,12 +134,16 @@
             p_ref[g, j * length : (j + 1) * length, :] = probs.astype(BF16)
 
 
-def score_probs(s, seg_row, seg_col, query, keyset, deps):
+def score_probs(s, seg_row, query, keyset, deps):
     length = query.shape[0]
     return call(
         score_probs_kernel, [((KV_HEADS, GROUP * length, length), BF16)],
-        s, [seg_row, seg_col, query, keyset], flops=1e9, deps=deps,
+        s, [seg_row, query, keyset], flops=1e9, deps=deps,
     )[0]
+
+
+def apart(half):
+    return half * 5 // 16
 
 
 def unpack_down(packed, half):
@@ -139,34 +161,104 @@
     return jnp.concatenate([block[i * rows : (i + 1) * rows] for i in range(parts)], axis=1)
 
 
-def low_of(pieces, half):
-    return jnp.concatenate([unpack_down(p[half // 2 :, :], half) for p in pieces], axis=0)
-
-
-def features_of(position, n, shard, half, core):
+def assemble(s, half, a, y, c, buffer):
+    rows = apart(half)
+    buffer[pl.ds(pl.multiple_of(s[3] * rows, 16), rows), :] = a[...]
+    buffer[pl.ds(pl.multiple_of((1 - s[3]) * rows, 16), rows), :] = y[...]
+    buffer[2 * rows :, :] = c[: half - 2 * rows, :]
+    return unpack_down(c[half - 2 * rows :, :], half)
+
+
+def prepare_kernel(half, w_hbm, d_hbm, a, y, c, down, sems):
+    core, task = lax.axis_index("view") % 2, lax.axis_index("task") % 2
+    rows = apart(half)
+    rest = half - 2 * rows
+
+    def weight_rows(start, count):
+        return w_hbm.at[pl.ds(pl.multiple_of(core * half + start, 16), count), :]
+
+    copies = [
+        pltpu.make_async_copy(weight_rows(task * rows, rows), a, sems.at[0]),
+        pltpu.make_async_copy(weight_rows((1 - task) * rows, rows), y, sems.at[1]),
+        pltpu.make_async_copy(weight_rows(2 * rows, rest), c.at[pl.ds(0, rest), :], sems.at[2]),
+        pltpu.make_async_copy(d_hbm.at[:, lanes_at(core * half, half)], down, sems.at[3]),
+    ]
+    for copy in copies:
+        copy.start()
+    copies[3].wait()
+    c[rest:, :] = pack_down(down[...].astype(BF16), half)
+    for copy in copies[:3]:
+        copy.wait()
+
+
+def prepare(weight, down_t):
+    half = weight.shape[0] // 2
+    rows = apart(half)
+    sizes = (rows, rows, half - 2 * rows + RANK * half // VALUE_WIDTH)
+    return pl.pallas_call(
+        functools.partial(prepare_kernel, half),
+        out_shape=[pltpu.VMEM((size, VALUE_WIDTH), BF16) for size in sizes],
+        in_specs=[HBM, HBM],
+        out_specs=[VM] * 3,
+        scratch_shapes=[pltpu.VMEM((RANK, half), F32), pltpu.SemaphoreType.DMA((4,))],
+        cost_estimate=cost(1e6, 2**20),
+        compiler_params=pltpu.CompilerParams(vmem_limit_bytes=VMEM_GRANT),
+        name="prepare",
+    )(far_off(weight), far_off(down_t))
+
+
+def owner_of(position, n):
     position = lax.rem(position, n)
-    owner = jnp.where(position < n // 2, 2 * position, 2 * (n - 1 - position) + 1)
-    return owner * shard + core * half
+    return jnp.where(position < n // 2, 2 * position, 2 * (n - 1 - position) + 1)
+
+
+def fetch_kernel(n, half, s, refs, outs, scratch):
+    (sems,) = scratch
+    copies = []
+    for i, (source, out) in enumerate(zip(refs, outs)):
+        for j in range(n):
+            here = lanes_at(2 * half * j + (1 - s[1]) * half, half)
+            copies.append(
+                pltpu.make_async_copy(source.at[:, here], out.at[:, pl.ds(j * half, half)], sems.at[i * n + j])
+            )
+    for copy in copies:
+        copy.start()
+    for copy in copies:
+        copy.wait()
+
+
+def fetch(s, n, half, arrays):
+    def kernel(scalar_ref, *refs):
+        m = len(arrays)
+        fetch_kernel(n, half, scalar_ref, refs[:m], refs[m : 2 * m], refs[2 * m :])
+
+    return pl.pallas_call(
+        kernel,
+        out_shape=[pltpu.VMEM((a.shape[0], n * half), BF16) for a in arrays],
+        in_specs=[SM] + [HBM] * len(arrays),
+        out_specs=[VM] * len(arrays),
+        scratch_shapes=[pltpu.SemaphoreType.DMA((len(arrays) * n,))],
+        cost_estimate=cost(1e6, 2**21),
+        compiler_params=pltpu.CompilerParams(vmem_limit_bytes=VMEM_GRANT),
+        name="fetch",
+    )(s, *[far_off(a) for a in arrays])
 
 
 def project_kernel(n, offsets, half, s, refs, outs, scratch):
     x, xo, xs, xso = refs[:4]
     refs = refs[4:]
-    (xb,) = scratch
+    xb, wb, db = scratch
     t, u = x.shape[0], xs.shape[0]
-    rows = half // 2
-    total = low = None
     for i, offset in enumerate(offsets):
-        here = lanes_at(features_of(s[2] + offset, n, 2 * half, half, s[1]), half)
-        for at, a in ((0, x), (t, xo), (2 * t, xs), (2 * t + u, xso)):
-            xb[i, at : at + a.shape[0], :] = a[:, here]
-        pieces = [refs[2 * i][...], refs[2 * i + 1][...]]
-        weight = jnp.concatenate([p[:rows, :] for p in pieces], axis=0)
-        part = dot_nn(xb[i], weight)
-        total = part if total is None else total + part
-        part = dot_nt(low_of(pieces, half), xb[i, : 2 * t, :])
-        low = part if low is None else low + part
-    before = refs[2 * len(offsets) :]
+        owner = owner_of(s[2] + offset, n)
+        whole, packed = lanes_at(owner * 2 * half + s[1] * half, half), lanes_at(owner * half, half)
+        there = slice(i * half, (i + 1) * half)
+        for at, a, here in ((0, x, whole), (t, xo, packed), (2 * t, xs, whole), (2 * t + u, xso, packed)):
+            xb[at : at + a.shape[0], there] = a[:, here]
+        db[:, there] = assemble(s, half, *refs[3 * i : 3 * i + 3], wb.at[pl.ds(i * half, half), :])
+    total = dot_nn(xb[...], wb[...])
+    low = dot_nt(db[...], xb[: 2 * t, :])
+    before = refs[3 * len(offsets) :]
     if before:
         total = total + before[0][...]
         low = low + before[1][...]
@@ -191,29 +283,32 @@
     return call(
         functools.partial(project_kernel, n, offsets, half),
         outs, s, [*raw, *pieces, *before],
-        scratch=[pltpu.VMEM((len(offsets), 2 * t + 2 * u, half), BF16)],
+        scratch=[
+            pltpu.VMEM((2 * t + 2 * u, len(offsets) * half), BF16),
+            pltpu.VMEM((len(offsets) * half, VALUE_WIDTH), BF16),
+            pltpu.VMEM((RANK, len(offsets) * half), BF16),
+        ],
         flops=len(offsets) * 3.4e8,
     )
 
 
 def grad_kernel(n, offset, half, s, refs, outs, scratch):
     x, xs = refs[:2]
-    pieces, (mine, got, up_ref), heads = refs[2:6], refs[6:9], refs[9:]
+    pieces, (mine, got, up_ref), heads = refs[2:8], refs[8:11], refs[11:]
     base, d_low_out, up_grad = outs
+    wb, db = scratch
     t, u = x.shape[0], xs.shape[0]
-    rows = half // 2
     total = mine[:t, :] + got[:t, :]
     base_total = mine[t : t + u, :] + got[t : t + u, :]
     packed = mine[t + u :, :] + got[t + u :, :]
     low = jnp.concatenate([packed[:, :t], packed[:, t : 2 * t]], axis=0)
     for i in range(2):
-        core = s[1] if i == 0 else 1 - s[1]
-        here = lanes_at(features_of(s[2] + offset, n, 2 * half, half, core), half)
-        pair = [pieces[2 * i][...], pieces[2 * i + 1][...]]
-        weight = jnp.concatenate([p[:rows, :] for p in pair], axis=0)
-        total = total + dot_nn(x[:, here], weight)
-        base_total = base_total + dot_nn(xs[:, here], weight)
-        low = low + dot_nt(low_of(pair, half), x[:, here])
+        start = pl.multiple_of((s[1] if i == 0 else 1 - s[1]) * half, half)
+        db[:, lanes_at(start, half)] = assemble(s, half, *pieces[3 * i : 3 * i + 3], wb.at[pl.ds(start, half), :])
+    here = lanes_at(owner_of(s[2] + offset, n) * 2 * half, 2 * half)
+    total = total + dot_nn(x[:, here], wb[...])
+    base_total = base_total + dot_nn(xs[:, here], wb[...])
+    low = low + dot_nt(db[...], x[:, here])
     base[...] = base_total
     low = low.astype(BF16)
     up_half = up_ref[...].astype(BF16)
@@ -236,7 +331,7 @@
         functools.partial(grad_kernel, n, offset, half),
         [((u, VALUE_WIDTH), F32), ((RANK, t), BF16), ((RANK, VALUE_WIDTH), F32)],
         s, [*raw, *pieces, mine, got, up, *[a for h in heads for a in h]],
-        flops=1e9,
+        scratch=[pltpu.VMEM((2 * half, VALUE_WIDTH), BF16), pltpu.VMEM((RANK, 2 * half), BF16)], flops=1e9,
     )
 
 
@@ -247,27 +342,29 @@
     return pl.ds(row, UP_ROWS), lanes_at(col, half)
 
 
-def down_kernel(n, half, s, refs, outs, scratch):
+def down_kernel(chosen, half, s, refs, outs, scratch):
     x, xo, d_low, d_low_got, up_grad, up_got = refs
     (up_sum,) = scratch
-    keep, keep_up, *out = outs
+    outs = list(outs)
     up_sum[...] = up_grad[...] + up_got[...]
-    for k in [*range(n - 1, 0, -1), 0]:
-        here = lanes_at((s[0] ^ k) * 2 * half + s[1] * half, half)
-        part = dot_nn(d_low[...], x[:, here]) + dot_nn(d_low_got[...], xo[:, here])
+    for k in chosen:
+        here, packed = lanes_at((s[0] ^ k) * 2 * half + s[1] * half, half), lanes_at((s[0] ^ k) * half, half)
+        part = dot_nn(d_low[...], x[:, here]) + dot_nn(d_low_got[...], xo[:, packed])
         up_piece = up_sum[up_place(s[0] ^ k, half)]
         if k == 0:
-            keep[...] = part
-            keep_up[...] = up_piece
+            outs.pop(0)[...] = part
+            outs.pop(0)[...] = up_piece
         else:
-            out[k - 1][:RANK, :] = part.astype(BF16)
-            out[k - 1][RANK:, :] = up_piece.astype(BF16)
-
-
-def down_pieces(s, n, half, d_low, d_low_got, up_grad, up_got, raw):
-    return call(
-        functools.partial(down_kernel, n, half),
-        [((RANK, half), F32), ((UP_ROWS, half), F32)] + [((RANK + UP_ROWS, half), BF16)] * (n - 1),
+            out = outs.pop(0)
+            out[:RANK, :] = part.astype(BF16)
+            out[RANK:, :] = up_piece.astype(BF16)
+
+
+def down_pieces(s, chosen, half, d_low, d_low_got, up_grad, up_got, raw):
+    keep = [((RANK, half), F32), ((UP_ROWS, half), F32)]
+    return call(
+        functools.partial(down_kernel, chosen, half),
+        [o for k in chosen for o in (keep if k == 0 else [((RANK + UP_ROWS, half), BF16)])],
         s, [*raw, d_low, d_low_got, up_grad, up_got],
         scratch=[pltpu.VMEM((RANK, VALUE_WIDTH), F32)], flops=1e9,
     )
@@ -310,7 +407,7 @@
         message = messages[k]
         part = dot_nt(xs[:, here], message[:RANK, :])
         low_mine = part if low_mine is None else low_mine + part
-        part = dot_nt(xso[:, here], message[:RANK, :])
+        part = dot_nt(xso[:, lanes_at((s[0] ^ k) * half, half)], message[:RANK, :])
         low_other = part if low_other is None else low_other + part
         high = message[RANK : RANK + UP_ROWS, :].astype(F32)
         up[up_place(s[0] ^ k, half)] = high + message[RANK + UP_ROWS :, :].astype(F32)
@@ -355,11 +452,13 @@
 
 
 def reduce_order(n):
-    return [*range(n - 2, 0, -2), *range(n - 1, 0, -2)]
+    far = [*range(n - 2, n // 2 - 1, -2), *range(n - 1, n // 2, -2)]
+    near_by = [*range(n // 2 - 1, 0, -1)]
+    return far, near_by
 
 
 def solution(mesh):
-    n_fsdp, n_view = mesh.shape["fsdp"], mesh.shape["view"]
+    n_fsdp, n_view, n_task = mesh.shape["fsdp"], mesh.shape["view"], mesh.shape["task"]
     line = n_fsdp // 2
 
     def ring_device(place):
@@ -402,67 +501,68 @@
         me = lax.axis_index("fsdp")
         core = lax.axis_index("view") % 2
         place = jnp.where(me % 2 == 0, me // 2, n_fsdp - 1 - me // 2)
-        s = jnp.stack([me, core, place]).astype(jnp.int32)
+        s = jnp.stack([me, core, place, lax.axis_index("task") % 2]).astype(jnp.int32)
 
         down_t = adapter_down.T
-        down_half = down_t.astype(BF16)
-        my_down = lax.dynamic_slice_in_dim(down_half, core * half, half, 1)
-        my_weight = lax.dynamic_slice_in_dim(value_weight, core * half, half, 0)
-        pieces = [
-            jnp.concatenate(
-                [
-                    my_weight[q * half // 2 : (q + 1) * half // 2],
-                    pack_down(my_down[q * RANK // 2 : (q + 1) * RANK // 2], half),
-                ],
-                axis=0,
-            )
-            for q in range(2)
-        ]
-
-        seg_row, seg_col = train_segments.reshape(1, -1), train_segments.reshape(-1, 1)
-        sseg_row, sseg_col = score_segments.reshape(1, -1), score_segments.reshape(-1, 1)
+        a_piece, y_piece, c_piece = prepare(value_weight, down_t)
+
+        seg_row, sseg_row = train_segments.reshape(1, -1), score_segments.reshape(1, -1)
         near_query, near_keys, near_target = near(query), near(keyset), near(target)
 
         def head(g, deps):
-            return train_head(s, g, seg_row, seg_col, near_query, near_keys, near_target, deps)
+            return train_head(s, g, seg_row, near_query, near_keys, near_target, deps)
 
         def onward(array, ahead):
             return lax.ppermute(array, "fsdp", forward if ahead else backward)
 
+        def over_task(array):
+            return lax.ppermute(array, "task", [(i, i ^ 1) for i in range(n_task)])
+
         steps = n_fsdp // 2
-        arrived, offsets = list(pieces), [0]
-        ahead, back = list(pieces), list(pieces)
+        arrived, offsets = [a_piece, y_piece, c_piece], [0]
+        a_ahead = a_back = a_piece
+        c_ahead = c_back = c_piece
         heads = [None] * KV_HEADS
-        for k in range(1, steps + 1):
-            if k < steps:
-                for q in range(2):
-                    ahead[q] = onward(ahead[q], True)
-                    back[q] = onward(back[q], False)
-            else:
-                last = [onward(ahead[0], True), onward(back[1], False)]
+        for k in range(1, steps):
+            a_ahead, a_back = onward(a_ahead, True), onward(a_back, False)
+            c_ahead, c_back = onward(c_ahead, True), onward(c_back, False)
             if k == 1:
-                xo, xso = swap(x), swap(xs)
+                xo, xso = fetch(s, n_fsdp, half, (x, xs))
+                xo, xso = swap(xo), swap(xso)
                 raw = tuple(near(a) for a in (x, xo, xs, xso))
-                heads[0] = head(0, ())
-                probs = score_probs(s, sseg_row, sseg_col, squery, skeyset, ())
+                touched = touch(s, (near_query, near_keys, near_target, seg_row))[0]
+                heads[0] = head(0, (touched,))
+                probs = score_probs(s, sseg_row, squery, skeyset, ())
             elif k == 2:
                 heads[1] = head(1, ())
                 heads[2] = head(2, ())
             elif k == 3:
                 partial = project(s, n_fsdp, offsets, half, arrived, (), raw, False)
                 cut = len(offsets)
-            if k < steps:
-                arrived += [*ahead, *back]
-                offsets += [n_fsdp - k, k]
-        sums, sums_out = project(s, n_fsdp, offsets[cut:], half, arrived[2 * cut :], partial, raw, True)
+            arrived += [a_ahead, over_task(a_ahead), c_ahead]
+            arrived += [a_back, over_task(a_back), c_back]
+            offsets += [n_fsdp - k, k]
+        a_last, c_last = onward(a_ahead, True), onward(c_back, False)
+        last = [a_last, over_task(a_last), c_last]
+        heads[3] = head(3, ())
+        sums, sums_out = project(s, n_fsdp, offsets[cut:], half, arrived[3 * cut :], partial, raw, True)
         sums_got = swap(sums_out)
-        heads[3] = head(3, ())
         last += [swap(a) for a in last]
         base, d_low, up_grad = value_grads(
             s, n_fsdp, steps, half, last, sums, sums_got, adapter_up, heads, (raw[0], raw[2])
         )
         d_low_got, up_got = swap(d_low), swap(up_grad)
-        keep, keep_up, *out = down_pieces(s, n_fsdp, half, d_low, d_low_got, up_grad, up_got, raw[:2])
+        far, near_by = reduce_order(n_fsdp)
+        out = [None] * (n_fsdp - 1)
+
+        def pieces_of(chosen):
+            return down_pieces(s, chosen, half, d_low, d_low_got, up_grad, up_got, raw[:2])
+
+        for k, array in zip(far, pieces_of(far)):
+            out[k - 1] = array
+        *some, keep, keep_up = pieces_of([*near_by, 0])
+        for k, array in zip(near_by, some):
+            out[k - 1] = array
         bit = 2
         while bit < n_view:
             keep, keep_up = (a + over_view(a, bit) for a in (keep, keep_up))
@@ -470,7 +570,7 @@
             bit *= 2
 
         got = [None] * len(out)
-        for k in reduce_order(n_fsdp):
+        for k in far + near_by:
             got[k - 1] = exchange(out[k - 1], k)
         fresh, message = update(s, keep, keep_up, down_t, adapter_up, got)
         messages = [message] + [None] * (n_fsdp - 1)

time: 118 us -> 120 us (1.017)
  local copies, waits for them, and re-layouts: 13.2 us -> 0.44 us
  waiting for transfers between devices: 32.4 us -> 44.8 us
  starting transfers between devices: 44.5 us -> 47.2 us
    unnamed x44 -> x22, local copies, waits for them, and re-layouts: 10.9 us -> 0.44 us
    ppermute x0 -> x7, starting transfers between devices: none -> 8.97 us  [over_task(): return lax.ppermute(array, 'task', [(i, i ^ 1) for i in range(n_task)])]
    ppermute x14, waiting for transfers between devices: 16.3 us -> 22.7 us  [onward(): return lax.ppermute(array, 'fsdp', forward if ahead else backward)]
    ppermute x0 -> x7, waiting for transfers between devices: none -> 5.39 us  [over_task(): return lax.ppermute(array, 'task', [(i, i ^ 1) for i in range(n_task)])]
    ppermute x14, starting transfers between devices: 21.5 us -> 17.5 us  [onward(): return lax.ppermute(array, 'fsdp', forward if ahead else backward)]
    pallas_call x12 -> x14, Pallas kernels: 26.3 us -> 22.3 us  [call(): pl.pallas_call(whole, out_shape=[jax.ShapeDtypeStruct(*o) if i in final e...]
    pallas_call x0 -> x2, Pallas kernels: none -> 3.79 us  [the longest x1 2.58 us: fetch(): pl.pallas_call(kernel, out_shape=[pltpu.VMEM((a.shape[0], n * half), BF16...]
    ppermute x14, starting transfers between devices: 20.9 us -> 18.9 us  [exchange(): return lax.ppermute(array, 'fsdp', [(i, i ^ k) for i in range(n_fsdp)])]
  transfers between devices with their start and end apart: 37 -> 45, of which waited for: 11 -> 20; matrix products, arithmetic and copies ran while one was open for 2% -> 0% of each run, Pallas kernels for 16% -> 15%
where the time goes in v1:
time: 120 us
  starting transfers between devices  47.2 us (39%)
  waiting for transfers between devices  44.8 us (37%)
  Pallas kernels  26.1 us (22%)
    ppermute x14, waiting for transfers between devices, onward(): return lax.ppermute(array, 'fsdp', forward if ahead else backward)  22.7 us
    pallas_call x14, Pallas kernels, call(): pl.pallas_call(whole, out_shape=[jax.ShapeDtypeStruct(*o) if i in final e...  22.3 us
    ppermute x14, starting transfers between devices, exchange(): return lax.ppermute(array, 'fsdp', [(i, i ^ k) for i in range(n_fsdp)])  18.9 us
    ppermute x14, starting transfers between devices, onward(): return lax.ppermute(array, 'fsdp', forward if ahead else backward)  17.5 us
    ppermute x14, waiting for transfers between devices, exchange(): return lax.ppermute(array, 'fsdp', [(i, i ^ k) for i in range(n_fsdp)])  15.5 us
    ppermute x7, starting transfers between devices, over_task(): return lax.ppermute(array, 'task', [(i, i ^ 1) for i in range(n_task)])  8.97 us
    ppermute x7, waiting for transfers between devices, over_task(): return lax.ppermute(array, 'task', [(i, i ^ 1) for i in range(n_task)])  5.39 us
    pallas_call x1, Pallas kernels, fetch(): pl.pallas_call(kernel, out_shape=[pltpu.VMEM((a.shape[0], n * half), BF16...  2.58 us
  transfers between devices with their start and end apart: 45, of which 20 were waited for; matrix products, arithmetic and copies ran while one was open for 0% of the time, Pallas kernels for 15%

profile of v1, /device:TPU:0, one launch (start us, length us, event | category | flops | bytes accessed | tf_op | source)
XLA Modules:
  0.0 119.7 jit_solution(13440152528183526725)
XLA Ops:
  0.7 2.6 %fetch.1 = (bf16[256,4096]{1,0:T(8,128)(2,1)S(1)}, bf16[64,4096]{1,0:T(8,128)(2,1)S(1)}) custom-call(s32[4]{0:T(128)S(1)} %pad_add_fusion.scalar_ref, bf16[256,8192]{1,0:T(8,128)(2,1)} %bitcast.16, bf16[64,8192]{1,0:T(8,128)(2,1)} %bitcast.22), custom_call_target="tpu_custom_call" | custom-call | flops 1000000 | bytes 2097152 | tf_op jit(solution)/shard_map/fetch/pallas_call | solution.py:235
  3.9 1.2 %prepare.1 = (bf16[160,512]{1,0:T(8,128)(2,1)S(1)}, bf16[160,512]{1,0:T(8,128)(2,1)S(1)}, bf16[256,512]{1,0:T(8,128)(2,1)S(1)}) custom-call(bf16[1024,512]{1,0:T(8,128)(2,1)} %w_hbm.1, f32[64,1024]{1,0:T(8,128)} %bitcast.37), custom_call_target="tpu_custom_call" | custom-call | flops 1000000 | bytes 1048576 | tf_op jit(solution)/shard_map/prepare/pallas_call | solution.py:198
  5.1 2.6 %collective-permute-start.15 = (bf16[256,512]{1,0:T(8,128)(2,1)S(1)}, bf16[256,512]{1,0:T(8,128)(2,1)S(1)}, u32[]{:S(2)}, u32[]{:S(2)}) collective-permute-start(bf16[256,512]{1,0:T(8,128)(2,1)S(1)} %get-tuple-element.45.refs_6_), channel_id=1, source_target_pairs={{0,4},{4,8},{8,12},{12,14},{14,10},{10,6},{6,2},{2,0},{1,5},{5,9},... | collective-permute-start | bytes 786440 | tf_op jit(solution)/shard_map/ppermute | solution.py:516
  7.8 2.0 %collective-permute-start = (bf16[160,512]{1,0:T(8,128)(2,1)S(1)}, bf16[160,512]{1,0:T(8,128)(2,1)S(1)}, u32[]{:S(2)}, u32[]{:S(2)}) collective-permute-start(bf16[160,512]{1,0:T(8,128)(2,1)S(1)} %get-tuple-element.44.refs_4_), channel_id=1, source_target_pairs={{0,4},{4,8},{8,12},{12,14},{14,10},{10,6},{6,2},{2,0},{1,5},{5,9},... | collective-permute-start | bytes 491528 | tf_op jit(solution)/shard_map/ppermute | solution.py:516
  9.8 8.3 %collective-permute-done.refs_7_ = bf16[160,512]{1,0:T(8,128)(2,1)S(1)} collective-permute-done((bf16[160,512]{1,0:T(8,128)(2,1)S(1)}, bf16[160,512]{1,0:T(8,128)(2,1)S(1)}, u32[]{:S(2)}, u32[]{:S(2)}) %collective-permute-start) | collective-permute-done | bytes 163872 | tf_op jit(solution)/shard_map/ppermute | solution.py:516
  18.1 1.8 %collective-permute-start.1 = (bf16[160,512]{1,0:T(8,128)(2,1)S(1)}, bf16[160,512]{1,0:T(8,128)(2,1)S(1)}, u32[]{:S(2)}, u32[]{:S(2)}) collective-permute-start(bf16[160,512]{1,0:T(8,128)(2,1)S(1)} %collective-permute-done.refs_7_), channel_id=1, source_target_pairs={{0,4},{4,8},{8,12},{12,14},{14,10},{10,6},{6,2},{2,0},{1,5},{5,9},... | collective-permute-start | bytes 491528 | tf_op jit(solution)/shard_map/ppermute | solution.py:516
  20.2 1.8 %collective-permute-start.22 = (bf16[160,512]{1,0:T(8,128)(2,1)S(1)}, bf16[160,512]{1,0:T(8,128)(2,1)S(1)}, u32[]{:S(2)}, u32[]{:S(2)}) collective-permute-start(bf16[160,512]{1,0:T(8,128)(2,1)S(1)} %collective-permute-done.refs_7_), channel_id=1, source_target_pairs={{0,16},{16,0},{1,17},{17,1},{2,18},{18,2},{3,19},{19,3},{4,20},{20... | collective-permute-start | bytes 491528 | tf_op jit(solution)/shard_map/ppermute | solution.py:519
  22.2 1.9 %collective-permute-done.1.refs_13_ = bf16[160,512]{1,0:T(8,128)(2,1)S(1)} collective-permute-done((bf16[160,512]{1,0:T(8,128)(2,1)S(1)}, bf16[160,512]{1,0:T(8,128)(2,1)S(1)}, u32[]{:S(2)}, u32[]{:S(2)}) %collective-permute-start.1) | collective-permute-done | bytes 163872 | tf_op jit(solution)/shard_map/ppermute | solution.py:516
  24.1 1.3 %collective-permute-done.19.refs_16_ = bf16[160,512]{1,0:T(8,128)(2,1)S(1)} collective-permute-done((bf16[160,512]{1,0:T(8,128)(2,1)S(1)}, bf16[160,512]{1,0:T(8,128)(2,1)S(1)}, u32[]{:S(2)}, u32[]{:S(2)}) %collective-permute-start.19) | collective-permute-done | bytes 163872 | tf_op jit(solution)/shard_map/ppermute | solution.py:516
  25.4 1.5 %collective-permute-start.24 = (bf16[160,512]{1,0:T(8,128)(2,1)S(1)}, bf16[160,512]{1,0:T(8,128)(2,1)S(1)}, u32[]{:S(2)}, u32[]{:S(2)}) collective-permute-start(bf16[160,512]{1,0:T(8,128)(2,1)S(1)} %collective-permute-done.1.refs_13_), channel_id=1, source_target_pairs={{0,16},{16,0},{1,17},{17,1},{2,18},{18,2},{3,19},{19,3},{4,20},{20... | collective-permute-start | bytes 491528 | tf_op jit(solution)/shard_map/ppermute | solution.py:519
  27.2 1.7 %collective-permute-start.6 = (bf16[256,512]{1,0:T(8,128)(2,1)S(1)}, bf16[256,512]{1,0:T(8,128)(2,1)S(1)}, u32[]{:S(2)}, u32[]{:S(2)}) collective-permute-start(bf16[256,512]{1,0:T(8,128)(2,1)S(1)} %collective-permute-done.5.refs_12_), channel_id=1, source_target_pairs={{4,0},{8,4},{12,8},{14,12},{10,14},{6,10},{2,6},{0,2},{5,1},{9,5},... | collective-permute-start | bytes 786440 | tf_op jit(solution)/shard_map/ppermute | solution.py:516
  28.9 1.8 %collective-permute-done.23.refs_11_ = bf16[160,512]{1,0:T(8,128)(2,1)S(1)} collective-permute-done((bf16[160,512]{1,0:T(8,128)(2,1)S(1)}, bf16[160,512]{1,0:T(8,128)(2,1)S(1)}, u32[]{:S(2)}, u32[]{:S(2)}) %collective-permute-start.23) | collective-permute-done | bytes 163872 | tf_op jit(solution)/shard_map/ppermute | solution.py:519
  30.7 1.7 %collective-permute-start.25 = (bf16[160,512]{1,0:T(8,128)(2,1)S(1)}, bf16[160,512]{1,0:T(8,128)(2,1)S(1)}, u32[]{:S(2)}, u32[]{:S(2)}) collective-permute-start(bf16[160,512]{1,0:T(8,128)(2,1)S(1)} %collective-permute-done.19.refs_16_), channel_id=1, source_target_pairs={{0,16},{16,0},{1,17},{17,1},{2,18},{18,2},{3,19},{19,3},{4,20},{20... | collective-permute-start | bytes 491528 | tf_op jit(solution)/shard_map/ppermute | solution.py:519
  32.5 1.8 %collective-permute-done.24.refs_14_ = bf16[160,512]{1,0:T(8,128)(2,1)S(1)} collective-permute-done((bf16[160,512]{1,0:T(8,128)(2,1)S(1)}, bf16[160,512]{1,0:T(8,128)(2,1)S(1)}, u32[]{:S(2)}, u32[]{:S(2)}) %collective-permute-start.24) | collective-permute-done | bytes 163872 | tf_op jit(solution)/shard_map/ppermute | solution.py:519
  34.3 1.7 %collective-permute-start.16 = (bf16[256,512]{1,0:T(8,128)(2,1)S(1)}, bf16[256,512]{1,0:T(8,128)(2,1)S(1)}, u32[]{:S(2)}, u32[]{:S(2)}) collective-permute-start(bf16[256,512]{1,0:T(8,128)(2,1)S(1)} %collective-permute-done.15.refs_9_), channel_id=1, source_target_pairs={{0,4},{4,8},{8,12},{12,14},{14,10},{10,6},{6,2},{2,0},{1,5},{5,9},... | collective-permute-start | bytes 786440 | tf_op jit(solution)/shard_map/ppermute | solution.py:516
  36.1 1.7 %collective-permute-start.2 = (bf16[160,512]{1,0:T(8,128)(2,1)S(1)}, bf16[160,512]{1,0:T(8,128)(2,1)S(1)}, u32[]{:S(2)}, u32[]{:S(2)}) collective-permute-start(bf16[160,512]{1,0:T(8,128)(2,1)S(1)} %collective-permute-done.1.refs_13_), channel_id=1, source_target_pairs={{0,4},{4,8},{8,12},{12,14},{14,10},{10,6},{6,2},{2,0},{1,5},{5,9},... | collective-permute-start | bytes 491528 | tf_op jit(solution)/shard_map/ppermute | solution.py:516
  38.2 5.4 %collective-permute-done.2.refs_4_ = bf16[160,512]{1,0:T(8,128)(2,1)S(1)} collective-permute-done((bf16[160,512]{1,0:T(8,128)(2,1)S(1)}, bf16[160,512]{1,0:T(8,128)(2,1)S(1)}, u32[]{:S(2)}, u32[]{:S(2)}) %collective-permute-start.2) | collective-permute-done | bytes 163872 | tf_op jit(solution)/shard_map/ppermute | solution.py:516
  43.6 1.2 collective-permute-start.20
  45.6 3.3 %collective-permute-done.20.refs_7_ = bf16[160,512]{1,0:T(8,128)(2,1)S(1)} collective-permute-done((bf16[160,512]{1,0:T(8,128)(2,1)S(1)}, bf16[160,512]{1,0:T(8,128)(2,1)S(1)}, u32[]{:S(2)}, u32[]{:S(2)}) %collective-permute-start.20) | collective-permute-done | bytes 163872 | tf_op jit(solution)/shard_map/ppermute | solution.py:516
  48.9 1.7 %collective-permute-start.14 = (bf16[160,512]{1,0:T(8,128)(2,1)S(1)}, bf16[160,512]{1,0:T(8,128)(2,1)S(1)}, u32[]{:S(2)}, u32[]{:S(2)}) collective-permute-start(bf16[160,512]{1,0:T(8,128)(2,1)S(1)} %collective-permute-done.2.refs_4_), channel_id=1, source_target_pairs={{0,16},{16,0},{1,17},{17,1},{2,18},{18,2},{3,19},{19,3},{4,20},{20... | collective-permute-start | bytes 491528 | tf_op jit(solution)/shard_map/ppermute | solution.py:519
  50.9 1.2 collective-permute-start.8
  52.1 3.3 %shard_map.139 = (f32[640,512]{1,0:T(8,128)S(1)}, f32[64,512]{1,0:T(8,128)S(1)}) custom-call(s32[4]{0:T(128)S(1)} %pad_add_fusion.scalar_ref, bf16[256,8192]{1,0:T(8,128)(2,1)S(1)} %bitcast.17, bf16[256,4096]{1,0:T(8,128)(2,1)S(1)} %collective-permute-done.12.refs_1_, bf16[64,8192]{1,0:T(8,128)(2,1)S(1)} %bitcast.23, ...), custom_call_target="tpu_custom_call" | custom-call | flops 1700000000 | bytes 1048576 | tf_op jit(solution)/shard_map/pallas_call | solution.py:66
  56.0 1.7 %shard_map.140 = (f32[352,512]{1,0:T(8,128)S(1)}, f32[352,512]{1,0:T(8,128)S(1)}) custom-call(s32[4]{0:T(128)S(1)} %pad_add_fusion.scalar_ref, bf16[256,8192]{1,0:T(8,128)(2,1)S(1)} %bitcast.18, bf16[256,4096]{1,0:T(8,128)(2,1)S(1)} %collective-permute-done.12.refs_1_, bf16[64,8192]{1,0:T(8,128)(2,1)S(1)} %bitcast.24, ...), custom_call_target="tpu_custom_call" | custom-call | flops 680000000 | bytes 1048576 | tf_op jit(solution)/shard_map/pallas_call | solution.py:66
  58.2 1.8 %shard_map.143 = (bf16[256,256]{1,0:T(8,128)(2,1)S(1)}, bf16[256,256]{1,0:T(8,128)(2,1)S(1)}, f32[256,128]{1,0:T(8,128)S(1)}) custom-call(s32[4]{0:T(128)S(1)} %pad_add_fusion.scalar_ref, s32[1,256]{1,0:T(1,128)S(1)} %bitcast.44, bf16[256,4096]{1,0:T(8,128)(2,1)S(1)} %bitcast.27, bf16[256,512]{1,0:T(8,128)(2,1)S(1)} %bitcast.39, bf16[256,4096]{1,0:T(8,128)(2,1)S(1)} %bitcast.32), custom_call_target="tpu_custom_call" | custom-call | flops 2000000000 | bytes 1048576 | tf_op jit(solution)/shard_map/pallas_call | solution.py:66
  60.0 2.2 %collective-permute-start.3 = (bf16[160,512]{1,0:T(8,128)(2,1)S(1)}, bf16[160,512]{1,0:T(8,128)(2,1)S(1)}, u32[]{:S(2)}, u32[]{:S(2)}) collective-permute-start(bf16[160,512]{1,0:T(8,128)(2,1)S(1)} %collective-permute-done.2.refs_4_), channel_id=1, source_target_pairs={{0,4},{4,8},{8,12},{12,14},{14,10},{10,6},{6,2},{2,0},{1,5},{5,9},... | collective-permute-start | bytes 491528 | tf_op jit(solution)/shard_map/ppermute | solution.py:516
  62.2 1.8 %shard_map.144 = (bf16[256,256]{1,0:T(8,128)(2,1)S(1)}, bf16[256,256]{1,0:T(8,128)(2,1)S(1)}, f32[256,128]{1,0:T(8,128)S(1)}) custom-call(s32[4]{0:T(128)S(1)} %pad_add_fusion.scalar_ref, s32[1,256]{1,0:T(1,128)S(1)} %bitcast.45, bf16[256,4096]{1,0:T(8,128)(2,1)S(1)} %bitcast.28, bf16[256,512]{1,0:T(8,128)(2,1)S(1)} %bitcast.40, bf16[256,4096]{1,0:T(8,128)(2,1)S(1)} %bitcast.33), custom_call_target="tpu_custom_call" | custom-call | flops 2000000000 | bytes 1048576 | tf_op jit(solution)/shard_map/pallas_call | solution.py:66
  64.0 2.5 %collective-permute-done.3.refs_2_ = bf16[160,512]{1,0:T(8,128)(2,1)S(1)} collective-permute-done((bf16[160,512]{1,0:T(8,128)(2,1)S(1)}, bf16[160,512]{1,0:T(8,128)(2,1)S(1)}, u32[]{:S(2)}, u32[]{:S(2)}) %collective-permute-start.3) | collective-permute-done | bytes 163872 | tf_op jit(solution)/shard_map/ppermute | solution.py:516
  66.4 1.7 %collective-permute-start.4 = (bf16[160,512]{1,0:T(8,128)(2,1)S(1)}, bf16[160,512]{1,0:T(8,128)(2,1)S(1)}, u32[]{:S(2)}, u32[]{:S(2)}) collective-permute-start(bf16[160,512]{1,0:T(8,128)(2,1)S(1)} %collective-permute-done.3.refs_2_), channel_id=1, source_target_pairs={{0,16},{16,0},{1,17},{17,1},{2,18},{18,2},{3,19},{19,3},{4,20},{20... | collective-permute-start | bytes 491528 | tf_op jit(solution)/shard_map/ppermute | solution.py:519
  68.1 1.8 %shard_map.145 = (bf16[256,256]{1,0:T(8,128)(2,1)S(1)}, bf16[256,256]{1,0:T(8,128)(2,1)S(1)}, f32[256,128]{1,0:T(8,128)S(1)}) custom-call(s32[4]{0:T(128)S(1)} %pad_add_fusion.scalar_ref, s32[1,256]{1,0:T(1,128)S(1)} %bitcast.46, bf16[256,4096]{1,0:T(8,128)(2,1)S(1)} %bitcast.29, bf16[256,512]{1,0:T(8,128)(2,1)S(1)} %bitcast.41, bf16[256,4096]{1,0:T(8,128)(2,1)S(1)} %bitcast.34), custom_call_target="tpu_custom_call" | custom-call | flops 2000000000 | bytes 1048576 | tf_op jit(solution)/shard_map/pallas_call | solution.py:66
  71.8 1.8 %shard_map.142 = (bf16[256,256]{1,0:T(8,128)(2,1)S(1)}, bf16[256,256]{1,0:T(8,128)(2,1)S(1)}, f32[256,128]{1,0:T(8,128)S(1)}) custom-call(s32[4]{0:T(128)S(1)} %pad_add_fusion.scalar_ref, s32[1,256]{1,0:T(1,128)S(1)} %bitcast.48, bf16[256,4096]{1,0:T(8,128)(2,1)S(1)} %bitcast.31, bf16[256,512]{1,0:T(8,128)(2,1)S(1)} %bitcast.43, ...), custom_call_target="tpu_custom_call" | custom-call | flops 2000000000 | bytes 1048576 | tf_op jit(solution)/shard_map/pallas_call | solution.py:66
  73.6 2.4 %shard_map.146 = (f32[64,512]{1,0:T(8,128)S(1)}, bf16[64,256]{1,0:T(8,128)(2,1)S(1)}, f32[64,512]{1,0:T(8,128)S(1)}) custom-call(s32[4]{0:T(128)S(1)} %pad_add_fusion.scalar_ref, bf16[256,8192]{1,0:T(8,128)(2,1)S(1)} %bitcast.19, bf16[64,8192]{1,0:T(8,128)(2,1)S(1)} %bitcast.25, bf16[160,512]{1,0:T(8,128)(2,1)S(1)} %collective-permute-done.3.refs_2_, ...), custom_call_target="tpu_custom_call" | custom-call | flops 1000000000 | bytes 1048576 | tf_op jit(solution)/shard_map/pallas_call | solution.py:66
  76.7 1.1 collective-permute-done.27.refs_3_
  77.8 1.0 shard_map.148
  78.9 3.2 %collective-permute-start.32 = (bf16[72,512]{1,0:T(8,128)(2,1)S(1)}, bf16[72,512]{1,0:T(8,128)(2,1)S(1)}, u32[]{:S(2)}, u32[]{:S(2)}) collective-permute-start(bf16[72,512]{1,0:T(8,128)(2,1)S(1)} %get-tuple-element.73), channel_id=1, source_target_pairs={{0,8},{2,10},{4,12},{6,14},{8,0},{10,2},{12,4},{14,6},{1,9},{3,11}... | collective-permute-start | bytes 221192 | tf_op jit(solution)/shard_map/ppermute | solution.py:478
  82.1 1.5 %collective-permute-start.33 = (bf16[72,512]{1,0:T(8,128)(2,1)S(1)}, bf16[72,512]{1,0:T(8,128)(2,1)S(1)}, u32[]{:S(2)}, u32[]{:S(2)}) collective-permute-start(bf16[72,512]{1,0:T(8,128)(2,1)S(1)} %get-tuple-element.74), channel_id=1, source_target_pairs={{0,10},{2,8},{4,14},{6,12},{8,2},{10,0},{12,6},{14,4},{1,11},{3,9}... | collective-permute-start | bytes 221192 | tf_op jit(solution)/shard_map/ppermute | solution.py:478
  83.6 3.9 %collective-permute-start.34 = (bf16[72,512]{1,0:T(8,128)(2,1)S(1)}, bf16[72,512]{1,0:T(8,128)(2,1)S(1)}, u32[]{:S(2)}, u32[]{:S(2)}) collective-permute-start(bf16[72,512]{1,0:T(8,128)(2,1)S(1)} %get-tuple-element.75), channel_id=1, source_target_pairs={{0,12},{2,14},{4,8},{6,10},{8,4},{10,6},{12,0},{14,2},{1,13},{3,15... | collective-permute-start | bytes 221192 | tf_op jit(solution)/shard_map/ppermute | solution.py:478
  88.6 1.5 %collective-permute-start.29 = (bf16[72,512]{1,0:T(8,128)(2,1)S(1)}, bf16[72,512]{1,0:T(8,128)(2,1)S(1)}, u32[]{:S(2)}, u32[]{:S(2)}) collective-permute-start(bf16[72,512]{1,0:T(8,128)(2,1)S(1)} %get-tuple-element.70), channel_id=1, source_target_pairs={{0,2},{2,0},{4,6},{6,4},{8,10},{10,8},{12,14},{14,12},{1,3},{3,1},... | collective-permute-start | bytes 221192 | tf_op jit(solution)/shard_map/ppermute | solution.py:478
  90.2 3.4 %collective-permute-done.33.refs_8_ = bf16[72,512]{1,0:T(8,128)(2,1)S(1)} collective-permute-done((bf16[72,512]{1,0:T(8,128)(2,1)S(1)}, bf16[72,512]{1,0:T(8,128)(2,1)S(1)}, u32[]{:S(2)}, u32[]{:S(2)}) %collective-permute-start.33) | collective-permute-done | bytes 73760 | tf_op jit(solution)/shard_map/ppermute | solution.py:478
  93.6 1.3 %collective-permute-start.31 = (bf16[72,512]{1,0:T(8,128)(2,1)S(1)}, bf16[72,512]{1,0:T(8,128)(2,1)S(1)}, u32[]{:S(2)}, u32[]{:S(2)}) collective-permute-start(bf16[72,512]{1,0:T(8,128)(2,1)S(1)} %get-tuple-element.72), channel_id=1, source_target_pairs={{0,6},{2,4},{4,2},{6,0},{8,14},{10,12},{12,10},{14,8},{1,7},{3,5},... | collective-permute-start | bytes 221192 | tf_op jit(solution)/shard_map/ppermute | solution.py:478
  95.3 3.5 %collective-permute-done.31.refs_6_ = bf16[72,512]{1,0:T(8,128)(2,1)S(1)} collective-permute-done((bf16[72,512]{1,0:T(8,128)(2,1)S(1)}, bf16[72,512]{1,0:T(8,128)(2,1)S(1)}, u32[]{:S(2)}, u32[]{:S(2)}) %collective-permute-start.31) | collective-permute-done | bytes 73760 | tf_op jit(solution)/shard_map/ppermute | solution.py:478
  100.3 3.9 %collective-permute-start.39 = (bf16[80,512]{1,0:T(8,128)(2,1)S(1)}, bf16[80,512]{1,0:T(8,128)(2,1)S(1)}, u32[]{:S(2)}, u32[]{:S(2)}) collective-permute-start(bf16[80,512]{1,0:T(8,128)(2,1)S(1)} %get-tuple-element.77.refs_2_), channel_id=1, source_target_pairs={{0,8},{2,10},{4,12},{6,14},{8,0},{10,2},{12,4},{14,6},{1,9},{3,11}... | collective-permute-start | bytes 245768 | tf_op jit(solution)/shard_map/ppermute | solution.py:478
  104.2 1.9 %collective-permute-start.36 = (bf16[80,512]{1,0:T(8,128)(2,1)S(1)}, bf16[80,512]{1,0:T(8,128)(2,1)S(1)}, u32[]{:S(2)}, u32[]{:S(2)}) collective-permute-start(bf16[80,512]{1,0:T(8,128)(2,1)S(1)} %get-tuple-element.77.refs_2_), channel_id=1, source_target_pairs={{0,2},{2,0},{4,6},{6,4},{8,10},{10,8},{12,14},{14,12},{1,3},{3,1},... | collective-permute-start | bytes 245768 | tf_op jit(solution)/shard_map/ppermute | solution.py:478
  106.3 2.6 %collective-permute-done.39.refs_6_ = bf16[80,512]{1,0:T(8,128)(2,1)S(1)} collective-permute-done((bf16[80,512]{1,0:T(8,128)(2,1)S(1)}, bf16[80,512]{1,0:T(8,128)(2,1)S(1)}, u32[]{:S(2)}, u32[]{:S(2)}) %collective-permute-start.39) | collective-permute-done | bytes 81952 | tf_op jit(solution)/shard_map/ppermute | solution.py:478
  109.1 1.4 %collective-permute-done.41.refs_8_ = bf16[80,512]{1,0:T(8,128)(2,1)S(1)} collective-permute-done((bf16[80,512]{1,0:T(8,128)(2,1)S(1)}, bf16[80,512]{1,0:T(8,128)(2,1)S(1)}, u32[]{:S(2)}, u32[]{:S(2)}) %collective-permute-start.41) | collective-permute-done | bytes 81952 | tf_op jit(solution)/shard_map/ppermute | solution.py:478
  110.9 2.4 %collective-permute-done.40.refs_7_ = bf16[80,512]{1,0:T(8,128)(2,1)S(1)} collective-permute-done((bf16[80,512]{1,0:T(8,128)(2,1)S(1)}, bf16[80,512]{1,0:T(8,128)(2,1)S(1)}, u32[]{:S(2)}, u32[]{:S(2)}) %collective-permute-start.40) | collective-permute-done | bytes 81952 | tf_op jit(solution)/shard_map/ppermute | solution.py:478
  113.3 1.7 %collective-permute-done.42.refs_9_ = bf16[80,512]{1,0:T(8,128)(2,1)S(1)} collective-permute-done((bf16[80,512]{1,0:T(8,128)(2,1)S(1)}, bf16[80,512]{1,0:T(8,128)(2,1)S(1)}, u32[]{:S(2)}, u32[]{:S(2)}) %collective-permute-start.42) | collective-permute-done | bytes 81952 | tf_op jit(solution)/shard_map/ppermute | solution.py:478
  116.0 1.7 %shard_map.151.refs_4_ = bf16[4,512,64]{2,1,0:T(8,128)(2,1)S(1)} custom-call(s32[4]{0:T(128)S(1)} %pad_add_fusion.scalar_ref, s32[1,64]{1,0:T(1,128)S(1)} %bitcast.51, bf16[64,4096]{1,0:T(8,128)(2,1)S(1)} %bitcast.49, bf16[64,512]{1,0:T(8,128)(2,1)S(1)} %bitcast.50), custom_call_target="tpu_custom_call" | custom-call | flops 1000000000 | bytes 1048576 | tf_op jit(solution)/shard_map/pallas_call | solution.py:66
  117.8 1.9 %shard_map.152 = (bf16[64,4096]{1,0:T(8,128)(2,1)}, f32[64,1024]{1,0:T(8,128)}, f32[64,512]{1,0:T(8,128)}) custom-call(s32[4]{0:T(128)S(1)} %pad_add_fusion.scalar_ref, f32[64,512]{1,0:T(8,128)S(1)} %get-tuple-element.65.refs_0_, f32[64,64]{1,0:T(8,128)S(1)} %get-tuple-element.78.refs_1_, f32[64,64]{1,0:T(8,128)S(1)} %collective-permute-done.43.refs_2_, ...), custom_call_target="tpu_custom_call" | custom-call | flops 200000000 | bytes 1048576 | tf_op jit(solution)/shard_map/pallas_call | solution.py:66
  (81 shorter events, 11.5 us)
Async XLA Ops:
  0.7 51.4 %copy-start = (bf16[1,256,8192]{2,1,0:T(8,128)(2,1)S(1)}, bf16[1,256,8192]{2,1,0:T(8,128)(2,1)}, u32[]{:S(2)}) copy-start(bf16[1,256,8192]{2,1,0:T(8,128)(2,1)} %param.12) | copy-start | bytes 12582916
  0.7 51.4 %copy-start.1 = (bf16[1,64,8192]{2,1,0:T(8,128)(2,1)S(1)}, bf16[1,64,8192]{2,1,0:T(8,128)(2,1)}, u32[]{:S(2)}) copy-start(bf16[1,64,8192]{2,1,0:T(8,128)(2,1)} %param.20) | copy-start | bytes 3145732
  3.3 48.8 %collective-permute-start.12 = (bf16[256,4096]{1,0:T(8,128)(2,1)S(1)}, bf16[256,4096]{1,0:T(8,128)(2,1)S(1)}, u32[]{:S(2)}, u32[]{:S(2)}) collective-permute-start(bf16[256,4096]{1,0:T(8,128)(2,1)S(1)} %get-tuple-element.46), channel_id=1, source_target_pairs={{0,1},{1,0},{2,3},{3,2},{4,5},{5,4},{6,7},{7,6},{8,9},{9,8},{10,11... | collective-permute-start | bytes 6291464 | tf_op jit(solution)/shard_map/ppermute | solution.py:475
  5.1 15.1 %collective-permute-start.15 = (bf16[256,512]{1,0:T(8,128)(2,1)S(1)}, bf16[256,512]{1,0:T(8,128)(2,1)S(1)}, u32[]{:S(2)}, u32[]{:S(2)}) collective-permute-start(bf16[256,512]{1,0:T(8,128)(2,1)S(1)} %get-tuple-element.45.refs_6_), channel_id=1, source_target_pairs={{0,4},{4,8},{8,12},{12,14},{14,10},{10,6},{6,2},{2,0},{1,5},{5,9},... | collective-permute-start | bytes 786440 | tf_op jit(solution)/shard_map/ppermute | solution.py:516
  7.8 14.2 %collective-permute-start.5 = (bf16[256,512]{1,0:T(8,128)(2,1)S(1)}, bf16[256,512]{1,0:T(8,128)(2,1)S(1)}, u32[]{:S(2)}, u32[]{:S(2)}) collective-permute-start(bf16[256,512]{1,0:T(8,128)(2,1)S(1)} %get-tuple-element.45.refs_6_), channel_id=1, source_target_pairs={{4,0},{8,4},{12,8},{14,12},{10,14},{6,10},{2,6},{0,2},{5,1},{9,5},... | collective-permute-start | bytes 786440 | tf_op jit(solution)/shard_map/ppermute | solution.py:516
  7.8 10.4 %collective-permute-start = (bf16[160,512]{1,0:T(8,128)(2,1)S(1)}, bf16[160,512]{1,0:T(8,128)(2,1)S(1)}, u32[]{:S(2)}, u32[]{:S(2)}) collective-permute-start(bf16[160,512]{1,0:T(8,128)(2,1)S(1)} %get-tuple-element.44.refs_4_), channel_id=1, source_target_pairs={{0,4},{4,8},{8,12},{12,14},{14,10},{10,6},{6,2},{2,0},{1,5},{5,9},... | collective-permute-start | bytes 491528 | tf_op jit(solution)/shard_map/ppermute | solution.py:516
  9.8 10.2 %collective-permute-start.18 = (bf16[160,512]{1,0:T(8,128)(2,1)S(1)}, bf16[160,512]{1,0:T(8,128)(2,1)S(1)}, u32[]{:S(2)}, u32[]{:S(2)}) collective-permute-start(bf16[160,512]{1,0:T(8,128)(2,1)S(1)} %get-tuple-element.44.refs_4_), channel_id=1, source_target_pairs={{4,0},{8,4},{12,8},{14,12},{10,14},{6,10},{2,6},{0,2},{5,1},{9,5},... | collective-permute-start | bytes 491528 | tf_op jit(solution)/shard_map/ppermute | solution.py:516
  18.1 6.0 %collective-permute-start.1 = (bf16[160,512]{1,0:T(8,128)(2,1)S(1)}, bf16[160,512]{1,0:T(8,128)(2,1)S(1)}, u32[]{:S(2)}, u32[]{:S(2)}) collective-permute-start(bf16[160,512]{1,0:T(8,128)(2,1)S(1)} %collective-permute-done.refs_7_), channel_id=1, source_target_pairs={{0,4},{4,8},{8,12},{12,14},{14,10},{10,6},{6,2},{2,0},{1,5},{5,9},... | collective-permute-start | bytes 491528 | tf_op jit(solution)/shard_map/ppermute | solution.py:516
  20.0 5.4 %collective-permute-start.19 = (bf16[160,512]{1,0:T(8,128)(2,1)S(1)}, bf16[160,512]{1,0:T(8,128)(2,1)S(1)}, u32[]{:S(2)}, u32[]{:S(2)}) collective-permute-start(bf16[160,512]{1,0:T(8,128)(2,1)S(1)} %collective-permute-done.18.refs_10_), channel_id=1, source_target_pairs={{4,0},{8,4},{12,8},{14,12},{10,14},{6,10},{2,6},{0,2},{5,1},{9,5},... | collective-permute-start | bytes 491528 | tf_op jit(solution)/shard_map/ppermute | solution.py:516
  20.2 7.1 %collective-permute-start.22 = (bf16[160,512]{1,0:T(8,128)(2,1)S(1)}, bf16[160,512]{1,0:T(8,128)(2,1)S(1)}, u32[]{:S(2)}, u32[]{:S(2)}) collective-permute-start(bf16[160,512]{1,0:T(8,128)(2,1)S(1)} %collective-permute-done.refs_7_), channel_id=1, source_target_pairs={{0,16},{16,0},{1,17},{17,1},{2,18},{18,2},{3,19},{19,3},{4,20},{20... | collective-permute-start | bytes 491528 | tf_op jit(solution)/shard_map/ppermute | solution.py:519
  21.9 8.8 %collective-permute-start.23 = (bf16[160,512]{1,0:T(8,128)(2,1)S(1)}, bf16[160,512]{1,0:T(8,128)(2,1)S(1)}, u32[]{:S(2)}, u32[]{:S(2)}) collective-permute-start(bf16[160,512]{1,0:T(8,128)(2,1)S(1)} %collective-permute-done.18.refs_10_), channel_id=1, source_target_pairs={{0,16},{16,0},{1,17},{17,1},{2,18},{18,2},{3,19},{19,3},{4,20},{20... | collective-permute-start | bytes 491528 | tf_op jit(solution)/shard_map/ppermute | solution.py:519
  24.1 26.4 %collective-permute-start.13 = (bf16[64,4096]{1,0:T(8,128)(2,1)S(1)}, bf16[64,4096]{1,0:T(8,128)(2,1)S(1)}, u32[]{:S(2)}, u32[]{:S(2)}) collective-permute-start(bf16[64,4096]{1,0:T(8,128)(2,1)S(1)} %get-tuple-element.47), channel_id=1, source_target_pairs={{0,1},{1,0},{2,3},{3,2},{4,5},{5,4},{6,7},{7,6},{8,9},{9,8},{10,11... | collective-permute-start | bytes 1572872 | tf_op jit(solution)/shard_map/ppermute | solution.py:475
  25.4 8.9 %collective-permute-start.24 = (bf16[160,512]{1,0:T(8,128)(2,1)S(1)}, bf16[160,512]{1,0:T(8,128)(2,1)S(1)}, u32[]{:S(2)}, u32[]{:S(2)}) collective-permute-start(bf16[160,512]{1,0:T(8,128)(2,1)S(1)} %collective-permute-done.1.refs_13_), channel_id=1, source_target_pairs={{0,16},{16,0},{1,17},{17,1},{2,18},{18,2},{3,19},{19,3},{4,20},{20... | collective-permute-start | bytes 491528 | tf_op jit(solution)/shard_map/ppermute | solution.py:519
  27.2 10.6 %collective-permute-start.6 = (bf16[256,512]{1,0:T(8,128)(2,1)S(1)}, bf16[256,512]{1,0:T(8,128)(2,1)S(1)}, u32[]{:S(2)}, u32[]{:S(2)}) collective-permute-start(bf16[256,512]{1,0:T(8,128)(2,1)S(1)} %collective-permute-done.5.refs_12_), channel_id=1, source_target_pairs={{4,0},{8,4},{12,8},{14,12},{10,14},{6,10},{2,6},{0,2},{5,1},{9,5},... | collective-permute-start | bytes 786440 | tf_op jit(solution)/shard_map/ppermute | solution.py:516
  30.7 5.4 %collective-permute-start.25 = (bf16[160,512]{1,0:T(8,128)(2,1)S(1)}, bf16[160,512]{1,0:T(8,128)(2,1)S(1)}, u32[]{:S(2)}, u32[]{:S(2)}) collective-permute-start(bf16[160,512]{1,0:T(8,128)(2,1)S(1)} %collective-permute-done.19.refs_16_), channel_id=1, source_target_pairs={{0,16},{16,0},{1,17},{17,1},{2,18},{18,2},{3,19},{19,3},{4,20},{20... | collective-permute-start | bytes 491528 | tf_op jit(solution)/shard_map/ppermute | solution.py:519
  34.3 10.5 %collective-permute-start.16 = (bf16[256,512]{1,0:T(8,128)(2,1)S(1)}, bf16[256,512]{1,0:T(8,128)(2,1)S(1)}, u32[]{:S(2)}, u32[]{:S(2)}) collective-permute-start(bf16[256,512]{1,0:T(8,128)(2,1)S(1)} %collective-permute-done.15.refs_9_), channel_id=1, source_target_pairs={{0,4},{4,8},{8,12},{12,14},{14,10},{10,6},{6,2},{2,0},{1,5},{5,9},... | collective-permute-start | bytes 786440 | tf_op jit(solution)/shard_map/ppermute | solution.py:516
  36.1 7.4 %collective-permute-start.2 = (bf16[160,512]{1,0:T(8,128)(2,1)S(1)}, bf16[160,512]{1,0:T(8,128)(2,1)S(1)}, u32[]{:S(2)}, u32[]{:S(2)}) collective-permute-start(bf16[160,512]{1,0:T(8,128)(2,1)S(1)} %collective-permute-done.1.refs_13_), channel_id=1, source_target_pairs={{0,4},{4,8},{8,12},{12,14},{14,10},{10,6},{6,2},{2,0},{1,5},{5,9},... | collective-permute-start | bytes 491528 | tf_op jit(solution)/shard_map/ppermute | solution.py:516
  37.9 13.1 %collective-permute-start.7 = (bf16[256,512]{1,0:T(8,128)(2,1)S(1)}, bf16[256,512]{1,0:T(8,128)(2,1)S(1)}, u32[]{:S(2)}, u32[]{:S(2)}) collective-permute-start(bf16[256,512]{1,0:T(8,128)(2,1)S(1)} %collective-permute-done.6.refs_18_), channel_id=1, source_target_pairs={{4,0},{8,4},{12,8},{14,12},{10,14},{6,10},{2,6},{0,2},{5,1},{9,5},... | collective-permute-start | bytes 786440 | tf_op jit(solution)/shard_map/ppermute | solution.py:516
  43.6 5.3 %collective-permute-start.20 = (bf16[160,512]{1,0:T(8,128)(2,1)S(1)}, bf16[160,512]{1,0:T(8,128)(2,1)S(1)}, u32[]{:S(2)}, u32[]{:S(2)}) collective-permute-start(bf16[160,512]{1,0:T(8,128)(2,1)S(1)} %collective-permute-done.19.refs_16_), channel_id=1, source_target_pairs={{4,0},{8,4},{12,8},{14,12},{10,14},{6,10},{2,6},{0,2},{5,1},{9,5},... | collective-permute-start | bytes 491528 | tf_op jit(solution)/shard_map/ppermute | solution.py:516
  44.7 11.2 %collective-permute-start.17 = (bf16[256,512]{1,0:T(8,128)(2,1)S(1)}, bf16[256,512]{1,0:T(8,128)(2,1)S(1)}, u32[]{:S(2)}, u32[]{:S(2)}) collective-permute-start(bf16[256,512]{1,0:T(8,128)(2,1)S(1)} %collective-permute-done.16.refs_15_), channel_id=1, source_target_pairs={{0,4},{4,8},{8,12},{12,14},{14,10},{10,6},{6,2},{2,0},{1,5},{5,9},... | collective-permute-start | bytes 786440 | tf_op jit(solution)/shard_map/ppermute | solution.py:516
  48.9 6.5 %collective-permute-start.14 = (bf16[160,512]{1,0:T(8,128)(2,1)S(1)}, bf16[160,512]{1,0:T(8,128)(2,1)S(1)}, u32[]{:S(2)}, u32[]{:S(2)}) collective-permute-start(bf16[160,512]{1,0:T(8,128)(2,1)S(1)} %collective-permute-done.2.refs_4_), channel_id=1, source_target_pairs={{0,16},{16,0},{1,17},{17,1},{2,18},{18,2},{3,19},{19,3},{4,20},{20... | collective-permute-start | bytes 491528 | tf_op jit(solution)/shard_map/ppermute | solution.py:519
  50.6 5.4 %collective-permute-start.21 = (bf16[160,512]{1,0:T(8,128)(2,1)S(1)}, bf16[160,512]{1,0:T(8,128)(2,1)S(1)}, u32[]{:S(2)}, u32[]{:S(2)}) collective-permute-start(bf16[160,512]{1,0:T(8,128)(2,1)S(1)} %collective-permute-done.20.refs_7_), channel_id=1, source_target_pairs={{0,16},{16,0},{1,17},{17,1},{2,18},{18,2},{3,19},{19,3},{4,20},{20... | collective-permute-start | bytes 491528 | tf_op jit(solution)/shard_map/ppermute | solution.py:519
  50.9 17.2 %collective-permute-start.8 = (bf16[256,512]{1,0:T(8,128)(2,1)S(1)}, bf16[256,512]{1,0:T(8,128)(2,1)S(1)}, u32[]{:S(2)}, u32[]{:S(2)}) collective-permute-start(bf16[256,512]{1,0:T(8,128)(2,1)S(1)} %collective-permute-done.7.refs_9_), channel_id=1, source_target_pairs={{4,0},{8,4},{12,8},{14,12},{10,14},{6,10},{2,6},{0,2},{5,1},{9,5},... | collective-permute-start | bytes 786440 | tf_op jit(solution)/shard_map/ppermute | solution.py:516
  57.7 15.9 %collective-permute-start.26 = (f32[352,512]{1,0:T(8,128)S(1)}, f32[352,512]{1,0:T(8,128)S(1)}, u32[]{:S(2)}, u32[]{:S(2)}) collective-permute-start(f32[352,512]{1,0:T(8,128)S(1)} %get-tuple-element.52), channel_id=1, source_target_pairs={{0,1},{1,0},{2,3},{3,2},{4,5},{5,4},{6,7},{7,6},{8,9},{9,8},{10,11... | collective-permute-start | bytes 2162696 | tf_op jit(solution)/shard_map/ppermute | solution.py:475
  60.0 6.4 %collective-permute-start.3 = (bf16[160,512]{1,0:T(8,128)(2,1)S(1)}, bf16[160,512]{1,0:T(8,128)(2,1)S(1)}, u32[]{:S(2)}, u32[]{:S(2)}) collective-permute-start(bf16[160,512]{1,0:T(8,128)(2,1)S(1)} %collective-permute-done.2.refs_4_), channel_id=1, source_target_pairs={{0,4},{4,8},{8,12},{12,14},{14,10},{10,6},{6,2},{2,0},{1,5},{5,9},... | collective-permute-start | bytes 491528 | tf_op jit(solution)/shard_map/ppermute | solution.py:516
  66.4 5.4 %collective-permute-start.4 = (bf16[160,512]{1,0:T(8,128)(2,1)S(1)}, bf16[160,512]{1,0:T(8,128)(2,1)S(1)}, u32[]{:S(2)}, u32[]{:S(2)}) collective-permute-start(bf16[160,512]{1,0:T(8,128)(2,1)S(1)} %collective-permute-done.3.refs_2_), channel_id=1, source_target_pairs={{0,16},{16,0},{1,17},{17,1},{2,18},{18,2},{3,19},{19,3},{4,20},{20... | collective-permute-start | bytes 491528 | tf_op jit(solution)/shard_map/ppermute | solution.py:519
  68.1 5.5 %collective-permute-start.11 = (bf16[256,512]{1,0:T(8,128)(2,1)S(1)}, bf16[256,512]{1,0:T(8,128)(2,1)S(1)}, u32[]{:S(2)}, u32[]{:S(2)}) collective-permute-start(bf16[256,512]{1,0:T(8,128)(2,1)S(1)} %collective-permute-done.8.refs_4_), channel_id=1, source_target_pairs={{0,1},{1,0},{2,3},{3,2},{4,5},{5,4},{6,7},{7,6},{8,9},{9,8},{10,11... | collective-permute-start | bytes 786440 | tf_op jit(solution)/shard_map/ppermute | solution.py:475
  70.5 3.1 %collective-permute-start.9 = (bf16[160,512]{1,0:T(8,128)(2,1)S(1)}, bf16[160,512]{1,0:T(8,128)(2,1)S(1)}, u32[]{:S(2)}, u32[]{:S(2)}) collective-permute-start(bf16[160,512]{1,0:T(8,128)(2,1)S(1)} %collective-permute-done.3.refs_2_), channel_id=1, source_target_pairs={{0,1},{1,0},{2,3},{3,2},{4,5},{5,4},{6,7},{7,6},{8,9},{9,8},{10,11... | collective-permute-start | bytes 491528 | tf_op jit(solution)/shard_map/ppermute | solution.py:475
  71.8 1.8 %collective-permute-start.10 = (bf16[160,512]{1,0:T(8,128)(2,1)S(1)}, bf16[160,512]{1,0:T(8,128)(2,1)S(1)}, u32[]{:S(2)}, u32[]{:S(2)}) collective-permute-start(bf16[160,512]{1,0:T(8,128)(2,1)S(1)} %collective-permute-done.4.refs_3_), channel_id=1, source_target_pairs={{0,1},{1,0},{2,3},{3,2},{4,5},{5,4},{6,7},{7,6},{8,9},{9,8},{10,11... | collective-permute-start | bytes 491528 | tf_op jit(solution)/shard_map/ppermute | solution.py:475
  76.0 1.8 %collective-permute-start.28 = (f32[64,512]{1,0:T(8,128)S(1)}, f32[64,512]{1,0:T(8,128)S(1)}, u32[]{:S(2)}, u32[]{:S(2)}) collective-permute-start(f32[64,512]{1,0:T(8,128)S(1)} %get-tuple-element.67.refs_4_), channel_id=1, source_target_pairs={{0,1},{1,0},{2,3},{3,2},{4,5},{5,4},{6,7},{7,6},{8,9},{9,8},{10,11... | collective-permute-start | bytes 393224 | tf_op jit(solution)/shard_map/ppermute | solution.py:475
  76.6 1.2 %collective-permute-start.27 = (bf16[64,256]{1,0:T(8,128)(2,1)S(1)}, bf16[64,256]{1,0:T(8,128)(2,1)S(1)}, u32[]{:S(2)}, u32[]{:S(2)}) collective-permute-start(bf16[64,256]{1,0:T(8,128)(2,1)S(1)} %get-tuple-element.66.refs_2_), channel_id=1, source_target_pairs={{0,1},{1,0},{2,3},{3,2},{4,5},{5,4},{6,7},{7,6},{8,9},{9,8},{10,11... | collective-permute-start | bytes 98312 | tf_op jit(solution)/shard_map/ppermute | solution.py:475
  78.9 11.3 %collective-permute-start.32 = (bf16[72,512]{1,0:T(8,128)(2,1)S(1)}, bf16[72,512]{1,0:T(8,128)(2,1)S(1)}, u32[]{:S(2)}, u32[]{:S(2)}) collective-permute-start(bf16[72,512]{1,0:T(8,128)(2,1)S(1)} %get-tuple-element.73), channel_id=1, source_target_pairs={{0,8},{2,10},{4,12},{6,14},{8,0},{10,2},{12,4},{14,6},{1,9},{3,11}... | collective-permute-start | bytes 221192 | tf_op jit(solution)/shard_map/ppermute | solution.py:478
  82.1 11.5 %collective-permute-start.33 = (bf16[72,512]{1,0:T(8,128)(2,1)S(1)}, bf16[72,512]{1,0:T(8,128)(2,1)S(1)}, u32[]{:S(2)}, u32[]{:S(2)}) collective-permute-start(bf16[72,512]{1,0:T(8,128)(2,1)S(1)} %get-tuple-element.74), channel_id=1, source_target_pairs={{0,10},{2,8},{4,14},{6,12},{8,2},{10,0},{12,6},{14,4},{1,11},{3,9}... | collective-permute-start | bytes 221192 | tf_op jit(solution)/shard_map/ppermute | solution.py:478
  83.6 11.2 %collective-permute-start.34 = (bf16[72,512]{1,0:T(8,128)(2,1)S(1)}, bf16[72,512]{1,0:T(8,128)(2,1)S(1)}, u32[]{:S(2)}, u32[]{:S(2)}) collective-permute-start(bf16[72,512]{1,0:T(8,128)(2,1)S(1)} %get-tuple-element.75), channel_id=1, source_target_pairs={{0,12},{2,14},{4,8},{6,10},{8,4},{10,6},{12,0},{14,2},{1,13},{3,15... | collective-permute-start | bytes 221192 | tf_op jit(solution)/shard_map/ppermute | solution.py:478
  87.5 7.3 %collective-permute-start.35 = (bf16[72,512]{1,0:T(8,128)(2,1)S(1)}, bf16[72,512]{1,0:T(8,128)(2,1)S(1)}, u32[]{:S(2)}, u32[]{:S(2)}) collective-permute-start(bf16[72,512]{1,0:T(8,128)(2,1)S(1)} %get-tuple-element.76), channel_id=1, source_target_pairs={{0,14},{2,12},{4,10},{6,8},{8,6},{10,4},{12,2},{14,0},{1,15},{3,13... | collective-permute-start | bytes 221192 | tf_op jit(solution)/shard_map/ppermute | solution.py:478
  88.6 27.5 %copy-start.8 = (bf16[1,64,4096]{2,1,0:T(8,128)(2,1)S(1)}, bf16[1,64,4096]{2,1,0:T(8,128)(2,1)}, u32[]{:S(2)}) copy-start(bf16[1,64,4096]{2,1,0:T(8,128)(2,1)} %param.21) | copy-start | bytes 1572868
  88.6 6.7 %collective-permute-start.29 = (bf16[72,512]{1,0:T(8,128)(2,1)S(1)}, bf16[72,512]{1,0:T(8,128)(2,1)S(1)}, u32[]{:S(2)}, u32[]{:S(2)}) collective-permute-start(bf16[72,512]{1,0:T(8,128)(2,1)S(1)} %get-tuple-element.70), channel_id=1, source_target_pairs={{0,2},{2,0},{4,6},{6,4},{8,10},{10,8},{12,14},{14,12},{1,3},{3,1},... | collective-permute-start | bytes 221192 | tf_op jit(solution)/shard_map/ppermute | solution.py:478
  90.1 5.2 %collective-permute-start.30 = (bf16[72,512]{1,0:T(8,128)(2,1)S(1)}, bf16[72,512]{1,0:T(8,128)(2,1)S(1)}, u32[]{:S(2)}, u32[]{:S(2)}) collective-permute-start(bf16[72,512]{1,0:T(8,128)(2,1)S(1)} %get-tuple-element.71), channel_id=1, source_target_pairs={{0,4},{2,6},{4,0},{6,2},{8,12},{10,14},{12,8},{14,10},{1,5},{3,7},... | collective-permute-start | bytes 221192 | tf_op jit(solution)/shard_map/ppermute | solution.py:478
  93.6 5.3 %collective-permute-start.31 = (bf16[72,512]{1,0:T(8,128)(2,1)S(1)}, bf16[72,512]{1,0:T(8,128)(2,1)S(1)}, u32[]{:S(2)}, u32[]{:S(2)}) collective-permute-start(bf16[72,512]{1,0:T(8,128)(2,1)S(1)} %get-tuple-element.72), channel_id=1, source_target_pairs={{0,6},{2,4},{4,2},{6,0},{8,14},{10,12},{12,10},{14,8},{1,7},{3,5},... | collective-permute-start | bytes 221192 | tf_op jit(solution)/shard_map/ppermute | solution.py:478
  99.5 6.7 %collective-permute-start.37 = (bf16[80,512]{1,0:T(8,128)(2,1)S(1)}, bf16[80,512]{1,0:T(8,128)(2,1)S(1)}, u32[]{:S(2)}, u32[]{:S(2)}) collective-permute-start(bf16[80,512]{1,0:T(8,128)(2,1)S(1)} %get-tuple-element.77.refs_2_), channel_id=1, source_target_pairs={{0,4},{2,6},{4,0},{6,2},{8,12},{10,14},{12,8},{14,10},{1,5},{3,7},... | collective-permute-start | bytes 245768 | tf_op jit(solution)/shard_map/ppermute | solution.py:478
  100.3 8.6 %collective-permute-start.39 = (bf16[80,512]{1,0:T(8,128)(2,1)S(1)}, bf16[80,512]{1,0:T(8,128)(2,1)S(1)}, u32[]{:S(2)}, u32[]{:S(2)}) collective-permute-start(bf16[80,512]{1,0:T(8,128)(2,1)S(1)} %get-tuple-element.77.refs_2_), channel_id=1, source_target_pairs={{0,8},{2,10},{4,12},{6,14},{8,0},{10,2},{12,4},{14,6},{1,9},{3,11}... | collective-permute-start | bytes 245768 | tf_op jit(solution)/shard_map/ppermute | solution.py:478
  104.2 6.3 %collective-permute-start.41 = (bf16[80,512]{1,0:T(8,128)(2,1)S(1)}, bf16[80,512]{1,0:T(8,128)(2,1)S(1)}, u32[]{:S(2)}, u32[]{:S(2)}) collective-permute-start(bf16[80,512]{1,0:T(8,128)(2,1)S(1)} %get-tuple-element.77.refs_2_), channel_id=1, source_target_pairs={{0,12},{2,14},{4,8},{6,10},{8,4},{10,6},{12,0},{14,2},{1,13},{3,15... | collective-permute-start | bytes 245768 | tf_op jit(solution)/shard_map/ppermute | solution.py:478
  104.2 6.7 %collective-permute-start.36 = (bf16[80,512]{1,0:T(8,128)(2,1)S(1)}, bf16[80,512]{1,0:T(8,128)(2,1)S(1)}, u32[]{:S(2)}, u32[]{:S(2)}) collective-permute-start(bf16[80,512]{1,0:T(8,128)(2,1)S(1)} %get-tuple-element.77.refs_2_), channel_id=1, source_target_pairs={{0,2},{2,0},{4,6},{6,4},{8,10},{10,8},{12,14},{14,12},{1,3},{3,1},... | collective-permute-start | bytes 245768 | tf_op jit(solution)/shard_map/ppermute | solution.py:478
  106.1 4.8 %collective-permute-start.38 = (bf16[80,512]{1,0:T(8,128)(2,1)S(1)}, bf16[80,512]{1,0:T(8,128)(2,1)S(1)}, u32[]{:S(2)}, u32[]{:S(2)}) collective-permute-start(bf16[80,512]{1,0:T(8,128)(2,1)S(1)} %collective-permute-done.37.refs_4_), channel_id=1, source_target_pairs={{0,2},{2,0},{4,6},{6,4},{8,10},{10,8},{12,14},{14,12},{1,3},{3,1},... | collective-permute-start | bytes 245768 | tf_op jit(solution)/shard_map/ppermute | solution.py:478
  108.8 4.4 %collective-permute-start.40 = (bf16[80,512]{1,0:T(8,128)(2,1)S(1)}, bf16[80,512]{1,0:T(8,128)(2,1)S(1)}, u32[]{:S(2)}, u32[]{:S(2)}) collective-permute-start(bf16[80,512]{1,0:T(8,128)(2,1)S(1)} %collective-permute-done.39.refs_6_), channel_id=1, source_target_pairs={{0,2},{2,0},{4,6},{6,4},{8,10},{10,8},{12,14},{14,12},{1,3},{3,1},... | collective-permute-start | bytes 245768 | tf_op jit(solution)/shard_map/ppermute | solution.py:478
  110.6 4.4 %collective-permute-start.42 = (bf16[80,512]{1,0:T(8,128)(2,1)S(1)}, bf16[80,512]{1,0:T(8,128)(2,1)S(1)}, u32[]{:S(2)}, u32[]{:S(2)}) collective-permute-start(bf16[80,512]{1,0:T(8,128)(2,1)S(1)} %collective-permute-done.41.refs_8_), channel_id=1, source_target_pairs={{0,2},{2,0},{4,6},{6,4},{8,10},{10,8},{12,14},{14,12},{1,3},{3,1},... | collective-permute-start | bytes 245768 | tf_op jit(solution)/shard_map/ppermute | solution.py:478
  110.9 6.9 %collective-permute-start.44 = (f32[64,512]{1,0:T(8,128)S(1)}, f32[64,512]{1,0:T(8,128)S(1)}, u32[]{:S(2)}, u32[]{:S(2)}) collective-permute-start(f32[64,512]{1,0:T(8,128)S(1)} %get-tuple-element.81.refs_5_), channel_id=1, source_target_pairs={{0,1},{1,0},{2,3},{3,2},{4,5},{5,4},{6,7},{7,6},{8,9},{9,8},{10,11... | collective-permute-start | bytes 393224 | tf_op jit(solution)/shard_map/ppermute | solution.py:475
  115.9 1.9 %collective-permute-start.43 = (f32[64,64]{1,0:T(8,128)S(1)}, f32[64,64]{1,0:T(8,128)S(1)}, u32[]{:S(2)}, u32[]{:S(2)}) collective-permute-start(f32[64,64]{1,0:T(8,128)S(1)} %get-tuple-element.79), channel_id=1, source_target_pairs={{0,1},{1,0},{2,3},{3,2},{4,5},{5,4},{6,7},{7,6},{8,9},{9,8},{10,11... | collective-permute-start | bytes 49160 | tf_op jit(solution)/shard_map/ppermute | solution.py:475
  (8 other events, 77.9 us)

commit v2 on v1

--- a/solution.py
+++ b/solution.py
@@ -99,7 +99,7 @@
         logits = jnp.where(allowed, logits, -1e30)
         peak = jnp.max(logits, axis=0, keepdims=True)
         weights = jnp.exp(logits - peak)
-        every.append((weights / jnp.sum(weights, axis=0, keepdims=True)).astype(BF16))
+        every.append((weights * (1.0 / jnp.sum(weights, axis=0, keepdims=True))).astype(BF16))
     gram = sum(dot_nt(probs, probs) for probs in every)
     high = gram.astype(BF16)
     high_out[...] = high
@@ -203,7 +203,6 @@
         scratch_shapes=[pltpu.VMEM((RANK, half), F32), pltpu.SemaphoreType.DMA((4,))],
         cost_estimate=cost(1e6, 2**20),
         compiler_params=pltpu.CompilerParams(vmem_limit_bytes=VMEM_GRANT),
-        name="prepare",
     )(far_off(weight), far_off(down_t))
 
 
@@ -240,7 +239,6 @@
         scratch_shapes=[pltpu.SemaphoreType.DMA((len(arrays) * n,))],
         cost_estimate=cost(1e6, 2**21),
         compiler_params=pltpu.CompilerParams(vmem_limit_bytes=VMEM_GRANT),
-        name="fetch",
     )(s, *[far_off(a) for a in arrays])
 
 
@@ -398,39 +396,76 @@
     )
 
 
-def score_low_kernel(n, half, s, refs, outs, scratch):
-    xs, xso, *messages = refs
-    mine, other, up = outs
-    low_mine = low_other = None
-    for k in range(n):
-        here = lanes_at((s[0] ^ k) * 2 * half + s[1] * half, half)
-        message = messages[k]
-        part = dot_nt(xs[:, here], message[:RANK, :])
-        low_mine = part if low_mine is None else low_mine + part
-        part = dot_nt(xso[:, lanes_at((s[0] ^ k) * half, half)], message[:RANK, :])
-        low_other = part if low_other is None else low_other + part
+def column_kernel(n, half, s, refs, outs, scratch):
+    xs, xso = refs
+    (out,) = outs
+    u = xs.shape[0]
+    for i in range(n // 2):
+        owner = 2 * i + 1 - lax.rem(s[0], 2)
+        there = slice(i * half, (i + 1) * half)
+        out[:u, there] = xs[:, lanes_at(owner * 2 * half + s[1] * half, half)]
+        out[u:, there] = xso[:, lanes_at(owner * half, half)]
+
+
+def column_rows(s, n, half, raw):
+    u = raw[0].shape[0]
+    return call(functools.partial(column_kernel, n, half), [((2 * u, n // 2 * half), BF16)], s, raw)[0]
+
+
+def up_kernel(s, refs, outs, scratch):
+    for i, message in enumerate(refs):
+        place = lax.div(s[0] ^ (2 * i), 2)
         high = message[RANK : RANK + UP_ROWS, :].astype(F32)
-        up[up_place(s[0] ^ k, half)] = high + message[RANK + UP_ROWS :, :].astype(F32)
-    mine[...] = low_mine
-    other[...] = low_other
+        there = pl.ds(pl.multiple_of(place * UP_ROWS, UP_ROWS), UP_ROWS)
+        outs[0][there, :] = high + message[RANK + UP_ROWS :, :].astype(F32)
+
+
+def column_up(s, half, messages):
+    return call(up_kernel, [((len(messages) * UP_ROWS, half), F32)], s, messages)[0]
+
+
+def score_low_kernel(half, s, refs, outs, scratch):
+    xs, xso, xz, *messages = refs
+    mine, other, near_by, cross = outs
+    u = xs.shape[0]
+    sums = [0.0, 0.0, 0.0]
+    for i, message in enumerate(messages):
+        owner = s[0] ^ (2 * i)
+        place = lax.div(owner, 2)
+        down = message[:RANK, :]
+        rows = (
+            xs[:, lanes_at(owner * 2 * half + s[1] * half, half)],
+            xso[:, lanes_at(owner * half, half)],
+            xz[:, lanes_at(place * half, half)],
+        )
+        sums = [a + dot_nt(b, down) for a, b in zip(sums, rows)]
+    mine[...] = sums[0]
+    other[...] = sums[1]
+    near_by[...] = sums[2][:u, :]
+    cross[...] = sums[2][u:, :]
 
 
 def score_low(s, half, messages, raw):
-    n, u = len(messages), raw[0].shape[0]
-    return call(
-        functools.partial(score_low_kernel, n, half),
-        [((u, RANK), F32), ((u, RANK), F32), ((RANK, VALUE_WIDTH), F32)],
+    u = raw[0].shape[0]
+    return call(
+        functools.partial(score_low_kernel, half),
+        [((u, RANK), F32)] * 4,
         s, [*raw, *messages], flops=2e8,
     )
 
 
 def score_kernel(s, refs, outs, scratch):
-    base, mine, got, up, probs, fresh, fresh_got = refs
+    base, probs, fresh, fresh_got, up, up_got, *lows = refs
     out, new_down, new_up = outs
     half = new_down.shape[1] // 2
-    low = (mine[...] + got[...]).astype(BF16)
+    parity = lax.rem(s[0], 2)
+    for i in range(up.shape[0] // UP_ROWS):
+        rows = slice(i * UP_ROWS, (i + 1) * UP_ROWS)
+        new_up[up_place(2 * i + parity, half)] = up[rows, :]
+        new_up[up_place(2 * i + 1 - parity, half)] = up_got[rows, :]
+    low = sum(a[...] for a in lows).astype(BF16)
     u = low.shape[0]
-    values = base[...] + adapter_scale_factor * dot_nn(low, up[...].astype(BF16))
+    values = base[...] + adapter_scale_factor * dot_nn(low, new_up[...].astype(BF16))
     values = values.astype(BF16)
     for g in range(KV_HEADS):
         attended = dot_nn(probs[g], values[:, g * HEAD_DIM : (g + 1) * HEAD_DIM]).astype(BF16)
@@ -439,15 +474,14 @@
             out[:, h * HEAD_DIM : (h + 1) * HEAD_DIM] = attended[j * u : (j + 1) * u, :]
     new_down[:, lanes_at(s[1] * half, half)] = fresh[...]
     new_down[:, lanes_at((1 - s[1]) * half, half)] = fresh_got[...]
-    new_up[...] = up[...]
-
-
-def score(s, base, mine, got, up, probs, fresh, fresh_got):
+
+
+def score(s, base, probs, fresh, fresh_got, up, up_got, lows):
     u, half = base.shape[0], fresh.shape[1]
     return call(
         score_kernel,
-        [((u, Q_HEADS * HEAD_DIM), BF16), ((RANK, 2 * half), F32), (up.shape, F32)],
-        s, [base, mine, got, up, probs, fresh, fresh_got], flops=2e8, final=(0, 1, 2),
+        [((u, Q_HEADS * HEAD_DIM), BF16), ((RANK, 2 * half), F32), ((RANK, VALUE_WIDTH), F32)],
+        s, [base, probs, fresh, fresh_got, up, up_got, *lows], flops=2e8, final=(0, 1, 2),
     )
 
 
@@ -573,30 +607,22 @@
         for k in far + near_by:
             got[k - 1] = exchange(out[k - 1], k)
         fresh, message = update(s, keep, keep_up, down_t, adapter_up, got)
-        messages = [message] + [None] * (n_fsdp - 1)
+        xz = exchange(column_rows(s, n_fsdp, half, raw[2:]), 1)
+        messages = [message] + [None] * (n_fsdp // 2 - 1)
         for k in range(n_fsdp - 2, 0, -2):
-            messages[k] = exchange(message, k)
-        for k in range(0, n_fsdp, 2):
-            messages[k + 1] = exchange(messages[k], 1)
+            messages[k // 2] = exchange(message, k)
         fresh_got = swap(fresh)
-        mine, other, new_up = score_low(s, half, messages, raw[2:])
-        other_got = swap(other)
-        scored, new_down, new_up = score(s, base, mine, other_got, new_up, probs, fresh, fresh_got)
+        up = column_up(s, half, messages)
+        up_got = exchange(up, 1)
+        low, other, near_by, cross = score_low(s, half, messages, [*raw[2:], xz])
+        pairs = [
+            (i * n_view + v, (i ^ 1) * n_view + (v ^ 1)) for i in range(n_fsdp) for v in range(n_view)
+        ]
+        lows = [low, exchange(near_by, 1), lax.ppermute(cross, ("fsdp", "view"), pairs), swap(other)]
+        scored, new_down, new_up = score(s, base, probs, fresh, fresh_got, up, up_got, lows)
         return (new_down.T, new_up, scored.reshape(score_query.shape))
 
-    in_specs = (
-        P(("task", "view"), "fsdp", None),
-        P(("task", "view"), "fsdp", None),
-        P(("task", "view"), "fsdp", None),
-        P(("task", "view"), "fsdp", None),
-        P(("task", "view"), "fsdp", None),
-        P("fsdp", None),
-        P(("task", "fsdp"), None),
-        P("task", None),
-        P(("task", "view"), "fsdp", None),
-        P(("task", "view"), "fsdp", None),
-        P(("task", "view"), "fsdp", None),
-        P(("task", "view"), "fsdp", None),
-    )
-    out_specs = (P(("task", "fsdp"), None), P("task", None), P(("task", "view"), "fsdp", None))
+    rows, rank_rows, tasks = P(("task", "view"), "fsdp", None), P(("task", "fsdp"), None), P("task", None)
+    in_specs = (*[rows] * 5, P("fsdp", None), rank_rows, tasks, *[rows] * 4)
+    out_specs = (rank_rows, tasks, rows)
     return jax.shard_map(body, mesh=mesh, in_specs=in_specs, out_specs=out_specs, check_vma=False)

time: 120 us -> 123 us (1.025)
  waiting for transfers between devices: 44.8 us -> 46.3 us
    ppermute x14 -> x13, waiting for transfers between devices: 15.5 us -> 17.2 us  [exchange(): return lax.ppermute(array, 'fsdp', [(i, i ^ k) for i in range(n_fsdp)])]
    ppermute x10, starting transfers between devices: 1.92 us -> 3.45 us  [swap(): return lax.ppermute(array, 'view', [(i, i ^ 1) for i in range(n_view)])]
    pallas_call x14 -> x16, Pallas kernels: 22.3 us -> 23.5 us  [call(): pl.pallas_call(whole, out_shape=[jax.ShapeDtypeStruct(*o) if i in final e...]
    ppermute x14 -> x13, starting transfers between devices: 18.9 us -> 17.9 us  [exchange(): return lax.ppermute(array, 'fsdp', [(i, i ^ k) for i in range(n_fsdp)])]
  transfers between devices with their start and end apart: 45 -> 45, of which waited for: 20 -> 21; matrix products, arithmetic and copies ran while one was open for 0% -> 0% of each run, Pallas kernels for 15% -> 19%
where the time goes in v2:
time: 123 us
  starting transfers between devices  47.8 us (39%)
  waiting for transfers between devices  46.3 us (38%)
  Pallas kernels  27.3 us (22%)
    pallas_call x16, Pallas kernels, call(): pl.pallas_call(whole, out_shape=[jax.ShapeDtypeStruct(*o) if i in final e...  23.5 us
    ppermute x14, waiting for transfers between devices, onward(): return lax.ppermute(array, 'fsdp', forward if ahead else backward)  22.7 us
    ppermute x13, starting transfers between devices, exchange(): return lax.ppermute(array, 'fsdp', [(i, i ^ k) for i in range(n_fsdp)])  17.9 us
    ppermute x14, starting transfers between devices, onward(): return lax.ppermute(array, 'fsdp', forward if ahead else backward)  17.5 us
    ppermute x13, waiting for transfers between devices, exchange(): return lax.ppermute(array, 'fsdp', [(i, i ^ k) for i in range(n_fsdp)])  17.2 us
    ppermute x7, starting transfers between devices, over_task(): return lax.ppermute(array, 'task', [(i, i ^ 1) for i in range(n_task)])  8.97 us
    ppermute x7, waiting for transfers between devices, over_task(): return lax.ppermute(array, 'task', [(i, i ^ 1) for i in range(n_task)])  5.4 us
    ppermute x10, starting transfers between devices, swap(): return lax.ppermute(array, 'view', [(i, i ^ 1) for i in range(n_view)])  3.45 us
  transfers between devices with their start and end apart: 45, of which 21 were waited for; matrix products, arithmetic and copies ran while one was open for 0% of the time, Pallas kernels for 19%

profile of v2, /device:TPU:0, one launch (start us, length us, event | category | flops | bytes accessed | tf_op | source)
XLA Modules:
  0.0 122.9 jit_solution(16127323664178648106)
XLA Ops:
  0.7 2.6 %shard_map.140 = (bf16[256,4096]{1,0:T(8,128)(2,1)S(1)}, bf16[64,4096]{1,0:T(8,128)(2,1)S(1)}) custom-call(s32[4]{0:T(128)S(1)} %pad_add_fusion.scalar_ref, bf16[256,8192]{1,0:T(8,128)(2,1)} %bitcast.16, bf16[64,8192]{1,0:T(8,128)(2,1)} %bitcast.22), custom_call_target="tpu_custom_call" | custom-call | flops 1000000 | bytes 2097152 | tf_op jit(solution)/shard_map/pallas_call | solution.py:234
  3.9 1.2 shard_map.139
  5.1 2.6 %collective-permute-start.15 = (bf16[256,512]{1,0:T(8,128)(2,1)S(1)}, bf16[256,512]{1,0:T(8,128)(2,1)S(1)}, u32[]{:S(2)}, u32[]{:S(2)}) collective-permute-start(bf16[256,512]{1,0:T(8,128)(2,1)S(1)} %get-tuple-element.46.refs_6_), channel_id=1, source_target_pairs={{0,4},{4,8},{8,12},{12,14},{14,10},{10,6},{6,2},{2,0},{1,5},{5,9},... | collective-permute-start | bytes 786440 | tf_op jit(solution)/shard_map/ppermute | solution.py:550
  7.8 2.0 %collective-permute-start = (bf16[160,512]{1,0:T(8,128)(2,1)S(1)}, bf16[160,512]{1,0:T(8,128)(2,1)S(1)}, u32[]{:S(2)}, u32[]{:S(2)}) collective-permute-start(bf16[160,512]{1,0:T(8,128)(2,1)S(1)} %get-tuple-element.45.refs_4_), channel_id=1, source_target_pairs={{0,4},{4,8},{8,12},{12,14},{14,10},{10,6},{6,2},{2,0},{1,5},{5,9},... | collective-permute-start | bytes 491528 | tf_op jit(solution)/shard_map/ppermute | solution.py:550
  9.8 8.3 %collective-permute-done.refs_7_ = bf16[160,512]{1,0:T(8,128)(2,1)S(1)} collective-permute-done((bf16[160,512]{1,0:T(8,128)(2,1)S(1)}, bf16[160,512]{1,0:T(8,128)(2,1)S(1)}, u32[]{:S(2)}, u32[]{:S(2)}) %collective-permute-start) | collective-permute-done | bytes 163872 | tf_op jit(solution)/shard_map/ppermute | solution.py:550
  18.1 1.8 %collective-permute-start.1 = (bf16[160,512]{1,0:T(8,128)(2,1)S(1)}, bf16[160,512]{1,0:T(8,128)(2,1)S(1)}, u32[]{:S(2)}, u32[]{:S(2)}) collective-permute-start(bf16[160,512]{1,0:T(8,128)(2,1)S(1)} %collective-permute-done.refs_7_), channel_id=1, source_target_pairs={{0,4},{4,8},{8,12},{12,14},{14,10},{10,6},{6,2},{2,0},{1,5},{5,9},... | collective-permute-start | bytes 491528 | tf_op jit(solution)/shard_map/ppermute | solution.py:550
  20.2 1.8 %collective-permute-start.22 = (bf16[160,512]{1,0:T(8,128)(2,1)S(1)}, bf16[160,512]{1,0:T(8,128)(2,1)S(1)}, u32[]{:S(2)}, u32[]{:S(2)}) collective-permute-start(bf16[160,512]{1,0:T(8,128)(2,1)S(1)} %collective-permute-done.refs_7_), channel_id=1, source_target_pairs={{0,16},{16,0},{1,17},{17,1},{2,18},{18,2},{3,19},{19,3},{4,20},{20... | collective-permute-start | bytes 491528 | tf_op jit(solution)/shard_map/ppermute | solution.py:553
  22.2 1.9 %collective-permute-done.1.refs_13_ = bf16[160,512]{1,0:T(8,128)(2,1)S(1)} collective-permute-done((bf16[160,512]{1,0:T(8,128)(2,1)S(1)}, bf16[160,512]{1,0:T(8,128)(2,1)S(1)}, u32[]{:S(2)}, u32[]{:S(2)}) %collective-permute-start.1) | collective-permute-done | bytes 163872 | tf_op jit(solution)/shard_map/ppermute | solution.py:550
  24.1 1.3 %collective-permute-done.19.refs_16_ = bf16[160,512]{1,0:T(8,128)(2,1)S(1)} collective-permute-done((bf16[160,512]{1,0:T(8,128)(2,1)S(1)}, bf16[160,512]{1,0:T(8,128)(2,1)S(1)}, u32[]{:S(2)}, u32[]{:S(2)}) %collective-permute-start.19) | collective-permute-done | bytes 163872 | tf_op jit(solution)/shard_map/ppermute | solution.py:550
  25.4 1.5 %collective-permute-start.24 = (bf16[160,512]{1,0:T(8,128)(2,1)S(1)}, bf16[160,512]{1,0:T(8,128)(2,1)S(1)}, u32[]{:S(2)}, u32[]{:S(2)}) collective-permute-start(bf16[160,512]{1,0:T(8,128)(2,1)S(1)} %collective-permute-done.1.refs_13_), channel_id=1, source_target_pairs={{0,16},{16,0},{1,17},{17,1},{2,18},{18,2},{3,19},{19,3},{4,20},{20... | collective-permute-start | bytes 491528 | tf_op jit(solution)/shard_map/ppermute | solution.py:553
  27.2 1.7 %collective-permute-start.6 = (bf16[256,512]{1,0:T(8,128)(2,1)S(1)}, bf16[256,512]{1,0:T(8,128)(2,1)S(1)}, u32[]{:S(2)}, u32[]{:S(2)}) collective-permute-start(bf16[256,512]{1,0:T(8,128)(2,1)S(1)} %collective-permute-done.5.refs_12_), channel_id=1, source_target_pairs={{4,0},{8,4},{12,8},{14,12},{10,14},{6,10},{2,6},{0,2},{5,1},{9,5},... | collective-permute-start | bytes 786440 | tf_op jit(solution)/shard_map/ppermute | solution.py:550
  28.9 1.8 %collective-permute-done.23.refs_11_ = bf16[160,512]{1,0:T(8,128)(2,1)S(1)} collective-permute-done((bf16[160,512]{1,0:T(8,128)(2,1)S(1)}, bf16[160,512]{1,0:T(8,128)(2,1)S(1)}, u32[]{:S(2)}, u32[]{:S(2)}) %collective-permute-start.23) | collective-permute-done | bytes 163872 | tf_op jit(solution)/shard_map/ppermute | solution.py:553
  30.7 1.7 %collective-permute-start.25 = (bf16[160,512]{1,0:T(8,128)(2,1)S(1)}, bf16[160,512]{1,0:T(8,128)(2,1)S(1)}, u32[]{:S(2)}, u32[]{:S(2)}) collective-permute-start(bf16[160,512]{1,0:T(8,128)(2,1)S(1)} %collective-permute-done.19.refs_16_), channel_id=1, source_target_pairs={{0,16},{16,0},{1,17},{17,1},{2,18},{18,2},{3,19},{19,3},{4,20},{20... | collective-permute-start | bytes 491528 | tf_op jit(solution)/shard_map/ppermute | solution.py:553
  32.5 1.8 %collective-permute-done.24.refs_14_ = bf16[160,512]{1,0:T(8,128)(2,1)S(1)} collective-permute-done((bf16[160,512]{1,0:T(8,128)(2,1)S(1)}, bf16[160,512]{1,0:T(8,128)(2,1)S(1)}, u32[]{:S(2)}, u32[]{:S(2)}) %collective-permute-start.24) | collective-permute-done | bytes 163872 | tf_op jit(solution)/shard_map/ppermute | solution.py:553
  34.3 1.7 %collective-permute-start.16 = (bf16[256,512]{1,0:T(8,128)(2,1)S(1)}, bf16[256,512]{1,0:T(8,128)(2,1)S(1)}, u32[]{:S(2)}, u32[]{:S(2)}) collective-permute-start(bf16[256,512]{1,0:T(8,128)(2,1)S(1)} %collective-permute-done.15.refs_9_), channel_id=1, source_target_pairs={{0,4},{4,8},{8,12},{12,14},{14,10},{10,6},{6,2},{2,0},{1,5},{5,9},... | collective-permute-start | bytes 786440 | tf_op jit(solution)/shard_map/ppermute | solution.py:550
  36.1 1.7 %collective-permute-start.2 = (bf16[160,512]{1,0:T(8,128)(2,1)S(1)}, bf16[160,512]{1,0:T(8,128)(2,1)S(1)}, u32[]{:S(2)}, u32[]{:S(2)}) collective-permute-start(bf16[160,512]{1,0:T(8,128)(2,1)S(1)} %collective-permute-done.1.refs_13_), channel_id=1, source_target_pairs={{0,4},{4,8},{8,12},{12,14},{14,10},{10,6},{6,2},{2,0},{1,5},{5,9},... | collective-permute-start | bytes 491528 | tf_op jit(solution)/shard_map/ppermute | solution.py:550
  38.2 5.4 %collective-permute-done.2.refs_4_ = bf16[160,512]{1,0:T(8,128)(2,1)S(1)} collective-permute-done((bf16[160,512]{1,0:T(8,128)(2,1)S(1)}, bf16[160,512]{1,0:T(8,128)(2,1)S(1)}, u32[]{:S(2)}, u32[]{:S(2)}) %collective-permute-start.2) | collective-permute-done | bytes 163872 | tf_op jit(solution)/shard_map/ppermute | solution.py:550
  43.6 1.2 collective-permute-start.20
  45.6 3.3 %collective-permute-done.20.refs_7_ = bf16[160,512]{1,0:T(8,128)(2,1)S(1)} collective-permute-done((bf16[160,512]{1,0:T(8,128)(2,1)S(1)}, bf16[160,512]{1,0:T(8,128)(2,1)S(1)}, u32[]{:S(2)}, u32[]{:S(2)}) %collective-permute-start.20) | collective-permute-done | bytes 163872 | tf_op jit(solution)/shard_map/ppermute | solution.py:550
  48.9 1.7 %collective-permute-start.14 = (bf16[160,512]{1,0:T(8,128)(2,1)S(1)}, bf16[160,512]{1,0:T(8,128)(2,1)S(1)}, u32[]{:S(2)}, u32[]{:S(2)}) collective-permute-start(bf16[160,512]{1,0:T(8,128)(2,1)S(1)} %collective-permute-done.2.refs_4_), channel_id=1, source_target_pairs={{0,16},{16,0},{1,17},{17,1},{2,18},{18,2},{3,19},{19,3},{4,20},{20... | collective-permute-start | bytes 491528 | tf_op jit(solution)/shard_map/ppermute | solution.py:553
  50.9 1.2 collective-permute-start.8
  52.1 3.3 %shard_map.141 = (f32[640,512]{1,0:T(8,128)S(1)}, f32[64,512]{1,0:T(8,128)S(1)}) custom-call(s32[4]{0:T(128)S(1)} %pad_add_fusion.scalar_ref, bf16[256,8192]{1,0:T(8,128)(2,1)S(1)} %bitcast.17, bf16[256,4096]{1,0:T(8,128)(2,1)S(1)} %collective-permute-done.12.refs_1_, bf16[64,8192]{1,0:T(8,128)(2,1)S(1)} %bitcast.23, ...), custom_call_target="tpu_custom_call" | custom-call | flops 1700000000 | bytes 1048576 | tf_op jit(solution)/shard_map/pallas_call | solution.py:66
  56.0 1.7 %shard_map.142 = (f32[352,512]{1,0:T(8,128)S(1)}, f32[352,512]{1,0:T(8,128)S(1)}) custom-call(s32[4]{0:T(128)S(1)} %pad_add_fusion.scalar_ref, bf16[256,8192]{1,0:T(8,128)(2,1)S(1)} %bitcast.18, bf16[256,4096]{1,0:T(8,128)(2,1)S(1)} %collective-permute-done.12.refs_1_, bf16[64,8192]{1,0:T(8,128)(2,1)S(1)} %bitcast.24, ...), custom_call_target="tpu_custom_call" | custom-call | flops 680000000 | bytes 1048576 | tf_op jit(solution)/shard_map/pallas_call | solution.py:66
  58.2 1.8 %shard_map.145 = (bf16[256,256]{1,0:T(8,128)(2,1)S(1)}, bf16[256,256]{1,0:T(8,128)(2,1)S(1)}, f32[256,128]{1,0:T(8,128)S(1)}) custom-call(s32[4]{0:T(128)S(1)} %pad_add_fusion.scalar_ref, s32[1,256]{1,0:T(1,128)S(1)} %bitcast.45, bf16[256,4096]{1,0:T(8,128)(2,1)S(1)} %bitcast.28, bf16[256,512]{1,0:T(8,128)(2,1)S(1)} %bitcast.40, bf16[256,4096]{1,0:T(8,128)(2,1)S(1)} %bitcast.33), custom_call_target="tpu_custom_call" | custom-call | flops 2000000000 | bytes 1048576 | tf_op jit(solution)/shard_map/pallas_call | solution.py:66
  60.0 2.2 %collective-permute-start.3 = (bf16[160,512]{1,0:T(8,128)(2,1)S(1)}, bf16[160,512]{1,0:T(8,128)(2,1)S(1)}, u32[]{:S(2)}, u32[]{:S(2)}) collective-permute-start(bf16[160,512]{1,0:T(8,128)(2,1)S(1)} %collective-permute-done.2.refs_4_), channel_id=1, source_target_pairs={{0,4},{4,8},{8,12},{12,14},{14,10},{10,6},{6,2},{2,0},{1,5},{5,9},... | collective-permute-start | bytes 491528 | tf_op jit(solution)/shard_map/ppermute | solution.py:550
  62.2 1.8 %shard_map.146 = (bf16[256,256]{1,0:T(8,128)(2,1)S(1)}, bf16[256,256]{1,0:T(8,128)(2,1)S(1)}, f32[256,128]{1,0:T(8,128)S(1)}) custom-call(s32[4]{0:T(128)S(1)} %pad_add_fusion.scalar_ref, s32[1,256]{1,0:T(1,128)S(1)} %bitcast.46, bf16[256,4096]{1,0:T(8,128)(2,1)S(1)} %bitcast.29, bf16[256,512]{1,0:T(8,128)(2,1)S(1)} %bitcast.41, bf16[256,4096]{1,0:T(8,128)(2,1)S(1)} %bitcast.34), custom_call_target="tpu_custom_call" | custom-call | flops 2000000000 | bytes 1048576 | tf_op jit(solution)/shard_map/pallas_call | solution.py:66
  64.0 2.5 %collective-permute-done.3.refs_2_ = bf16[160,512]{1,0:T(8,128)(2,1)S(1)} collective-permute-done((bf16[160,512]{1,0:T(8,128)(2,1)S(1)}, bf16[160,512]{1,0:T(8,128)(2,1)S(1)}, u32[]{:S(2)}, u32[]{:S(2)}) %collective-permute-start.3) | collective-permute-done | bytes 163872 | tf_op jit(solution)/shard_map/ppermute | solution.py:550
  66.4 1.7 %collective-permute-start.4 = (bf16[160,512]{1,0:T(8,128)(2,1)S(1)}, bf16[160,512]{1,0:T(8,128)(2,1)S(1)}, u32[]{:S(2)}, u32[]{:S(2)}) collective-permute-start(bf16[160,512]{1,0:T(8,128)(2,1)S(1)} %collective-permute-done.3.refs_2_), channel_id=1, source_target_pairs={{0,16},{16,0},{1,17},{17,1},{2,18},{18,2},{3,19},{19,3},{4,20},{20... | collective-permute-start | bytes 491528 | tf_op jit(solution)/shard_map/ppermute | solution.py:553
  68.1 1.8 %shard_map.147 = (bf16[256,256]{1,0:T(8,128)(2,1)S(1)}, bf16[256,256]{1,0:T(8,128)(2,1)S(1)}, f32[256,128]{1,0:T(8,128)S(1)}) custom-call(s32[4]{0:T(128)S(1)} %pad_add_fusion.scalar_ref, s32[1,256]{1,0:T(1,128)S(1)} %bitcast.47, bf16[256,4096]{1,0:T(8,128)(2,1)S(1)} %bitcast.30, bf16[256,512]{1,0:T(8,128)(2,1)S(1)} %bitcast.42, bf16[256,4096]{1,0:T(8,128)(2,1)S(1)} %bitcast.35), custom_call_target="tpu_custom_call" | custom-call | flops 2000000000 | bytes 1048576 | tf_op jit(solution)/shard_map/pallas_call | solution.py:66
  71.8 1.8 %shard_map.144 = (bf16[256,256]{1,0:T(8,128)(2,1)S(1)}, bf16[256,256]{1,0:T(8,128)(2,1)S(1)}, f32[256,128]{1,0:T(8,128)S(1)}) custom-call(s32[4]{0:T(128)S(1)} %pad_add_fusion.scalar_ref, s32[1,256]{1,0:T(1,128)S(1)} %bitcast.49, bf16[256,4096]{1,0:T(8,128)(2,1)S(1)} %bitcast.32, bf16[256,512]{1,0:T(8,128)(2,1)S(1)} %bitcast.44, ...), custom_call_target="tpu_custom_call" | custom-call | flops 2000000000 | bytes 1048576 | tf_op jit(solution)/shard_map/pallas_call | solution.py:66
  74.2 1.8 %collective-permute-start.41 = (bf16[128,2048]{1,0:T(8,128)(2,1)S(1)}, bf16[128,2048]{1,0:T(8,128)(2,1)S(1)}, u32[]{:S(2)}, u32[]{:S(2)}) collective-permute-start(bf16[128,2048]{1,0:T(8,128)(2,1)S(1)} %shard_map.154), channel_id=1, source_target_pairs={{0,2},{2,0},{4,6},{6,4},{8,10},{10,8},{12,14},{14,12},{1,3},{3,1},... | collective-permute-start | bytes 1572872 | tf_op jit(solution)/shard_map/ppermute | solution.py:512
  76.1 2.4 %shard_map.148 = (f32[64,512]{1,0:T(8,128)S(1)}, bf16[64,256]{1,0:T(8,128)(2,1)S(1)}, f32[64,512]{1,0:T(8,128)S(1)}) custom-call(s32[4]{0:T(128)S(1)} %pad_add_fusion.scalar_ref, bf16[256,8192]{1,0:T(8,128)(2,1)S(1)} %bitcast.19, bf16[64,8192]{1,0:T(8,128)(2,1)S(1)} %bitcast.26, bf16[160,512]{1,0:T(8,128)(2,1)S(1)} %collective-permute-done.3.refs_2_, ...), custom_call_target="tpu_custom_call" | custom-call | flops 1000000000 | bytes 1048576 | tf_op jit(solution)/shard_map/pallas_call | solution.py:66
  80.0 1.0 shard_map.151
  81.0 3.5 %collective-permute-start.32 = (bf16[72,512]{1,0:T(8,128)(2,1)S(1)}, bf16[72,512]{1,0:T(8,128)(2,1)S(1)}, u32[]{:S(2)}, u32[]{:S(2)}) collective-permute-start(bf16[72,512]{1,0:T(8,128)(2,1)S(1)} %get-tuple-element.74), channel_id=1, source_target_pairs={{0,8},{2,10},{4,12},{6,14},{8,0},{10,2},{12,4},{14,6},{1,9},{3,11}... | collective-permute-start | bytes 221192 | tf_op jit(solution)/shard_map/ppermute | solution.py:512
  84.5 3.9 %collective-permute-start.34 = (bf16[72,512]{1,0:T(8,128)(2,1)S(1)}, bf16[72,512]{1,0:T(8,128)(2,1)S(1)}, u32[]{:S(2)}, u32[]{:S(2)}) collective-permute-start(bf16[72,512]{1,0:T(8,128)(2,1)S(1)} %get-tuple-element.76), channel_id=1, source_target_pairs={{0,12},{2,14},{4,8},{6,10},{8,4},{10,6},{12,0},{14,2},{1,13},{3,15... | collective-permute-start | bytes 221192 | tf_op jit(solution)/shard_map/ppermute | solution.py:512
  89.4 1.0 shard_map.150
  90.4 1.8 %collective-permute-done.32.refs_7_ = bf16[72,512]{1,0:T(8,128)(2,1)S(1)} collective-permute-done((bf16[72,512]{1,0:T(8,128)(2,1)S(1)}, bf16[72,512]{1,0:T(8,128)(2,1)S(1)}, u32[]{:S(2)}, u32[]{:S(2)}) %collective-permute-start.32) | collective-permute-done | bytes 73760 | tf_op jit(solution)/shard_map/ppermute | solution.py:512
  92.2 3.9 %collective-permute-done.33.refs_8_ = bf16[72,512]{1,0:T(8,128)(2,1)S(1)} collective-permute-done((bf16[72,512]{1,0:T(8,128)(2,1)S(1)}, bf16[72,512]{1,0:T(8,128)(2,1)S(1)}, u32[]{:S(2)}, u32[]{:S(2)}) %collective-permute-start.33) | collective-permute-done | bytes 73760 | tf_op jit(solution)/shard_map/ppermute | solution.py:512
  96.2 2.0 %collective-permute-start.31 = (bf16[72,512]{1,0:T(8,128)(2,1)S(1)}, bf16[72,512]{1,0:T(8,128)(2,1)S(1)}, u32[]{:S(2)}, u32[]{:S(2)}) collective-permute-start(bf16[72,512]{1,0:T(8,128)(2,1)S(1)} %get-tuple-element.73), channel_id=1, source_target_pairs={{0,6},{2,4},{4,2},{6,0},{8,14},{10,12},{12,10},{14,8},{1,7},{3,5},... | collective-permute-start | bytes 221192 | tf_op jit(solution)/shard_map/ppermute | solution.py:512
  98.1 2.4 %collective-permute-done.30.refs_5_ = bf16[72,512]{1,0:T(8,128)(2,1)S(1)} collective-permute-done((bf16[72,512]{1,0:T(8,128)(2,1)S(1)}, bf16[72,512]{1,0:T(8,128)(2,1)S(1)}, u32[]{:S(2)}, u32[]{:S(2)}) %collective-permute-start.30) | collective-permute-done | bytes 73760 | tf_op jit(solution)/shard_map/ppermute | solution.py:512
  102.1 2.1 %collective-permute-start.37 = (bf16[80,512]{1,0:T(8,128)(2,1)S(1)}, bf16[80,512]{1,0:T(8,128)(2,1)S(1)}, u32[]{:S(2)}, u32[]{:S(2)}) collective-permute-start(bf16[80,512]{1,0:T(8,128)(2,1)S(1)} %get-tuple-element.79.refs_0_.refs_3_), channel_id=1, source_target_pairs={{0,4},{2,6},{4,0},{6,2},{8,12},{10,14},{12,8},{14,10},{1,5},{3,7},... | collective-permute-start | bytes 245768 | tf_op jit(solution)/shard_map/ppermute | solution.py:512
  104.1 2.5 %collective-permute-start.38 = (bf16[80,512]{1,0:T(8,128)(2,1)S(1)}, bf16[80,512]{1,0:T(8,128)(2,1)S(1)}, u32[]{:S(2)}, u32[]{:S(2)}) collective-permute-start(bf16[80,512]{1,0:T(8,128)(2,1)S(1)} %get-tuple-element.79.refs_0_.refs_3_), channel_id=1, source_target_pairs={{0,8},{2,10},{4,12},{6,14},{8,0},{10,2},{12,4},{14,6},{1,9},{3,11}... | collective-permute-start | bytes 245768 | tf_op jit(solution)/shard_map/ppermute | solution.py:512
  107.5 4.0 %collective-permute-done.38.refs_2_.refs_5_ = bf16[80,512]{1,0:T(8,128)(2,1)S(1)} collective-permute-done((bf16[80,512]{1,0:T(8,128)(2,1)S(1)}, bf16[80,512]{1,0:T(8,128)(2,1)S(1)}, u32[]{:S(2)}, u32[]{:S(2)}) %collective-permute-start.38) | collective-permute-done | bytes 81952 | tf_op jit(solution)/shard_map/ppermute | solution.py:512
  111.5 1.5 %collective-permute-done.39.refs_3_.refs_6_ = bf16[80,512]{1,0:T(8,128)(2,1)S(1)} collective-permute-done((bf16[80,512]{1,0:T(8,128)(2,1)S(1)}, bf16[80,512]{1,0:T(8,128)(2,1)S(1)}, u32[]{:S(2)}, u32[]{:S(2)}) %collective-permute-start.39) | collective-permute-done | bytes 81952 | tf_op jit(solution)/shard_map/ppermute | solution.py:512
  114.4 1.7 %collective-permute-start.44 = (f32[64,64]{1,0:T(8,128)S(1)}, f32[64,64]{1,0:T(8,128)S(1)}, u32[]{:S(2)}, u32[]{:S(2)}) collective-permute-start(f32[64,64]{1,0:T(8,128)S(1)} %get-tuple-element.83), channel_id=1, source_target_pairs={{0,1},{1,0},{2,3},{3,2},{4,5},{5,4},{6,7},{7,6},{8,9},{9,8},{10,11... | collective-permute-start | bytes 49160 | tf_op jit(solution)/shard_map/ppermute | solution.py:509
  117.2 1.7 %shard_map.149.refs_1_ = bf16[4,512,64]{2,1,0:T(8,128)(2,1)S(1)} custom-call(s32[4]{0:T(128)S(1)} %pad_add_fusion.scalar_ref, s32[1,64]{1,0:T(1,128)S(1)} %bitcast.52, bf16[64,4096]{1,0:T(8,128)(2,1)S(1)} %bitcast.50, bf16[64,512]{1,0:T(8,128)(2,1)S(1)} %bitcast.51), custom_call_target="tpu_custom_call" | custom-call | flops 1000000000 | bytes 1048576 | tf_op jit(solution)/shard_map/pallas_call | solution.py:66
  119.0 2.0 %collective-permute-done.40.refs_5_ = f32[32,512]{1,0:T(8,128)S(1)} collective-permute-done((f32[32,512]{1,0:T(8,128)S(1)}, f32[32,512]{1,0:T(8,128)S(1)}, u32[]{:S(2)}, u32[]{:S(2)}) %collective-permute-start.40) | collective-permute-done | bytes 65568 | tf_op jit(solution)/shard_map/ppermute | solution.py:512
  121.0 1.9 %shard_map.156 = (bf16[64,4096]{1,0:T(8,128)(2,1)}, f32[64,1024]{1,0:T(8,128)}, f32[64,512]{1,0:T(8,128)}) custom-call(s32[4]{0:T(128)S(1)} %pad_add_fusion.scalar_ref, f32[64,512]{1,0:T(8,128)S(1)} %get-tuple-element.66.refs_0_, bf16[4,512,64]{2,1,0:T(8,128)(2,1)S(1)} %shard_map.149.refs_1_, f32[64,512]{1,0:T(8,128)S(1)} %get-tuple-element.78.refs_2_, ...), custom_call_target="tpu_custom_call" | custom-call | flops 200000000 | bytes 1048576 | tf_op jit(solution)/shard_map/pallas_call | solution.py:66
  (83 shorter events, 14.2 us)
Async XLA Ops:
  0.7 51.4 %copy-start = (bf16[1,256,8192]{2,1,0:T(8,128)(2,1)S(1)}, bf16[1,256,8192]{2,1,0:T(8,128)(2,1)}, u32[]{:S(2)}) copy-start(bf16[1,256,8192]{2,1,0:T(8,128)(2,1)} %param.12) | copy-start | bytes 12582916
  0.7 51.4 %copy-start.1 = (bf16[1,64,8192]{2,1,0:T(8,128)(2,1)S(1)}, bf16[1,64,8192]{2,1,0:T(8,128)(2,1)}, u32[]{:S(2)}) copy-start(bf16[1,64,8192]{2,1,0:T(8,128)(2,1)} %param.20) | copy-start | bytes 3145732
  3.3 48.8 %collective-permute-start.12 = (bf16[256,4096]{1,0:T(8,128)(2,1)S(1)}, bf16[256,4096]{1,0:T(8,128)(2,1)S(1)}, u32[]{:S(2)}, u32[]{:S(2)}) collective-permute-start(bf16[256,4096]{1,0:T(8,128)(2,1)S(1)} %get-tuple-element.47), channel_id=1, source_target_pairs={{0,1},{1,0},{2,3},{3,2},{4,5},{5,4},{6,7},{7,6},{8,9},{9,8},{10,11... | collective-permute-start | bytes 6291464 | tf_op jit(solution)/shard_map/ppermute | solution.py:509
  5.1 15.1 %collective-permute-start.15 = (bf16[256,512]{1,0:T(8,128)(2,1)S(1)}, bf16[256,512]{1,0:T(8,128)(2,1)S(1)}, u32[]{:S(2)}, u32[]{:S(2)}) collective-permute-start(bf16[256,512]{1,0:T(8,128)(2,1)S(1)} %get-tuple-element.46.refs_6_), channel_id=1, source_target_pairs={{0,4},{4,8},{8,12},{12,14},{14,10},{10,6},{6,2},{2,0},{1,5},{5,9},... | collective-permute-start | bytes 786440 | tf_op jit(solution)/shard_map/ppermute | solution.py:550
  7.8 14.2 %collective-permute-start.5 = (bf16[256,512]{1,0:T(8,128)(2,1)S(1)}, bf16[256,512]{1,0:T(8,128)(2,1)S(1)}, u32[]{:S(2)}, u32[]{:S(2)}) collective-permute-start(bf16[256,512]{1,0:T(8,128)(2,1)S(1)} %get-tuple-element.46.refs_6_), channel_id=1, source_target_pairs={{4,0},{8,4},{12,8},{14,12},{10,14},{6,10},{2,6},{0,2},{5,1},{9,5},... | collective-permute-start | bytes 786440 | tf_op jit(solution)/shard_map/ppermute | solution.py:550
  7.8 10.4 %collective-permute-start = (bf16[160,512]{1,0:T(8,128)(2,1)S(1)}, bf16[160,512]{1,0:T(8,128)(2,1)S(1)}, u32[]{:S(2)}, u32[]{:S(2)}) collective-permute-start(bf16[160,512]{1,0:T(8,128)(2,1)S(1)} %get-tuple-element.45.refs_4_), channel_id=1, source_target_pairs={{0,4},{4,8},{8,12},{12,14},{14,10},{10,6},{6,2},{2,0},{1,5},{5,9},... | collective-permute-start | bytes 491528 | tf_op jit(solution)/shard_map/ppermute | solution.py:550
  9.8 10.2 %collective-permute-start.18 = (bf16[160,512]{1,0:T(8,128)(2,1)S(1)}, bf16[160,512]{1,0:T(8,128)(2,1)S(1)}, u32[]{:S(2)}, u32[]{:S(2)}) collective-permute-start(bf16[160,512]{1,0:T(8,128)(2,1)S(1)} %get-tuple-element.45.refs_4_), channel_id=1, source_target_pairs={{4,0},{8,4},{12,8},{14,12},{10,14},{6,10},{2,6},{0,2},{5,1},{9,5},... | collective-permute-start | bytes 491528 | tf_op jit(solution)/shard_map/ppermute | solution.py:550
  18.1 6.0 %collective-permute-start.1 = (bf16[160,512]{1,0:T(8,128)(2,1)S(1)}, bf16[160,512]{1,0:T(8,128)(2,1)S(1)}, u32[]{:S(2)}, u32[]{:S(2)}) collective-permute-start(bf16[160,512]{1,0:T(8,128)(2,1)S(1)} %collective-permute-done.refs_7_), channel_id=1, source_target_pairs={{0,4},{4,8},{8,12},{12,14},{14,10},{10,6},{6,2},{2,0},{1,5},{5,9},... | collective-permute-start | bytes 491528 | tf_op jit(solution)/shard_map/ppermute | solution.py:550
  20.0 5.4 %collective-permute-start.19 = (bf16[160,512]{1,0:T(8,128)(2,1)S(1)}, bf16[160,512]{1,0:T(8,128)(2,1)S(1)}, u32[]{:S(2)}, u32[]{:S(2)}) collective-permute-start(bf16[160,512]{1,0:T(8,128)(2,1)S(1)} %collective-permute-done.18.refs_10_), channel_id=1, source_target_pairs={{4,0},{8,4},{12,8},{14,12},{10,14},{6,10},{2,6},{0,2},{5,1},{9,5},... | collective-permute-start | bytes 491528 | tf_op jit(solution)/shard_map/ppermute | solution.py:550
  20.2 7.1 %collective-permute-start.22 = (bf16[160,512]{1,0:T(8,128)(2,1)S(1)}, bf16[160,512]{1,0:T(8,128)(2,1)S(1)}, u32[]{:S(2)}, u32[]{:S(2)}) collective-permute-start(bf16[160,512]{1,0:T(8,128)(2,1)S(1)} %collective-permute-done.refs_7_), channel_id=1, source_target_pairs={{0,16},{16,0},{1,17},{17,1},{2,18},{18,2},{3,19},{19,3},{4,20},{20... | collective-permute-start | bytes 491528 | tf_op jit(solution)/shard_map/ppermute | solution.py:553
  21.9 8.8 %collective-permute-start.23 = (bf16[160,512]{1,0:T(8,128)(2,1)S(1)}, bf16[160,512]{1,0:T(8,128)(2,1)S(1)}, u32[]{:S(2)}, u32[]{:S(2)}) collective-permute-start(bf16[160,512]{1,0:T(8,128)(2,1)S(1)} %collective-permute-done.18.refs_10_), channel_id=1, source_target_pairs={{0,16},{16,0},{1,17},{17,1},{2,18},{18,2},{3,19},{19,3},{4,20},{20... | collective-permute-start | bytes 491528 | tf_op jit(solution)/shard_map/ppermute | solution.py:553
  24.1 26.4 %collective-permute-start.13 = (bf16[64,4096]{1,0:T(8,128)(2,1)S(1)}, bf16[64,4096]{1,0:T(8,128)(2,1)S(1)}, u32[]{:S(2)}, u32[]{:S(2)}) collective-permute-start(bf16[64,4096]{1,0:T(8,128)(2,1)S(1)} %get-tuple-element.48), channel_id=1, source_target_pairs={{0,1},{1,0},{2,3},{3,2},{4,5},{5,4},{6,7},{7,6},{8,9},{9,8},{10,11... | collective-permute-start | bytes 1572872 | tf_op jit(solution)/shard_map/ppermute | solution.py:509
  25.4 8.9 %collective-permute-start.24 = (bf16[160,512]{1,0:T(8,128)(2,1)S(1)}, bf16[160,512]{1,0:T(8,128)(2,1)S(1)}, u32[]{:S(2)}, u32[]{:S(2)}) collective-permute-start(bf16[160,512]{1,0:T(8,128)(2,1)S(1)} %collective-permute-done.1.refs_13_), channel_id=1, source_target_pairs={{0,16},{16,0},{1,17},{17,1},{2,18},{18,2},{3,19},{19,3},{4,20},{20... | collective-permute-start | bytes 491528 | tf_op jit(solution)/shard_map/ppermute | solution.py:553
  27.2 10.6 %collective-permute-start.6 = (bf16[256,512]{1,0:T(8,128)(2,1)S(1)}, bf16[256,512]{1,0:T(8,128)(2,1)S(1)}, u32[]{:S(2)}, u32[]{:S(2)}) collective-permute-start(bf16[256,512]{1,0:T(8,128)(2,1)S(1)} %collective-permute-done.5.refs_12_), channel_id=1, source_target_pairs={{4,0},{8,4},{12,8},{14,12},{10,14},{6,10},{2,6},{0,2},{5,1},{9,5},... | collective-permute-start | bytes 786440 | tf_op jit(solution)/shard_map/ppermute | solution.py:550
  30.7 5.4 %collective-permute-start.25 = (bf16[160,512]{1,0:T(8,128)(2,1)S(1)}, bf16[160,512]{1,0:T(8,128)(2,1)S(1)}, u32[]{:S(2)}, u32[]{:S(2)}) collective-permute-start(bf16[160,512]{1,0:T(8,128)(2,1)S(1)} %collective-permute-done.19.refs_16_), channel_id=1, source_target_pairs={{0,16},{16,0},{1,17},{17,1},{2,18},{18,2},{3,19},{19,3},{4,20},{20... | collective-permute-start | bytes 491528 | tf_op jit(solution)/shard_map/ppermute | solution.py:553
  34.3 10.5 %collective-permute-start.16 = (bf16[256,512]{1,0:T(8,128)(2,1)S(1)}, bf16[256,512]{1,0:T(8,128)(2,1)S(1)}, u32[]{:S(2)}, u32[]{:S(2)}) collective-permute-start(bf16[256,512]{1,0:T(8,128)(2,1)S(1)} %collective-permute-done.15.refs_9_), channel_id=1, source_target_pairs={{0,4},{4,8},{8,12},{12,14},{14,10},{10,6},{6,2},{2,0},{1,5},{5,9},... | collective-permute-start | bytes 786440 | tf_op jit(solution)/shard_map/ppermute | solution.py:550
  36.1 7.4 %collective-permute-start.2 = (bf16[160,512]{1,0:T(8,128)(2,1)S(1)}, bf16[160,512]{1,0:T(8,128)(2,1)S(1)}, u32[]{:S(2)}, u32[]{:S(2)}) collective-permute-start(bf16[160,512]{1,0:T(8,128)(2,1)S(1)} %collective-permute-done.1.refs_13_), channel_id=1, source_target_pairs={{0,4},{4,8},{8,12},{12,14},{14,10},{10,6},{6,2},{2,0},{1,5},{5,9},... | collective-permute-start | bytes 491528 | tf_op jit(solution)/shard_map/ppermute | solution.py:550
  37.9 13.1 %collective-permute-start.7 = (bf16[256,512]{1,0:T(8,128)(2,1)S(1)}, bf16[256,512]{1,0:T(8,128)(2,1)S(1)}, u32[]{:S(2)}, u32[]{:S(2)}) collective-permute-start(bf16[256,512]{1,0:T(8,128)(2,1)S(1)} %collective-permute-done.6.refs_18_), channel_id=1, source_target_pairs={{4,0},{8,4},{12,8},{14,12},{10,14},{6,10},{2,6},{0,2},{5,1},{9,5},... | collective-permute-start | bytes 786440 | tf_op jit(solution)/shard_map/ppermute | solution.py:550
  43.6 5.3 %collective-permute-start.20 = (bf16[160,512]{1,0:T(8,128)(2,1)S(1)}, bf16[160,512]{1,0:T(8,128)(2,1)S(1)}, u32[]{:S(2)}, u32[]{:S(2)}) collective-permute-start(bf16[160,512]{1,0:T(8,128)(2,1)S(1)} %collective-permute-done.19.refs_16_), channel_id=1, source_target_pairs={{4,0},{8,4},{12,8},{14,12},{10,14},{6,10},{2,6},{0,2},{5,1},{9,5},... | collective-permute-start | bytes 491528 | tf_op jit(solution)/shard_map/ppermute | solution.py:550
  44.7 11.2 %collective-permute-start.17 = (bf16[256,512]{1,0:T(8,128)(2,1)S(1)}, bf16[256,512]{1,0:T(8,128)(2,1)S(1)}, u32[]{:S(2)}, u32[]{:S(2)}) collective-permute-start(bf16[256,512]{1,0:T(8,128)(2,1)S(1)} %collective-permute-done.16.refs_15_), channel_id=1, source_target_pairs={{0,4},{4,8},{8,12},{12,14},{14,10},{10,6},{6,2},{2,0},{1,5},{5,9},... | collective-permute-start | bytes 786440 | tf_op jit(solution)/shard_map/ppermute | solution.py:550
  48.9 6.5 %collective-permute-start.14 = (bf16[160,512]{1,0:T(8,128)(2,1)S(1)}, bf16[160,512]{1,0:T(8,128)(2,1)S(1)}, u32[]{:S(2)}, u32[]{:S(2)}) collective-permute-start(bf16[160,512]{1,0:T(8,128)(2,1)S(1)} %collective-permute-done.2.refs_4_), channel_id=1, source_target_pairs={{0,16},{16,0},{1,17},{17,1},{2,18},{18,2},{3,19},{19,3},{4,20},{20... | collective-permute-start | bytes 491528 | tf_op jit(solution)/shard_map/ppermute | solution.py:553
  50.6 5.4 %collective-permute-start.21 = (bf16[160,512]{1,0:T(8,128)(2,1)S(1)}, bf16[160,512]{1,0:T(8,128)(2,1)S(1)}, u32[]{:S(2)}, u32[]{:S(2)}) collective-permute-start(bf16[160,512]{1,0:T(8,128)(2,1)S(1)} %collective-permute-done.20.refs_7_), channel_id=1, source_target_pairs={{0,16},{16,0},{1,17},{17,1},{2,18},{18,2},{3,19},{19,3},{4,20},{20... | collective-permute-start | bytes 491528 | tf_op jit(solution)/shard_map/ppermute | solution.py:553
  50.9 17.2 %collective-permute-start.8 = (bf16[256,512]{1,0:T(8,128)(2,1)S(1)}, bf16[256,512]{1,0:T(8,128)(2,1)S(1)}, u32[]{:S(2)}, u32[]{:S(2)}) collective-permute-start(bf16[256,512]{1,0:T(8,128)(2,1)S(1)} %collective-permute-done.7.refs_9_), channel_id=1, source_target_pairs={{4,0},{8,4},{12,8},{14,12},{10,14},{6,10},{2,6},{0,2},{5,1},{9,5},... | collective-permute-start | bytes 786440 | tf_op jit(solution)/shard_map/ppermute | solution.py:550
  57.7 18.3 %collective-permute-start.26 = (f32[352,512]{1,0:T(8,128)S(1)}, f32[352,512]{1,0:T(8,128)S(1)}, u32[]{:S(2)}, u32[]{:S(2)}) collective-permute-start(f32[352,512]{1,0:T(8,128)S(1)} %get-tuple-element.53), channel_id=1, source_target_pairs={{0,1},{1,0},{2,3},{3,2},{4,5},{5,4},{6,7},{7,6},{8,9},{9,8},{10,11... | collective-permute-start | bytes 2162696 | tf_op jit(solution)/shard_map/ppermute | solution.py:509
  60.0 6.4 %collective-permute-start.3 = (bf16[160,512]{1,0:T(8,128)(2,1)S(1)}, bf16[160,512]{1,0:T(8,128)(2,1)S(1)}, u32[]{:S(2)}, u32[]{:S(2)}) collective-permute-start(bf16[160,512]{1,0:T(8,128)(2,1)S(1)} %collective-permute-done.2.refs_4_), channel_id=1, source_target_pairs={{0,4},{4,8},{8,12},{12,14},{14,10},{10,6},{6,2},{2,0},{1,5},{5,9},... | collective-permute-start | bytes 491528 | tf_op jit(solution)/shard_map/ppermute | solution.py:550
  66.4 5.4 %collective-permute-start.4 = (bf16[160,512]{1,0:T(8,128)(2,1)S(1)}, bf16[160,512]{1,0:T(8,128)(2,1)S(1)}, u32[]{:S(2)}, u32[]{:S(2)}) collective-permute-start(bf16[160,512]{1,0:T(8,128)(2,1)S(1)} %collective-permute-done.3.refs_2_), channel_id=1, source_target_pairs={{0,16},{16,0},{1,17},{17,1},{2,18},{18,2},{3,19},{19,3},{4,20},{20... | collective-permute-start | bytes 491528 | tf_op jit(solution)/shard_map/ppermute | solution.py:553
  68.1 7.9 %collective-permute-start.11 = (bf16[256,512]{1,0:T(8,128)(2,1)S(1)}, bf16[256,512]{1,0:T(8,128)(2,1)S(1)}, u32[]{:S(2)}, u32[]{:S(2)}) collective-permute-start(bf16[256,512]{1,0:T(8,128)(2,1)S(1)} %collective-permute-done.8.refs_4_), channel_id=1, source_target_pairs={{0,1},{1,0},{2,3},{3,2},{4,5},{5,4},{6,7},{7,6},{8,9},{9,8},{10,11... | collective-permute-start | bytes 786440 | tf_op jit(solution)/shard_map/ppermute | solution.py:509
  70.5 5.6 %collective-permute-start.9 = (bf16[160,512]{1,0:T(8,128)(2,1)S(1)}, bf16[160,512]{1,0:T(8,128)(2,1)S(1)}, u32[]{:S(2)}, u32[]{:S(2)}) collective-permute-start(bf16[160,512]{1,0:T(8,128)(2,1)S(1)} %collective-permute-done.3.refs_2_), channel_id=1, source_target_pairs={{0,1},{1,0},{2,3},{3,2},{4,5},{5,4},{6,7},{7,6},{8,9},{9,8},{10,11... | collective-permute-start | bytes 491528 | tf_op jit(solution)/shard_map/ppermute | solution.py:509
  71.8 4.2 %collective-permute-start.10 = (bf16[160,512]{1,0:T(8,128)(2,1)S(1)}, bf16[160,512]{1,0:T(8,128)(2,1)S(1)}, u32[]{:S(2)}, u32[]{:S(2)}) collective-permute-start(bf16[160,512]{1,0:T(8,128)(2,1)S(1)} %collective-permute-done.4.refs_3_), channel_id=1, source_target_pairs={{0,1},{1,0},{2,3},{3,2},{4,5},{5,4},{6,7},{7,6},{8,9},{9,8},{10,11... | collective-permute-start | bytes 491528 | tf_op jit(solution)/shard_map/ppermute | solution.py:509
  74.2 32.6 %collective-permute-start.41 = (bf16[128,2048]{1,0:T(8,128)(2,1)S(1)}, bf16[128,2048]{1,0:T(8,128)(2,1)S(1)}, u32[]{:S(2)}, u32[]{:S(2)}) collective-permute-start(bf16[128,2048]{1,0:T(8,128)(2,1)S(1)} %shard_map.154), channel_id=1, source_target_pairs={{0,2},{2,0},{4,6},{6,4},{8,10},{10,8},{12,14},{14,12},{1,3},{3,1},... | collective-permute-start | bytes 1572872 | tf_op jit(solution)/shard_map/ppermute | solution.py:512
  78.5 1.5 %collective-permute-start.28 = (f32[64,512]{1,0:T(8,128)S(1)}, f32[64,512]{1,0:T(8,128)S(1)}, u32[]{:S(2)}, u32[]{:S(2)}) collective-permute-start(f32[64,512]{1,0:T(8,128)S(1)} %get-tuple-element.68.refs_4_), channel_id=1, source_target_pairs={{0,1},{1,0},{2,3},{3,2},{4,5},{5,4},{6,7},{7,6},{8,9},{9,8},{10,11... | collective-permute-start | bytes 393224 | tf_op jit(solution)/shard_map/ppermute | solution.py:509
  78.7 1.2 collective-permute-start.27
  81.0 11.2 %collective-permute-start.32 = (bf16[72,512]{1,0:T(8,128)(2,1)S(1)}, bf16[72,512]{1,0:T(8,128)(2,1)S(1)}, u32[]{:S(2)}, u32[]{:S(2)}) collective-permute-start(bf16[72,512]{1,0:T(8,128)(2,1)S(1)} %get-tuple-element.74), channel_id=1, source_target_pairs={{0,8},{2,10},{4,12},{6,14},{8,0},{10,2},{12,4},{14,6},{1,9},{3,11}... | collective-permute-start | bytes 221192 | tf_op jit(solution)/shard_map/ppermute | solution.py:512
  84.5 11.7 %collective-permute-start.33 = (bf16[72,512]{1,0:T(8,128)(2,1)S(1)}, bf16[72,512]{1,0:T(8,128)(2,1)S(1)}, u32[]{:S(2)}, u32[]{:S(2)}) collective-permute-start(bf16[72,512]{1,0:T(8,128)(2,1)S(1)} %get-tuple-element.75), channel_id=1, source_target_pairs={{0,10},{2,8},{4,14},{6,12},{8,2},{10,0},{12,6},{14,4},{1,11},{3,9}... | collective-permute-start | bytes 221192 | tf_op jit(solution)/shard_map/ppermute | solution.py:512
  84.5 11.7 %collective-permute-start.34 = (bf16[72,512]{1,0:T(8,128)(2,1)S(1)}, bf16[72,512]{1,0:T(8,128)(2,1)S(1)}, u32[]{:S(2)}, u32[]{:S(2)}) collective-permute-start(bf16[72,512]{1,0:T(8,128)(2,1)S(1)} %get-tuple-element.76), channel_id=1, source_target_pairs={{0,12},{2,14},{4,8},{6,10},{8,4},{10,6},{12,0},{14,2},{1,13},{3,15... | collective-permute-start | bytes 221192 | tf_op jit(solution)/shard_map/ppermute | solution.py:512
  88.4 9.8 %collective-permute-start.35 = (bf16[72,512]{1,0:T(8,128)(2,1)S(1)}, bf16[72,512]{1,0:T(8,128)(2,1)S(1)}, u32[]{:S(2)}, u32[]{:S(2)}) collective-permute-start(bf16[72,512]{1,0:T(8,128)(2,1)S(1)} %get-tuple-element.77), channel_id=1, source_target_pairs={{0,14},{2,12},{4,10},{6,8},{8,6},{10,4},{12,2},{14,0},{1,15},{3,13... | collective-permute-start | bytes 221192 | tf_op jit(solution)/shard_map/ppermute | solution.py:512
  90.4 26.8 %copy-start.8 = (bf16[1,64,4096]{2,1,0:T(8,128)(2,1)S(1)}, bf16[1,64,4096]{2,1,0:T(8,128)(2,1)}, u32[]{:S(2)}) copy-start(bf16[1,64,4096]{2,1,0:T(8,128)(2,1)} %param.21) | copy-start | bytes 1572868
  92.2 5.9 %collective-permute-start.29 = (bf16[72,512]{1,0:T(8,128)(2,1)S(1)}, bf16[72,512]{1,0:T(8,128)(2,1)S(1)}, u32[]{:S(2)}, u32[]{:S(2)}) collective-permute-start(bf16[72,512]{1,0:T(8,128)(2,1)S(1)} %get-tuple-element.71), channel_id=1, source_target_pairs={{0,2},{2,0},{4,6},{6,4},{8,10},{10,8},{12,14},{14,12},{1,3},{3,1},... | collective-permute-start | bytes 221192 | tf_op jit(solution)/shard_map/ppermute | solution.py:512
  96.2 4.4 %collective-permute-start.30 = (bf16[72,512]{1,0:T(8,128)(2,1)S(1)}, bf16[72,512]{1,0:T(8,128)(2,1)S(1)}, u32[]{:S(2)}, u32[]{:S(2)}) collective-permute-start(bf16[72,512]{1,0:T(8,128)(2,1)S(1)} %get-tuple-element.72), channel_id=1, source_target_pairs={{0,4},{2,6},{4,0},{6,2},{8,12},{10,14},{12,8},{14,10},{1,5},{3,7},... | collective-permute-start | bytes 221192 | tf_op jit(solution)/shard_map/ppermute | solution.py:512
  96.2 5.3 %collective-permute-start.31 = (bf16[72,512]{1,0:T(8,128)(2,1)S(1)}, bf16[72,512]{1,0:T(8,128)(2,1)S(1)}, u32[]{:S(2)}, u32[]{:S(2)}) collective-permute-start(bf16[72,512]{1,0:T(8,128)(2,1)S(1)} %get-tuple-element.73), channel_id=1, source_target_pairs={{0,6},{2,4},{4,2},{6,0},{8,14},{10,12},{12,10},{14,8},{1,7},{3,5},... | collective-permute-start | bytes 221192 | tf_op jit(solution)/shard_map/ppermute | solution.py:512
  102.1 5.4 %collective-permute-start.37 = (bf16[80,512]{1,0:T(8,128)(2,1)S(1)}, bf16[80,512]{1,0:T(8,128)(2,1)S(1)}, u32[]{:S(2)}, u32[]{:S(2)}) collective-permute-start(bf16[80,512]{1,0:T(8,128)(2,1)S(1)} %get-tuple-element.79.refs_0_.refs_3_), channel_id=1, source_target_pairs={{0,4},{2,6},{4,0},{6,2},{8,12},{10,14},{12,8},{14,10},{1,5},{3,7},... | collective-permute-start | bytes 245768 | tf_op jit(solution)/shard_map/ppermute | solution.py:512
  104.1 7.3 %collective-permute-start.38 = (bf16[80,512]{1,0:T(8,128)(2,1)S(1)}, bf16[80,512]{1,0:T(8,128)(2,1)S(1)}, u32[]{:S(2)}, u32[]{:S(2)}) collective-permute-start(bf16[80,512]{1,0:T(8,128)(2,1)S(1)} %get-tuple-element.79.refs_0_.refs_3_), channel_id=1, source_target_pairs={{0,8},{2,10},{4,12},{6,14},{8,0},{10,2},{12,4},{14,6},{1,9},{3,11}... | collective-permute-start | bytes 245768 | tf_op jit(solution)/shard_map/ppermute | solution.py:512
  106.6 6.3 %collective-permute-start.39 = (bf16[80,512]{1,0:T(8,128)(2,1)S(1)}, bf16[80,512]{1,0:T(8,128)(2,1)S(1)}, u32[]{:S(2)}, u32[]{:S(2)}) collective-permute-start(bf16[80,512]{1,0:T(8,128)(2,1)S(1)} %get-tuple-element.79.refs_0_.refs_3_), channel_id=1, source_target_pairs={{0,12},{2,14},{4,8},{6,10},{8,4},{10,6},{12,0},{14,2},{1,13},{3,15... | collective-permute-start | bytes 245768 | tf_op jit(solution)/shard_map/ppermute | solution.py:512
  106.8 12.2 %collective-permute-start.36 = (f32[64,512]{1,0:T(8,128)S(1)}, f32[64,512]{1,0:T(8,128)S(1)}, u32[]{:S(2)}, u32[]{:S(2)}) collective-permute-start(f32[64,512]{1,0:T(8,128)S(1)} %get-tuple-element.78.refs_2_), channel_id=1, source_target_pairs={{0,1},{1,0},{2,3},{3,2},{4,5},{5,4},{6,7},{7,6},{8,9},{9,8},{10,11... | collective-permute-start | bytes 393224 | tf_op jit(solution)/shard_map/ppermute | solution.py:509
  113.9 5.1 %collective-permute-start.42 = (f32[64,64]{1,0:T(8,128)S(1)}, f32[64,64]{1,0:T(8,128)S(1)}, u32[]{:S(2)}, u32[]{:S(2)}) collective-permute-start(f32[64,64]{1,0:T(8,128)S(1)} %get-tuple-element.81), channel_id=1, source_target_pairs={{0,2},{2,0},{4,6},{6,4},{8,10},{10,8},{12,14},{14,12},{1,3},{3,1},... | collective-permute-start | bytes 49160 | tf_op jit(solution)/shard_map/ppermute | solution.py:512
  114.4 4.5 %collective-permute-start.43 = (f32[64,64]{1,0:T(8,128)S(1)}, f32[64,64]{1,0:T(8,128)S(1)}, u32[]{:S(2)}, u32[]{:S(2)}) collective-permute-start(f32[64,64]{1,0:T(8,128)S(1)} %get-tuple-element.82), channel_id=1, source_target_pairs={{0,3},{1,2},{2,1},{3,0},{4,7},{5,6},{6,5},{7,4},{8,11},{9,10},{10,... | collective-permute-start | bytes 49160 | tf_op jit(solution)/shard_map/ppermute | solution.py:621
  114.4 4.5 %collective-permute-start.44 = (f32[64,64]{1,0:T(8,128)S(1)}, f32[64,64]{1,0:T(8,128)S(1)}, u32[]{:S(2)}, u32[]{:S(2)}) collective-permute-start(f32[64,64]{1,0:T(8,128)S(1)} %get-tuple-element.83), channel_id=1, source_target_pairs={{0,1},{1,0},{2,3},{3,2},{4,5},{5,4},{6,7},{7,6},{8,9},{9,8},{10,11... | collective-permute-start | bytes 49160 | tf_op jit(solution)/shard_map/ppermute | solution.py:509
  116.7 4.3 %collective-permute-start.40 = (f32[32,512]{1,0:T(8,128)S(1)}, f32[32,512]{1,0:T(8,128)S(1)}, u32[]{:S(2)}, u32[]{:S(2)}) collective-permute-start(f32[32,512]{1,0:T(8,128)S(1)} %shard_map.153.refs_4_), channel_id=1, source_target_pairs={{0,2},{2,0},{4,6},{6,4},{8,10},{10,8},{12,14},{14,12},{1,3},{3,1},... | collective-permute-start | bytes 196616 | tf_op jit(solution)/shard_map/ppermute | solution.py:512
  (8 other events, 77.6 us)

commit v3 on v2

--- a/solution.py
+++ b/solution.py
@@ -48,13 +48,6 @@
 
 def far_off(array):
     return pltpu.with_memory_space_constraint(array, pltpu.MemorySpace.HBM)
-
-
-def touch(s, arrays):
-    def kernel(s, refs, outs, scratch):
-        outs[0][...] = jnp.zeros_like(outs[0])
-
-    return call(kernel, [((8, 128), F32)], s, arrays)
 
 
 def call(kernel, outs, scalars, operands, scratch=(), flops=1e6, final=(), deps=()):
@@ -84,36 +77,38 @@
     return across == across.T
 
 
-def train_head_kernel(g, s, refs, outs, scratch):
+def train_heads_kernel(some, s, refs, outs, scratch):
     seg_row, q_ref, k_ref, t_ref = refs
-    high_out, rest_out, aimed_out = outs
     length = k_ref.shape[0]
-    keys = k_ref[:, g * HEAD_DIM : (g + 1) * HEAD_DIM]
     row = lax.broadcasted_iota(jnp.int32, (length, length), 0)
     col = lax.broadcasted_iota(jnp.int32, (length, length), 1)
     allowed = (row <= col) & same_segment(seg_row)
-    lanes = [slice(h * HEAD_DIM, (h + 1) * HEAD_DIM) for h in range(g * GROUP, (g + 1) * GROUP)]
-    every = []
-    for j in range(GROUP):
-        logits = dot_nt(keys, q_ref[:, lanes[j]]) * HEAD_DIM ** (-0.5)
-        logits = jnp.where(allowed, logits, -1e30)
-        peak = jnp.max(logits, axis=0, keepdims=True)
-        weights = jnp.exp(logits - peak)
-        every.append((weights * (1.0 / jnp.sum(weights, axis=0, keepdims=True))).astype(BF16))
-    gram = sum(dot_nt(probs, probs) for probs in every)
-    high = gram.astype(BF16)
-    high_out[...] = high
-    rest_out[...] = (gram - high.astype(F32)).astype(BF16)
-    aimed_out[...] = sum(dot_nn(probs, t_ref[:, lanes[j]]) for j, probs in enumerate(every))
-
-
-def train_head(s, g, seg_row, query, keyset, target, deps):
+    for i, g in enumerate(some):
+        high_out, rest_out, aimed_out = outs[3 * i : 3 * i + 3]
+        keys = k_ref[:, g * HEAD_DIM : (g + 1) * HEAD_DIM]
+        lanes = [slice(h * HEAD_DIM, (h + 1) * HEAD_DIM) for h in range(g * GROUP, (g + 1) * GROUP)]
+        every = []
+        for j in range(GROUP):
+            logits = dot_nt(keys, q_ref[:, lanes[j]]) * HEAD_DIM ** (-0.5)
+            logits = jnp.where(allowed, logits, -1e30)
+            peak = jnp.max(logits, axis=0, keepdims=True)
+            weights = jnp.exp(logits - peak)
+            every.append((weights * (1.0 / jnp.sum(weights, axis=0, keepdims=True))).astype(BF16))
+        gram = sum(dot_nt(probs, probs) for probs in every)
+        high = gram.astype(BF16)
+        high_out[...] = high
+        rest_out[...] = (gram - high.astype(F32)).astype(BF16)
+        aimed_out[...] = sum(dot_nn(probs, t_ref[:, lanes[j]]) for j, probs in enumerate(every))
+
+
+def train_heads(s, some, seg_row, query, keyset, target):
     length = query.shape[0]
-    return call(
-        functools.partial(train_head_kernel, g),
-        [((length, length), BF16), ((length, length), BF16), ((length, HEAD_DIM), F32)],
-        s, [seg_row, query, keyset, target], flops=2e9, deps=deps,
+    got = call(
+        functools.partial(train_heads_kernel, some),
+        [((length, length), BF16), ((length, length), BF16), ((length, HEAD_DIM), F32)] * len(some),
+        s, [seg_row, query, keyset, target], flops=2e9,
     )
+    return [got[3 * i : 3 * i + 3] for i in range(len(some))]
 
 
 def score_probs_kernel(s, refs, outs, scratch):
@@ -454,15 +449,31 @@
     )
 
 
-def score_kernel(s, refs, outs, scratch):
-    base, probs, fresh, fresh_got, up, up_got, *lows = refs
-    out, new_down, new_up = outs
+def renew_kernel(s, refs, outs, scratch):
+    fresh, fresh_got, up, up_got = refs
+    new_down, new_up, kept_up = outs
     half = new_down.shape[1] // 2
     parity = lax.rem(s[0], 2)
     for i in range(up.shape[0] // UP_ROWS):
         rows = slice(i * UP_ROWS, (i + 1) * UP_ROWS)
         new_up[up_place(2 * i + parity, half)] = up[rows, :]
         new_up[up_place(2 * i + 1 - parity, half)] = up_got[rows, :]
+    new_down[:, lanes_at(s[1] * half, half)] = fresh[...]
+    new_down[:, lanes_at((1 - s[1]) * half, half)] = fresh_got[...]
+    kept_up[...] = new_up[...]
+
+
+def renew(s, fresh, fresh_got, up, up_got):
+    half = fresh.shape[1]
+    return call(
+        renew_kernel, [((RANK, 2 * half), F32)] + [((RANK, VALUE_WIDTH), F32)] * 2,
+        s, [fresh, fresh_got, up, up_got], final=(0, 1),
+    )
+
+
+def score_kernel(s, refs, outs, scratch):
+    base, probs, new_up, *lows = refs
+    (out,) = outs
     low = sum(a[...] for a in lows).astype(BF16)
     u = low.shape[0]
     values = base[...] + adapter_scale_factor * dot_nn(low, new_up[...].astype(BF16))
@@ -472,17 +483,13 @@
         for j in range(GROUP):
             h = g * GROUP + j
             out[:, h * HEAD_DIM : (h + 1) * HEAD_DIM] = attended[j * u : (j + 1) * u, :]
-    new_down[:, lanes_at(s[1] * half, half)] = fresh[...]
-    new_down[:, lanes_at((1 - s[1]) * half, half)] = fresh_got[...]
-
-
-def score(s, base, probs, fresh, fresh_got, up, up_got, lows):
-    u, half = base.shape[0], fresh.shape[1]
-    return call(
-        score_kernel,
-        [((u, Q_HEADS * HEAD_DIM), BF16), ((RANK, 2 * half), F32), ((RANK, VALUE_WIDTH), F32)],
-        s, [base, probs, fresh, fresh_got, up, up_got, *lows], flops=2e8, final=(0, 1, 2),
-    )
+
+
+def score(s, base, probs, new_up, lows):
+    return call(
+        score_kernel, [((base.shape[0], Q_HEADS * HEAD_DIM), BF16)], s, [base, probs, new_up, *lows],
+        flops=2e8, final=(0,),
+    )[0]
 
 
 def reduce_order(n):
@@ -543,8 +550,8 @@
         seg_row, sseg_row = train_segments.reshape(1, -1), score_segments.reshape(1, -1)
         near_query, near_keys, near_target = near(query), near(keyset), near(target)
 
-        def head(g, deps):
-            return train_head(s, g, seg_row, near_query, near_keys, near_target, deps)
+        def head_pair(some):
+            return train_heads(s, some, seg_row, near_query, near_keys, near_target)
 
         def onward(array, ahead):
             return lax.ppermute(array, "fsdp", forward if ahead else backward)
@@ -556,7 +563,6 @@
         arrived, offsets = [a_piece, y_piece, c_piece], [0]
         a_ahead = a_back = a_piece
         c_ahead = c_back = c_piece
-        heads = [None] * KV_HEADS
         for k in range(1, steps):
             a_ahead, a_back = onward(a_ahead, True), onward(a_back, False)
             c_ahead, c_back = onward(c_ahead, True), onward(c_back, False)
@@ -564,12 +570,8 @@
                 xo, xso = fetch(s, n_fsdp, half, (x, xs))
                 xo, xso = swap(xo), swap(xso)
                 raw = tuple(near(a) for a in (x, xo, xs, xso))
-                touched = touch(s, (near_query, near_keys, near_target, seg_row))[0]
-                heads[0] = head(0, (touched,))
+                heads = head_pair((0, 1)) + head_pair((2, 3))
                 probs = score_probs(s, sseg_row, squery, skeyset, ())
-            elif k == 2:
-                heads[1] = head(1, ())
-                heads[2] = head(2, ())
             elif k == 3:
                 partial = project(s, n_fsdp, offsets, half, arrived, (), raw, False)
                 cut = len(offsets)
@@ -578,7 +580,6 @@
             offsets += [n_fsdp - k, k]
         a_last, c_last = onward(a_ahead, True), onward(c_back, False)
         last = [a_last, over_task(a_last), c_last]
-        heads[3] = head(3, ())
         sums, sums_out = project(s, n_fsdp, offsets[cut:], half, arrived[3 * cut :], partial, raw, True)
         sums_got = swap(sums_out)
         last += [swap(a) for a in last]
@@ -619,7 +620,8 @@
             (i * n_view + v, (i ^ 1) * n_view + (v ^ 1)) for i in range(n_fsdp) for v in range(n_view)
         ]
         lows = [low, exchange(near_by, 1), lax.ppermute(cross, ("fsdp", "view"), pairs), swap(other)]
-        scored, new_down, new_up = score(s, base, probs, fresh, fresh_got, up, up_got, lows)
+        new_down, new_up, kept_up = renew(s, fresh, fresh_got, up, up_got)
+        scored = score(s, base, probs, kept_up, lows)
         return (new_down.T, new_up, scored.reshape(score_query.shape))
 
     rows, rank_rows, tasks = P(("task", "view"), "fsdp", None), P(("task", "fsdp"), None), P("task", None)

time: 123 us -> 123 us (level)
  waiting for transfers between devices: 46.3 us -> 47.7 us
    ppermute x7, waiting for transfers between devices: 5.4 us -> 7.81 us  [over_task(): return lax.ppermute(array, 'task', [(i, i ^ 1) for i in range(n_task)])]
    ppermute x13, waiting for transfers between devices: 17.2 us -> 15.4 us  [exchange(): return lax.ppermute(array, 'fsdp', [(i, i ^ k) for i in range(n_fsdp)])]
    pallas_call x16 -> x14, Pallas kernels: 23.5 us -> 22.7 us  [call(): pl.pallas_call(whole, out_shape=[jax.ShapeDtypeStruct(*o) if i in final e...]
  transfers between devices with their start and end apart: 45 -> 45, of which waited for: 21 -> 19; matrix products, arithmetic and copies ran while one was open for 0% -> 0% of each run, Pallas kernels for 19% -> 17%
where the time goes in v3:
time: 123 us
  starting transfers between devices  47.7 us (39%)
  waiting for transfers between devices  47.7 us (39%)
  Pallas kernels  26.5 us (22%)
    ppermute x14, waiting for transfers between devices, onward(): return lax.ppermute(array, 'fsdp', forward if ahead else backward)  23.6 us
    pallas_call x14, Pallas kernels, call(): pl.pallas_call(whole, out_shape=[jax.ShapeDtypeStruct(*o) if i in final e...  22.7 us
    ppermute x13, starting transfers between devices, exchange(): return lax.ppermute(array, 'fsdp', [(i, i ^ k) for i in range(n_fsdp)])  18.9 us
    ppermute x14, starting transfers between devices, onward(): return lax.ppermute(array, 'fsdp', forward if ahead else backward)  16.9 us
    ppermute x13, waiting for transfers between devices, exchange(): return lax.ppermute(array, 'fsdp', [(i, i ^ k) for i in range(n_fsdp)])  15.4 us
    ppermute x7, starting transfers between devices, over_task(): return lax.ppermute(array, 'task', [(i, i ^ 1) for i in range(n_task)])  8.83 us
    ppermute x7, waiting for transfers between devices, over_task(): return lax.ppermute(array, 'task', [(i, i ^ 1) for i in range(n_task)])  7.81 us
    ppermute x10, starting transfers between devices, swap(): return lax.ppermute(array, 'view', [(i, i ^ 1) for i in range(n_view)])  3.15 us
  transfers between devices with their start and end apart: 45, of which 19 were waited for; matrix products, arithmetic and copies ran while one was open for 0% of the time, Pallas kernels for 17%

profile of v3, /device:TPU:0, one launch (start us, length us, event | category | flops | bytes accessed | tf_op | source)
XLA Modules:
  0.0 123.0 jit_solution(14067204454078709556)
XLA Ops:
  0.7 2.6 %shard_map.139 = (bf16[256,4096]{1,0:T(8,128)(2,1)S(1)}, bf16[64,4096]{1,0:T(8,128)(2,1)S(1)}) custom-call(s32[4]{0:T(128)S(1)} %pad_add_fusion.scalar_ref, bf16[256,8192]{1,0:T(8,128)(2,1)} %bitcast.16, bf16[64,8192]{1,0:T(8,128)(2,1)} %bitcast.22), custom_call_target="tpu_custom_call" | custom-call | flops 1000000 | bytes 2097152 | tf_op jit(solution)/shard_map/pallas_call | solution.py:229
  3.9 1.2 shard_map.140
  5.1 2.6 %collective-permute-start.15 = (bf16[256,512]{1,0:T(8,128)(2,1)S(1)}, bf16[256,512]{1,0:T(8,128)(2,1)S(1)}, u32[]{:S(2)}, u32[]{:S(2)}) collective-permute-start(bf16[256,512]{1,0:T(8,128)(2,1)S(1)} %get-tuple-element.47.refs_6_), channel_id=1, source_target_pairs={{0,4},{4,8},{8,12},{12,14},{14,10},{10,6},{6,2},{2,0},{1,5},{5,9},... | collective-permute-start | bytes 786440 | tf_op jit(solution)/shard_map/ppermute | solution.py:557
  7.8 1.6 %collective-permute-start.1 = (bf16[160,512]{1,0:T(8,128)(2,1)S(1)}, bf16[160,512]{1,0:T(8,128)(2,1)S(1)}, u32[]{:S(2)}, u32[]{:S(2)}) collective-permute-start(bf16[160,512]{1,0:T(8,128)(2,1)S(1)} %get-tuple-element.46.refs_4_), channel_id=1, source_target_pairs={{0,4},{4,8},{8,12},{12,14},{14,10},{10,6},{6,2},{2,0},{1,5},{5,9},... | collective-permute-start | bytes 491528 | tf_op jit(solution)/shard_map/ppermute | solution.py:557
  9.8 8.3 %collective-permute-done.1.refs_7_ = bf16[160,512]{1,0:T(8,128)(2,1)S(1)} collective-permute-done((bf16[160,512]{1,0:T(8,128)(2,1)S(1)}, bf16[160,512]{1,0:T(8,128)(2,1)S(1)}, u32[]{:S(2)}, u32[]{:S(2)}) %collective-permute-start.1) | collective-permute-done | bytes 163872 | tf_op jit(solution)/shard_map/ppermute | solution.py:557
  18.1 1.8 %collective-permute-start.2 = (bf16[160,512]{1,0:T(8,128)(2,1)S(1)}, bf16[160,512]{1,0:T(8,128)(2,1)S(1)}, u32[]{:S(2)}, u32[]{:S(2)}) collective-permute-start(bf16[160,512]{1,0:T(8,128)(2,1)S(1)} %collective-permute-done.1.refs_7_), channel_id=1, source_target_pairs={{0,4},{4,8},{8,12},{12,14},{14,10},{10,6},{6,2},{2,0},{1,5},{5,9},... | collective-permute-start | bytes 491528 | tf_op jit(solution)/shard_map/ppermute | solution.py:557
  20.2 1.8 %collective-permute-start.22 = (bf16[160,512]{1,0:T(8,128)(2,1)S(1)}, bf16[160,512]{1,0:T(8,128)(2,1)S(1)}, u32[]{:S(2)}, u32[]{:S(2)}) collective-permute-start(bf16[160,512]{1,0:T(8,128)(2,1)S(1)} %collective-permute-done.1.refs_7_), channel_id=1, source_target_pairs={{0,16},{16,0},{1,17},{17,1},{2,18},{18,2},{3,19},{19,3},{4,20},{20... | collective-permute-start | bytes 491528 | tf_op jit(solution)/shard_map/ppermute | solution.py:560
  21.9 2.2 %collective-permute-done.2.refs_13_ = bf16[160,512]{1,0:T(8,128)(2,1)S(1)} collective-permute-done((bf16[160,512]{1,0:T(8,128)(2,1)S(1)}, bf16[160,512]{1,0:T(8,128)(2,1)S(1)}, u32[]{:S(2)}, u32[]{:S(2)}) %collective-permute-start.2) | collective-permute-done | bytes 163872 | tf_op jit(solution)/shard_map/ppermute | solution.py:557
  24.1 1.5 %collective-permute-start.23 = (bf16[160,512]{1,0:T(8,128)(2,1)S(1)}, bf16[160,512]{1,0:T(8,128)(2,1)S(1)}, u32[]{:S(2)}, u32[]{:S(2)}) collective-permute-start(bf16[160,512]{1,0:T(8,128)(2,1)S(1)} %collective-permute-done.18.refs_10_), channel_id=1, source_target_pairs={{0,16},{16,0},{1,17},{17,1},{2,18},{18,2},{3,19},{19,3},{4,20},{20... | collective-permute-start | bytes 491528 | tf_op jit(solution)/shard_map/ppermute | solution.py:560
  25.6 1.3 %collective-permute-start.24 = (bf16[160,512]{1,0:T(8,128)(2,1)S(1)}, bf16[160,512]{1,0:T(8,128)(2,1)S(1)}, u32[]{:S(2)}, u32[]{:S(2)}) collective-permute-start(bf16[160,512]{1,0:T(8,128)(2,1)S(1)} %collective-permute-done.2.refs_13_), channel_id=1, source_target_pairs={{0,16},{16,0},{1,17},{17,1},{2,18},{18,2},{3,19},{19,3},{4,20},{20... | collective-permute-start | bytes 491528 | tf_op jit(solution)/shard_map/ppermute | solution.py:560
  27.7 3.5 %collective-permute-done.23.refs_11_ = bf16[160,512]{1,0:T(8,128)(2,1)S(1)} collective-permute-done((bf16[160,512]{1,0:T(8,128)(2,1)S(1)}, bf16[160,512]{1,0:T(8,128)(2,1)S(1)}, u32[]{:S(2)}, u32[]{:S(2)}) %collective-permute-start.23) | collective-permute-done | bytes 163872 | tf_op jit(solution)/shard_map/ppermute | solution.py:560
  31.2 1.5 %collective-permute-start.7 = (bf16[256,512]{1,0:T(8,128)(2,1)S(1)}, bf16[256,512]{1,0:T(8,128)(2,1)S(1)}, u32[]{:S(2)}, u32[]{:S(2)}) collective-permute-start(bf16[256,512]{1,0:T(8,128)(2,1)S(1)} %collective-permute-done.6.refs_12_), channel_id=1, source_target_pairs={{4,0},{8,4},{12,8},{14,12},{10,14},{6,10},{2,6},{0,2},{5,1},{9,5},... | collective-permute-start | bytes 786440 | tf_op jit(solution)/shard_map/ppermute | solution.py:557
  32.7 1.9 %collective-permute-done.24.refs_14_ = bf16[160,512]{1,0:T(8,128)(2,1)S(1)} collective-permute-done((bf16[160,512]{1,0:T(8,128)(2,1)S(1)}, bf16[160,512]{1,0:T(8,128)(2,1)S(1)}, u32[]{:S(2)}, u32[]{:S(2)}) %collective-permute-start.24) | collective-permute-done | bytes 163872 | tf_op jit(solution)/shard_map/ppermute | solution.py:560
  34.5 1.5 %collective-permute-start.16 = (bf16[256,512]{1,0:T(8,128)(2,1)S(1)}, bf16[256,512]{1,0:T(8,128)(2,1)S(1)}, u32[]{:S(2)}, u32[]{:S(2)}) collective-permute-start(bf16[256,512]{1,0:T(8,128)(2,1)S(1)} %collective-permute-done.15.refs_9_), channel_id=1, source_target_pairs={{0,4},{4,8},{8,12},{12,14},{14,10},{10,6},{6,2},{2,0},{1,5},{5,9},... | collective-permute-start | bytes 786440 | tf_op jit(solution)/shard_map/ppermute | solution.py:557
  36.3 1.5 %collective-permute-start.3 = (bf16[160,512]{1,0:T(8,128)(2,1)S(1)}, bf16[160,512]{1,0:T(8,128)(2,1)S(1)}, u32[]{:S(2)}, u32[]{:S(2)}) collective-permute-start(bf16[160,512]{1,0:T(8,128)(2,1)S(1)} %collective-permute-done.2.refs_13_), channel_id=1, source_target_pairs={{0,4},{4,8},{8,12},{12,14},{14,10},{10,6},{6,2},{2,0},{1,5},{5,9},... | collective-permute-start | bytes 491528 | tf_op jit(solution)/shard_map/ppermute | solution.py:557
  37.8 5.6 %collective-permute-done.3.refs_4_ = bf16[160,512]{1,0:T(8,128)(2,1)S(1)} collective-permute-done((bf16[160,512]{1,0:T(8,128)(2,1)S(1)}, bf16[160,512]{1,0:T(8,128)(2,1)S(1)}, u32[]{:S(2)}, u32[]{:S(2)}) %collective-permute-start.3) | collective-permute-done | bytes 163872 | tf_op jit(solution)/shard_map/ppermute | solution.py:557
  43.4 1.5 %collective-permute-start.20 = (bf16[160,512]{1,0:T(8,128)(2,1)S(1)}, bf16[160,512]{1,0:T(8,128)(2,1)S(1)}, u32[]{:S(2)}, u32[]{:S(2)}) collective-permute-start(bf16[160,512]{1,0:T(8,128)(2,1)S(1)} %collective-permute-done.19.refs_16_), channel_id=1, source_target_pairs={{4,0},{8,4},{12,8},{14,12},{10,14},{6,10},{2,6},{0,2},{5,1},{9,5},... | collective-permute-start | bytes 491528 | tf_op jit(solution)/shard_map/ppermute | solution.py:557
  44.9 1.6 %collective-permute-start.8 = (bf16[256,512]{1,0:T(8,128)(2,1)S(1)}, bf16[256,512]{1,0:T(8,128)(2,1)S(1)}, u32[]{:S(2)}, u32[]{:S(2)}) collective-permute-start(bf16[256,512]{1,0:T(8,128)(2,1)S(1)} %collective-permute-done.7.refs_18_), channel_id=1, source_target_pairs={{4,0},{8,4},{12,8},{14,12},{10,14},{6,10},{2,6},{0,2},{5,1},{9,5},... | collective-permute-start | bytes 786440 | tf_op jit(solution)/shard_map/ppermute | solution.py:557
  46.9 1.8 %collective-permute-done.20.refs_7_ = bf16[160,512]{1,0:T(8,128)(2,1)S(1)} collective-permute-done((bf16[160,512]{1,0:T(8,128)(2,1)S(1)}, bf16[160,512]{1,0:T(8,128)(2,1)S(1)}, u32[]{:S(2)}, u32[]{:S(2)}) %collective-permute-start.20) | collective-permute-done | bytes 163872 | tf_op jit(solution)/shard_map/ppermute | solution.py:557
  48.7 1.5 %collective-permute-start.14 = (bf16[160,512]{1,0:T(8,128)(2,1)S(1)}, bf16[160,512]{1,0:T(8,128)(2,1)S(1)}, u32[]{:S(2)}, u32[]{:S(2)}) collective-permute-start(bf16[160,512]{1,0:T(8,128)(2,1)S(1)} %collective-permute-done.3.refs_4_), channel_id=1, source_target_pairs={{0,16},{16,0},{1,17},{17,1},{2,18},{18,2},{3,19},{19,3},{4,20},{20... | collective-permute-start | bytes 491528 | tf_op jit(solution)/shard_map/ppermute | solution.py:560
  50.8 3.3 %shard_map.141 = (f32[640,512]{1,0:T(8,128)S(1)}, f32[64,512]{1,0:T(8,128)S(1)}) custom-call(s32[4]{0:T(128)S(1)} %pad_add_fusion.scalar_ref, bf16[256,8192]{1,0:T(8,128)(2,1)S(1)} %bitcast.17, bf16[256,4096]{1,0:T(8,128)(2,1)S(1)} %collective-permute-done.refs_1_, bf16[64,8192]{1,0:T(8,128)(2,1)S(1)} %bitcast.23, ...), custom_call_target="tpu_custom_call" | custom-call | flops 1700000000 | bytes 1048576 | tf_op jit(solution)/shard_map/pallas_call | solution.py:59
  54.1 1.7 %collective-permute-done.21.refs_8_ = bf16[160,512]{1,0:T(8,128)(2,1)S(1)} collective-permute-done((bf16[160,512]{1,0:T(8,128)(2,1)S(1)}, bf16[160,512]{1,0:T(8,128)(2,1)S(1)}, u32[]{:S(2)}, u32[]{:S(2)}) %collective-permute-start.21) | collective-permute-done | bytes 163872 | tf_op jit(solution)/shard_map/ppermute | solution.py:560
  55.8 1.7 %shard_map.142 = (f32[352,512]{1,0:T(8,128)S(1)}, f32[352,512]{1,0:T(8,128)S(1)}) custom-call(s32[4]{0:T(128)S(1)} %pad_add_fusion.scalar_ref, bf16[256,8192]{1,0:T(8,128)(2,1)S(1)} %bitcast.18, bf16[256,4096]{1,0:T(8,128)(2,1)S(1)} %collective-permute-done.refs_1_, bf16[64,8192]{1,0:T(8,128)(2,1)S(1)} %bitcast.24, ...), custom_call_target="tpu_custom_call" | custom-call | flops 680000000 | bytes 1048576 | tf_op jit(solution)/shard_map/pallas_call | solution.py:59
  57.6 1.5 %collective-permute-start.9 = (bf16[256,512]{1,0:T(8,128)(2,1)S(1)}, bf16[256,512]{1,0:T(8,128)(2,1)S(1)}, u32[]{:S(2)}, u32[]{:S(2)}) collective-permute-start(bf16[256,512]{1,0:T(8,128)(2,1)S(1)} %collective-permute-done.8.refs_9_), channel_id=1, source_target_pairs={{4,0},{8,4},{12,8},{14,12},{10,14},{6,10},{2,6},{0,2},{5,1},{9,5},... | collective-permute-start | bytes 786440 | tf_op jit(solution)/shard_map/ppermute | solution.py:557
  59.8 5.6 %collective-permute-done.4.refs_2_ = bf16[160,512]{1,0:T(8,128)(2,1)S(1)} collective-permute-done((bf16[160,512]{1,0:T(8,128)(2,1)S(1)}, bf16[160,512]{1,0:T(8,128)(2,1)S(1)}, u32[]{:S(2)}, u32[]{:S(2)}) %collective-permute-start.4) | collective-permute-done | bytes 163872 | tf_op jit(solution)/shard_map/ppermute | solution.py:557
  65.4 1.5 %collective-permute-start.5 = (bf16[160,512]{1,0:T(8,128)(2,1)S(1)}, bf16[160,512]{1,0:T(8,128)(2,1)S(1)}, u32[]{:S(2)}, u32[]{:S(2)}) collective-permute-start(bf16[160,512]{1,0:T(8,128)(2,1)S(1)} %collective-permute-done.4.refs_2_), channel_id=1, source_target_pairs={{0,16},{16,0},{1,17},{17,1},{2,18},{18,2},{3,19},{19,3},{4,20},{20... | collective-permute-start | bytes 491528 | tf_op jit(solution)/shard_map/ppermute | solution.py:560
  67.0 2.8 %shard_map.143 = (bf16[256,256]{1,0:T(8,128)(2,1)S(1)}, bf16[256,256]{1,0:T(8,128)(2,1)S(1)}, f32[256,128]{1,0:T(8,128)S(1)}, bf16[256,256]{1,0:T(8,128)(2,1)S(1...) custom-call(s32[4]{0:T(128)S(1)} %pad_add_fusion.scalar_ref, s32[1,256]{1,0:T(1,128)S(1)} %bitcast.38, ...), custom_call_target="tpu_custom_call" | custom-call | flops 2000000000 | bytes 1048576 | tf_op jit(solution)/shard_map/pallas_call | solution.py:59
  70.8 2.8 %shard_map.144 = (bf16[256,256]{1,0:T(8,128)(2,1)S(1)}, bf16[256,256]{1,0:T(8,128)(2,1)S(1)}, f32[256,128]{1,0:T(8,128)S(1)}, bf16[256,256]{1,0:T(8,128)(2,1)S(1...) custom-call(s32[4]{0:T(128)S(1)} %pad_add_fusion.scalar_ref, s32[1,256]{1,0:T(1,128)S(1)} %bitcast.39, ...), custom_call_target="tpu_custom_call" | custom-call | flops 2000000000 | bytes 1048576 | tf_op jit(solution)/shard_map/pallas_call | solution.py:59
  74.3 1.6 %collective-permute-start.41 = (bf16[128,2048]{1,0:T(8,128)(2,1)S(1)}, bf16[128,2048]{1,0:T(8,128)(2,1)S(1)}, u32[]{:S(2)}, u32[]{:S(2)}) collective-permute-start(bf16[128,2048]{1,0:T(8,128)(2,1)S(1)} %shard_map.152), channel_id=1, source_target_pairs={{0,2},{2,0},{4,6},{6,4},{8,10},{10,8},{12,14},{14,12},{1,3},{3,1},... | collective-permute-start | bytes 1572872 | tf_op jit(solution)/shard_map/ppermute | solution.py:519
  76.0 2.4 %shard_map.145 = (f32[64,512]{1,0:T(8,128)S(1)}, bf16[64,256]{1,0:T(8,128)(2,1)S(1)}, f32[64,512]{1,0:T(8,128)S(1)}) custom-call(s32[4]{0:T(128)S(1)} %pad_add_fusion.scalar_ref, bf16[256,8192]{1,0:T(8,128)(2,1)S(1)} %bitcast.19, bf16[64,8192]{1,0:T(8,128)(2,1)S(1)} %bitcast.26, bf16[160,512]{1,0:T(8,128)(2,1)S(1)} %collective-permute-done.4.refs_2_, ...), custom_call_target="tpu_custom_call" | custom-call | flops 1000000000 | bytes 1048576 | tf_op jit(solution)/shard_map/pallas_call | solution.py:59
  79.9 1.0 shard_map.147
  80.9 3.4 %collective-permute-start.32 = (bf16[72,512]{1,0:T(8,128)(2,1)S(1)}, bf16[72,512]{1,0:T(8,128)(2,1)S(1)}, u32[]{:S(2)}, u32[]{:S(2)}) collective-permute-start(bf16[72,512]{1,0:T(8,128)(2,1)S(1)} %get-tuple-element.73), channel_id=1, source_target_pairs={{0,8},{2,10},{4,12},{6,14},{8,0},{10,2},{12,4},{14,6},{1,9},{3,11}... | collective-permute-start | bytes 221192 | tf_op jit(solution)/shard_map/ppermute | solution.py:519
  84.2 2.9 %collective-permute-start.34 = (bf16[72,512]{1,0:T(8,128)(2,1)S(1)}, bf16[72,512]{1,0:T(8,128)(2,1)S(1)}, u32[]{:S(2)}, u32[]{:S(2)}) collective-permute-start(bf16[72,512]{1,0:T(8,128)(2,1)S(1)} %get-tuple-element.75), channel_id=1, source_target_pairs={{0,12},{2,14},{4,8},{6,10},{8,4},{10,6},{12,0},{14,2},{1,13},{3,15... | collective-permute-start | bytes 221192 | tf_op jit(solution)/shard_map/ppermute | solution.py:519
  87.1 1.9 %collective-permute-start.35 = (bf16[72,512]{1,0:T(8,128)(2,1)S(1)}, bf16[72,512]{1,0:T(8,128)(2,1)S(1)}, u32[]{:S(2)}, u32[]{:S(2)}) collective-permute-start(bf16[72,512]{1,0:T(8,128)(2,1)S(1)} %get-tuple-element.76), channel_id=1, source_target_pairs={{0,14},{2,12},{4,10},{6,8},{8,6},{10,4},{12,2},{14,0},{1,15},{3,13... | collective-permute-start | bytes 221192 | tf_op jit(solution)/shard_map/ppermute | solution.py:519
  90.1 1.9 %collective-permute-done.32.refs_7_ = bf16[72,512]{1,0:T(8,128)(2,1)S(1)} collective-permute-done((bf16[72,512]{1,0:T(8,128)(2,1)S(1)}, bf16[72,512]{1,0:T(8,128)(2,1)S(1)}, u32[]{:S(2)}, u32[]{:S(2)}) %collective-permute-start.32) | collective-permute-done | bytes 73760 | tf_op jit(solution)/shard_map/ppermute | solution.py:519
  92.0 3.1 %collective-permute-done.33.refs_8_ = bf16[72,512]{1,0:T(8,128)(2,1)S(1)} collective-permute-done((bf16[72,512]{1,0:T(8,128)(2,1)S(1)}, bf16[72,512]{1,0:T(8,128)(2,1)S(1)}, u32[]{:S(2)}, u32[]{:S(2)}) %collective-permute-start.33) | collective-permute-done | bytes 73760 | tf_op jit(solution)/shard_map/ppermute | solution.py:519
  95.4 2.7 %collective-permute-start.31 = (bf16[72,512]{1,0:T(8,128)(2,1)S(1)}, bf16[72,512]{1,0:T(8,128)(2,1)S(1)}, u32[]{:S(2)}, u32[]{:S(2)}) collective-permute-start(bf16[72,512]{1,0:T(8,128)(2,1)S(1)} %get-tuple-element.72), channel_id=1, source_target_pairs={{0,6},{2,4},{4,2},{6,0},{8,14},{10,12},{12,10},{14,8},{1,7},{3,5},... | collective-permute-start | bytes 221192 | tf_op jit(solution)/shard_map/ppermute | solution.py:519
  98.1 1.8 %collective-permute-done.30.refs_5_ = bf16[72,512]{1,0:T(8,128)(2,1)S(1)} collective-permute-done((bf16[72,512]{1,0:T(8,128)(2,1)S(1)}, bf16[72,512]{1,0:T(8,128)(2,1)S(1)}, u32[]{:S(2)}, u32[]{:S(2)}) %collective-permute-start.30) | collective-permute-done | bytes 73760 | tf_op jit(solution)/shard_map/ppermute | solution.py:519
  99.9 1.4 %collective-permute-done.31.refs_6_ = bf16[72,512]{1,0:T(8,128)(2,1)S(1)} collective-permute-done((bf16[72,512]{1,0:T(8,128)(2,1)S(1)}, bf16[72,512]{1,0:T(8,128)(2,1)S(1)}, u32[]{:S(2)}, u32[]{:S(2)}) %collective-permute-start.31) | collective-permute-done | bytes 73760 | tf_op jit(solution)/shard_map/ppermute | solution.py:519
  102.0 1.3 %collective-permute-start.37 = (bf16[80,512]{1,0:T(8,128)(2,1)S(1)}, bf16[80,512]{1,0:T(8,128)(2,1)S(1)}, u32[]{:S(2)}, u32[]{:S(2)}) collective-permute-start(bf16[80,512]{1,0:T(8,128)(2,1)S(1)} %get-tuple-element.78.refs_0_.refs_3_), channel_id=1, source_target_pairs={{0,4},{2,6},{4,0},{6,2},{8,12},{10,14},{12,8},{14,10},{1,5},{3,7},... | collective-permute-start | bytes 245768 | tf_op jit(solution)/shard_map/ppermute | solution.py:519
  103.3 2.2 %collective-permute-start.38 = (bf16[80,512]{1,0:T(8,128)(2,1)S(1)}, bf16[80,512]{1,0:T(8,128)(2,1)S(1)}, u32[]{:S(2)}, u32[]{:S(2)}) collective-permute-start(bf16[80,512]{1,0:T(8,128)(2,1)S(1)} %get-tuple-element.78.refs_0_.refs_3_), channel_id=1, source_target_pairs={{0,8},{2,10},{4,12},{6,14},{8,0},{10,2},{12,4},{14,6},{1,9},{3,11}... | collective-permute-start | bytes 245768 | tf_op jit(solution)/shard_map/ppermute | solution.py:519
  106.7 3.9 %collective-permute-done.38.refs_2_.refs_5_ = bf16[80,512]{1,0:T(8,128)(2,1)S(1)} collective-permute-done((bf16[80,512]{1,0:T(8,128)(2,1)S(1)}, bf16[80,512]{1,0:T(8,128)(2,1)S(1)}, u32[]{:S(2)}, u32[]{:S(2)}) %collective-permute-start.38) | collective-permute-done | bytes 81952 | tf_op jit(solution)/shard_map/ppermute | solution.py:519
  110.6 1.2 %collective-permute-done.39.refs_3_.refs_6_ = bf16[80,512]{1,0:T(8,128)(2,1)S(1)} collective-permute-done((bf16[80,512]{1,0:T(8,128)(2,1)S(1)}, bf16[80,512]{1,0:T(8,128)(2,1)S(1)}, u32[]{:S(2)}, u32[]{:S(2)}) %collective-permute-start.39) | collective-permute-done | bytes 81952 | tf_op jit(solution)/shard_map/ppermute | solution.py:519
  113.6 1.4 %collective-permute-start.44 = (f32[64,64]{1,0:T(8,128)S(1)}, f32[64,64]{1,0:T(8,128)S(1)}, u32[]{:S(2)}, u32[]{:S(2)}) collective-permute-start(f32[64,64]{1,0:T(8,128)S(1)} %get-tuple-element.86), channel_id=1, source_target_pairs={{0,1},{1,0},{2,3},{3,2},{4,5},{5,4},{6,7},{7,6},{8,9},{9,8},{10,11... | collective-permute-start | bytes 49160 | tf_op jit(solution)/shard_map/ppermute | solution.py:516
  116.4 1.7 %shard_map.151.refs_1_ = bf16[4,512,64]{2,1,0:T(8,128)(2,1)S(1)} custom-call(s32[4]{0:T(128)S(1)} %pad_add_fusion.scalar_ref, s32[1,64]{1,0:T(1,128)S(1)} %bitcast.40, bf16[64,4096]{1,0:T(8,128)(2,1)S(1)} %bitcast.34, bf16[64,512]{1,0:T(8,128)(2,1)S(1)} %bitcast.37), custom_call_target="tpu_custom_call" | custom-call | flops 1000000000 | bytes 1048576 | tf_op jit(solution)/shard_map/pallas_call | solution.py:59
  118.2 1.7 %collective-permute-done.40.refs_3_ = f32[32,512]{1,0:T(8,128)S(1)} collective-permute-done((f32[32,512]{1,0:T(8,128)S(1)}, f32[32,512]{1,0:T(8,128)S(1)}, u32[]{:S(2)}, u32[]{:S(2)}) %collective-permute-start.40) | collective-permute-done | bytes 65568 | tf_op jit(solution)/shard_map/ppermute | solution.py:519
  119.9 1.3 %shard_map.150 = (f32[64,1024]{1,0:T(8,128)}, f32[64,512]{1,0:T(8,128)}, f32[64,512]{1,0:T(8,128)S(1)}) custom-call(s32[4]{0:T(128)S(1)} %pad_add_fusion.scalar_ref, f32[64,512]{1,0:T(8,128)S(1)} %get-tuple-element.77.refs_0_, f32[64,512]{1,0:T(8,128)S(1)} %collective-permute-done.36.refs_1_, f32[32,512]{1,0:T(8,128)S(1)} %shard_map.149.refs_2_, ...), custom_call_target="tpu_custom_call" | custom-call | flops 1000000 | bytes 1048576 | tf_op jit(solution)/shard_map/pallas_call | solution.py:59
  121.2 1.8 %shard_map.154 = bf16[64,4096]{1,0:T(8,128)(2,1)} custom-call(s32[4]{0:T(128)S(1)} %pad_add_fusion.scalar_ref, f32[64,512]{1,0:T(8,128)S(1)} %get-tuple-element.81.refs_0_, bf16[4,512,64]{2,1,0:T(8,128)(2,1)S(1)} %shard_map.151.refs_1_, f32[64,512]{1,0:T(8,128)S(1)} %get-tuple-element.82.refs_2_, f32[64,64]{1,0:T(8,128)S(1)} %get-tuple-element.83.refs_3_, ...), custom_call_target="tpu_custom_call" | custom-call | flops 200000000 | bytes 1048576 | tf_op jit(solution)/shard_map/pallas_call | solution.py:59
  (81 shorter events, 13.4 us)
Async XLA Ops:
  0.7 50.0 %copy-start = (bf16[1,256,8192]{2,1,0:T(8,128)(2,1)S(1)}, bf16[1,256,8192]{2,1,0:T(8,128)(2,1)}, u32[]{:S(2)}) copy-start(bf16[1,256,8192]{2,1,0:T(8,128)(2,1)} %param.12) | copy-start | bytes 12582916
  0.7 50.0 %copy-start.1 = (bf16[1,64,8192]{2,1,0:T(8,128)(2,1)S(1)}, bf16[1,64,8192]{2,1,0:T(8,128)(2,1)}, u32[]{:S(2)}) copy-start(bf16[1,64,8192]{2,1,0:T(8,128)(2,1)} %param.20) | copy-start | bytes 3145732
  3.3 47.4 %collective-permute-start = (bf16[256,4096]{1,0:T(8,128)(2,1)S(1)}, bf16[256,4096]{1,0:T(8,128)(2,1)S(1)}, u32[]{:S(2)}, u32[]{:S(2)}) collective-permute-start(bf16[256,4096]{1,0:T(8,128)(2,1)S(1)} %get-tuple-element.45), channel_id=1, source_target_pairs={{0,1},{1,0},{2,3},{3,2},{4,5},{5,4},{6,7},{7,6},{8,9},{9,8},{10,11... | collective-permute-start | bytes 6291464 | tf_op jit(solution)/shard_map/ppermute | solution.py:516
  5.1 15.1 %collective-permute-start.15 = (bf16[256,512]{1,0:T(8,128)(2,1)S(1)}, bf16[256,512]{1,0:T(8,128)(2,1)S(1)}, u32[]{:S(2)}, u32[]{:S(2)}) collective-permute-start(bf16[256,512]{1,0:T(8,128)(2,1)S(1)} %get-tuple-element.47.refs_6_), channel_id=1, source_target_pairs={{0,4},{4,8},{8,12},{12,14},{14,10},{10,6},{6,2},{2,0},{1,5},{5,9},... | collective-permute-start | bytes 786440 | tf_op jit(solution)/shard_map/ppermute | solution.py:557
  7.8 10.4 %collective-permute-start.1 = (bf16[160,512]{1,0:T(8,128)(2,1)S(1)}, bf16[160,512]{1,0:T(8,128)(2,1)S(1)}, u32[]{:S(2)}, u32[]{:S(2)}) collective-permute-start(bf16[160,512]{1,0:T(8,128)(2,1)S(1)} %get-tuple-element.46.refs_4_), channel_id=1, source_target_pairs={{0,4},{4,8},{8,12},{12,14},{14,10},{10,6},{6,2},{2,0},{1,5},{5,9},... | collective-permute-start | bytes 491528 | tf_op jit(solution)/shard_map/ppermute | solution.py:557
  9.3 10.6 %collective-permute-start.18 = (bf16[160,512]{1,0:T(8,128)(2,1)S(1)}, bf16[160,512]{1,0:T(8,128)(2,1)S(1)}, u32[]{:S(2)}, u32[]{:S(2)}) collective-permute-start(bf16[160,512]{1,0:T(8,128)(2,1)S(1)} %get-tuple-element.46.refs_4_), channel_id=1, source_target_pairs={{4,0},{8,4},{12,8},{14,12},{10,14},{6,10},{2,6},{0,2},{5,1},{9,5},... | collective-permute-start | bytes 491528 | tf_op jit(solution)/shard_map/ppermute | solution.py:557
  9.8 12.2 %collective-permute-start.6 = (bf16[256,512]{1,0:T(8,128)(2,1)S(1)}, bf16[256,512]{1,0:T(8,128)(2,1)S(1)}, u32[]{:S(2)}, u32[]{:S(2)}) collective-permute-start(bf16[256,512]{1,0:T(8,128)(2,1)S(1)} %get-tuple-element.47.refs_6_), channel_id=1, source_target_pairs={{4,0},{8,4},{12,8},{14,12},{10,14},{6,10},{2,6},{0,2},{5,1},{9,5},... | collective-permute-start | bytes 786440 | tf_op jit(solution)/shard_map/ppermute | solution.py:557
  18.1 6.0 %collective-permute-start.2 = (bf16[160,512]{1,0:T(8,128)(2,1)S(1)}, bf16[160,512]{1,0:T(8,128)(2,1)S(1)}, u32[]{:S(2)}, u32[]{:S(2)}) collective-permute-start(bf16[160,512]{1,0:T(8,128)(2,1)S(1)} %collective-permute-done.1.refs_7_), channel_id=1, source_target_pairs={{0,4},{4,8},{8,12},{12,14},{14,10},{10,6},{6,2},{2,0},{1,5},{5,9},... | collective-permute-start | bytes 491528 | tf_op jit(solution)/shard_map/ppermute | solution.py:557
  20.0 5.7 %collective-permute-start.19 = (bf16[160,512]{1,0:T(8,128)(2,1)S(1)}, bf16[160,512]{1,0:T(8,128)(2,1)S(1)}, u32[]{:S(2)}, u32[]{:S(2)}) collective-permute-start(bf16[160,512]{1,0:T(8,128)(2,1)S(1)} %collective-permute-done.18.refs_10_), channel_id=1, source_target_pairs={{4,0},{8,4},{12,8},{14,12},{10,14},{6,10},{2,6},{0,2},{5,1},{9,5},... | collective-permute-start | bytes 491528 | tf_op jit(solution)/shard_map/ppermute | solution.py:557
  20.2 6.8 %collective-permute-start.22 = (bf16[160,512]{1,0:T(8,128)(2,1)S(1)}, bf16[160,512]{1,0:T(8,128)(2,1)S(1)}, u32[]{:S(2)}, u32[]{:S(2)}) collective-permute-start(bf16[160,512]{1,0:T(8,128)(2,1)S(1)} %collective-permute-done.1.refs_7_), channel_id=1, source_target_pairs={{0,16},{16,0},{1,17},{17,1},{2,18},{18,2},{3,19},{19,3},{4,20},{20... | collective-permute-start | bytes 491528 | tf_op jit(solution)/shard_map/ppermute | solution.py:560
  21.9 28.3 %collective-permute-start.13 = (bf16[64,4096]{1,0:T(8,128)(2,1)S(1)}, bf16[64,4096]{1,0:T(8,128)(2,1)S(1)}, u32[]{:S(2)}, u32[]{:S(2)}) collective-permute-start(bf16[64,4096]{1,0:T(8,128)(2,1)S(1)} %get-tuple-element.48), channel_id=1, source_target_pairs={{0,1},{1,0},{2,3},{3,2},{4,5},{5,4},{6,7},{7,6},{8,9},{9,8},{10,11... | collective-permute-start | bytes 1572872 | tf_op jit(solution)/shard_map/ppermute | solution.py:516
  24.1 7.1 %collective-permute-start.23 = (bf16[160,512]{1,0:T(8,128)(2,1)S(1)}, bf16[160,512]{1,0:T(8,128)(2,1)S(1)}, u32[]{:S(2)}, u32[]{:S(2)}) collective-permute-start(bf16[160,512]{1,0:T(8,128)(2,1)S(1)} %collective-permute-done.18.refs_10_), channel_id=1, source_target_pairs={{0,16},{16,0},{1,17},{17,1},{2,18},{18,2},{3,19},{19,3},{4,20},{20... | collective-permute-start | bytes 491528 | tf_op jit(solution)/shard_map/ppermute | solution.py:560
  25.6 8.9 %collective-permute-start.24 = (bf16[160,512]{1,0:T(8,128)(2,1)S(1)}, bf16[160,512]{1,0:T(8,128)(2,1)S(1)}, u32[]{:S(2)}, u32[]{:S(2)}) collective-permute-start(bf16[160,512]{1,0:T(8,128)(2,1)S(1)} %collective-permute-done.2.refs_13_), channel_id=1, source_target_pairs={{0,16},{16,0},{1,17},{17,1},{2,18},{18,2},{3,19},{19,3},{4,20},{20... | collective-permute-start | bytes 491528 | tf_op jit(solution)/shard_map/ppermute | solution.py:560
  26.9 9.4 %collective-permute-start.25 = (bf16[160,512]{1,0:T(8,128)(2,1)S(1)}, bf16[160,512]{1,0:T(8,128)(2,1)S(1)}, u32[]{:S(2)}, u32[]{:S(2)}) collective-permute-start(bf16[160,512]{1,0:T(8,128)(2,1)S(1)} %collective-permute-done.19.refs_16_), channel_id=1, source_target_pairs={{0,16},{16,0},{1,17},{17,1},{2,18},{18,2},{3,19},{19,3},{4,20},{20... | collective-permute-start | bytes 491528 | tf_op jit(solution)/shard_map/ppermute | solution.py:560
  31.2 13.7 %collective-permute-start.7 = (bf16[256,512]{1,0:T(8,128)(2,1)S(1)}, bf16[256,512]{1,0:T(8,128)(2,1)S(1)}, u32[]{:S(2)}, u32[]{:S(2)}) collective-permute-start(bf16[256,512]{1,0:T(8,128)(2,1)S(1)} %collective-permute-done.6.refs_12_), channel_id=1, source_target_pairs={{4,0},{8,4},{12,8},{14,12},{10,14},{6,10},{2,6},{0,2},{5,1},{9,5},... | collective-permute-start | bytes 786440 | tf_op jit(solution)/shard_map/ppermute | solution.py:557
  34.5 11.9 %collective-permute-start.16 = (bf16[256,512]{1,0:T(8,128)(2,1)S(1)}, bf16[256,512]{1,0:T(8,128)(2,1)S(1)}, u32[]{:S(2)}, u32[]{:S(2)}) collective-permute-start(bf16[256,512]{1,0:T(8,128)(2,1)S(1)} %collective-permute-done.15.refs_9_), channel_id=1, source_target_pairs={{0,4},{4,8},{8,12},{12,14},{14,10},{10,6},{6,2},{2,0},{1,5},{5,9},... | collective-permute-start | bytes 786440 | tf_op jit(solution)/shard_map/ppermute | solution.py:557
  36.3 7.1 %collective-permute-start.3 = (bf16[160,512]{1,0:T(8,128)(2,1)S(1)}, bf16[160,512]{1,0:T(8,128)(2,1)S(1)}, u32[]{:S(2)}, u32[]{:S(2)}) collective-permute-start(bf16[160,512]{1,0:T(8,128)(2,1)S(1)} %collective-permute-done.2.refs_13_), channel_id=1, source_target_pairs={{0,4},{4,8},{8,12},{12,14},{14,10},{10,6},{6,2},{2,0},{1,5},{5,9},... | collective-permute-start | bytes 491528 | tf_op jit(solution)/shard_map/ppermute | solution.py:557
  43.4 5.3 %collective-permute-start.20 = (bf16[160,512]{1,0:T(8,128)(2,1)S(1)}, bf16[160,512]{1,0:T(8,128)(2,1)S(1)}, u32[]{:S(2)}, u32[]{:S(2)}) collective-permute-start(bf16[160,512]{1,0:T(8,128)(2,1)S(1)} %collective-permute-done.19.refs_16_), channel_id=1, source_target_pairs={{4,0},{8,4},{12,8},{14,12},{10,14},{6,10},{2,6},{0,2},{5,1},{9,5},... | collective-permute-start | bytes 491528 | tf_op jit(solution)/shard_map/ppermute | solution.py:557
  44.9 10.9 %collective-permute-start.8 = (bf16[256,512]{1,0:T(8,128)(2,1)S(1)}, bf16[256,512]{1,0:T(8,128)(2,1)S(1)}, u32[]{:S(2)}, u32[]{:S(2)}) collective-permute-start(bf16[256,512]{1,0:T(8,128)(2,1)S(1)} %collective-permute-done.7.refs_18_), channel_id=1, source_target_pairs={{4,0},{8,4},{12,8},{14,12},{10,14},{6,10},{2,6},{0,2},{5,1},{9,5},... | collective-permute-start | bytes 786440 | tf_op jit(solution)/shard_map/ppermute | solution.py:557
  46.4 9.4 %collective-permute-start.17 = (bf16[256,512]{1,0:T(8,128)(2,1)S(1)}, bf16[256,512]{1,0:T(8,128)(2,1)S(1)}, u32[]{:S(2)}, u32[]{:S(2)}) collective-permute-start(bf16[256,512]{1,0:T(8,128)(2,1)S(1)} %collective-permute-done.16.refs_15_), channel_id=1, source_target_pairs={{0,4},{4,8},{8,12},{12,14},{14,10},{10,6},{6,2},{2,0},{1,5},{5,9},... | collective-permute-start | bytes 786440 | tf_op jit(solution)/shard_map/ppermute | solution.py:557
  48.7 5.4 %collective-permute-start.14 = (bf16[160,512]{1,0:T(8,128)(2,1)S(1)}, bf16[160,512]{1,0:T(8,128)(2,1)S(1)}, u32[]{:S(2)}, u32[]{:S(2)}) collective-permute-start(bf16[160,512]{1,0:T(8,128)(2,1)S(1)} %collective-permute-done.3.refs_4_), channel_id=1, source_target_pairs={{0,16},{16,0},{1,17},{17,1},{2,18},{18,2},{3,19},{19,3},{4,20},{20... | collective-permute-start | bytes 491528 | tf_op jit(solution)/shard_map/ppermute | solution.py:560
  50.2 5.6 %collective-permute-start.21 = (bf16[160,512]{1,0:T(8,128)(2,1)S(1)}, bf16[160,512]{1,0:T(8,128)(2,1)S(1)}, u32[]{:S(2)}, u32[]{:S(2)}) collective-permute-start(bf16[160,512]{1,0:T(8,128)(2,1)S(1)} %collective-permute-done.20.refs_7_), channel_id=1, source_target_pairs={{0,16},{16,0},{1,17},{17,1},{2,18},{18,2},{3,19},{19,3},{4,20},{20... | collective-permute-start | bytes 491528 | tf_op jit(solution)/shard_map/ppermute | solution.py:560
  57.6 18.4 %collective-permute-start.26 = (f32[352,512]{1,0:T(8,128)S(1)}, f32[352,512]{1,0:T(8,128)S(1)}, u32[]{:S(2)}, u32[]{:S(2)}) collective-permute-start(f32[352,512]{1,0:T(8,128)S(1)} %get-tuple-element.53), channel_id=1, source_target_pairs={{0,1},{1,0},{2,3},{3,2},{4,5},{5,4},{6,7},{7,6},{8,9},{9,8},{10,11... | collective-permute-start | bytes 2162696 | tf_op jit(solution)/shard_map/ppermute | solution.py:516
  57.6 9.3 %collective-permute-start.9 = (bf16[256,512]{1,0:T(8,128)(2,1)S(1)}, bf16[256,512]{1,0:T(8,128)(2,1)S(1)}, u32[]{:S(2)}, u32[]{:S(2)}) collective-permute-start(bf16[256,512]{1,0:T(8,128)(2,1)S(1)} %collective-permute-done.8.refs_9_), channel_id=1, source_target_pairs={{4,0},{8,4},{12,8},{14,12},{10,14},{6,10},{2,6},{0,2},{5,1},{9,5},... | collective-permute-start | bytes 786440 | tf_op jit(solution)/shard_map/ppermute | solution.py:557
  59.1 6.3 %collective-permute-start.4 = (bf16[160,512]{1,0:T(8,128)(2,1)S(1)}, bf16[160,512]{1,0:T(8,128)(2,1)S(1)}, u32[]{:S(2)}, u32[]{:S(2)}) collective-permute-start(bf16[160,512]{1,0:T(8,128)(2,1)S(1)} %collective-permute-done.3.refs_4_), channel_id=1, source_target_pairs={{0,4},{4,8},{8,12},{12,14},{14,10},{10,6},{6,2},{2,0},{1,5},{5,9},... | collective-permute-start | bytes 491528 | tf_op jit(solution)/shard_map/ppermute | solution.py:557
  65.4 5.4 %collective-permute-start.5 = (bf16[160,512]{1,0:T(8,128)(2,1)S(1)}, bf16[160,512]{1,0:T(8,128)(2,1)S(1)}, u32[]{:S(2)}, u32[]{:S(2)}) collective-permute-start(bf16[160,512]{1,0:T(8,128)(2,1)S(1)} %collective-permute-done.4.refs_2_), channel_id=1, source_target_pairs={{0,16},{16,0},{1,17},{17,1},{2,18},{18,2},{3,19},{19,3},{4,20},{20... | collective-permute-start | bytes 491528 | tf_op jit(solution)/shard_map/ppermute | solution.py:560
  66.9 9.0 %collective-permute-start.12 = (bf16[256,512]{1,0:T(8,128)(2,1)S(1)}, bf16[256,512]{1,0:T(8,128)(2,1)S(1)}, u32[]{:S(2)}, u32[]{:S(2)}) collective-permute-start(bf16[256,512]{1,0:T(8,128)(2,1)S(1)} %collective-permute-done.9.refs_4_), channel_id=1, source_target_pairs={{0,1},{1,0},{2,3},{3,2},{4,5},{5,4},{6,7},{7,6},{8,9},{9,8},{10,11... | collective-permute-start | bytes 786440 | tf_op jit(solution)/shard_map/ppermute | solution.py:516
  69.8 6.1 %collective-permute-start.10 = (bf16[160,512]{1,0:T(8,128)(2,1)S(1)}, bf16[160,512]{1,0:T(8,128)(2,1)S(1)}, u32[]{:S(2)}, u32[]{:S(2)}) collective-permute-start(bf16[160,512]{1,0:T(8,128)(2,1)S(1)} %collective-permute-done.4.refs_2_), channel_id=1, source_target_pairs={{0,1},{1,0},{2,3},{3,2},{4,5},{5,4},{6,7},{7,6},{8,9},{9,8},{10,11... | collective-permute-start | bytes 491528 | tf_op jit(solution)/shard_map/ppermute | solution.py:516
  70.8 5.1 %collective-permute-start.11 = (bf16[160,512]{1,0:T(8,128)(2,1)S(1)}, bf16[160,512]{1,0:T(8,128)(2,1)S(1)}, u32[]{:S(2)}, u32[]{:S(2)}) collective-permute-start(bf16[160,512]{1,0:T(8,128)(2,1)S(1)} %collective-permute-done.5.refs_3_), channel_id=1, source_target_pairs={{0,1},{1,0},{2,3},{3,2},{4,5},{5,4},{6,7},{7,6},{8,9},{9,8},{10,11... | collective-permute-start | bytes 491528 | tf_op jit(solution)/shard_map/ppermute | solution.py:516
  74.3 32.1 %collective-permute-start.41 = (bf16[128,2048]{1,0:T(8,128)(2,1)S(1)}, bf16[128,2048]{1,0:T(8,128)(2,1)S(1)}, u32[]{:S(2)}, u32[]{:S(2)}) collective-permute-start(bf16[128,2048]{1,0:T(8,128)(2,1)S(1)} %shard_map.152), channel_id=1, source_target_pairs={{0,2},{2,0},{4,6},{6,4},{8,10},{10,8},{12,14},{14,12},{1,3},{3,1},... | collective-permute-start | bytes 1572872 | tf_op jit(solution)/shard_map/ppermute | solution.py:519
  78.4 1.5 %collective-permute-start.28 = (f32[64,512]{1,0:T(8,128)S(1)}, f32[64,512]{1,0:T(8,128)S(1)}, u32[]{:S(2)}, u32[]{:S(2)}) collective-permute-start(f32[64,512]{1,0:T(8,128)S(1)} %get-tuple-element.67.refs_4_), channel_id=1, source_target_pairs={{0,1},{1,0},{2,3},{3,2},{4,5},{5,4},{6,7},{7,6},{8,9},{9,8},{10,11... | collective-permute-start | bytes 393224 | tf_op jit(solution)/shard_map/ppermute | solution.py:516
  78.6 1.2 collective-permute-start.27
  80.9 11.1 %collective-permute-start.32 = (bf16[72,512]{1,0:T(8,128)(2,1)S(1)}, bf16[72,512]{1,0:T(8,128)(2,1)S(1)}, u32[]{:S(2)}, u32[]{:S(2)}) collective-permute-start(bf16[72,512]{1,0:T(8,128)(2,1)S(1)} %get-tuple-element.73), channel_id=1, source_target_pairs={{0,8},{2,10},{4,12},{6,14},{8,0},{10,2},{12,4},{14,6},{1,9},{3,11}... | collective-permute-start | bytes 221192 | tf_op jit(solution)/shard_map/ppermute | solution.py:519
  84.2 10.9 %collective-permute-start.33 = (bf16[72,512]{1,0:T(8,128)(2,1)S(1)}, bf16[72,512]{1,0:T(8,128)(2,1)S(1)}, u32[]{:S(2)}, u32[]{:S(2)}) collective-permute-start(bf16[72,512]{1,0:T(8,128)(2,1)S(1)} %get-tuple-element.74), channel_id=1, source_target_pairs={{0,10},{2,8},{4,14},{6,12},{8,2},{10,0},{12,6},{14,4},{1,11},{3,9}... | collective-permute-start | bytes 221192 | tf_op jit(solution)/shard_map/ppermute | solution.py:519
  84.2 11.1 %collective-permute-start.34 = (bf16[72,512]{1,0:T(8,128)(2,1)S(1)}, bf16[72,512]{1,0:T(8,128)(2,1)S(1)}, u32[]{:S(2)}, u32[]{:S(2)}) collective-permute-start(bf16[72,512]{1,0:T(8,128)(2,1)S(1)} %get-tuple-element.75), channel_id=1, source_target_pairs={{0,12},{2,14},{4,8},{6,10},{8,4},{10,6},{12,0},{14,2},{1,13},{3,15... | collective-permute-start | bytes 221192 | tf_op jit(solution)/shard_map/ppermute | solution.py:519
  87.1 11.0 %collective-permute-start.35 = (bf16[72,512]{1,0:T(8,128)(2,1)S(1)}, bf16[72,512]{1,0:T(8,128)(2,1)S(1)}, u32[]{:S(2)}, u32[]{:S(2)}) collective-permute-start(bf16[72,512]{1,0:T(8,128)(2,1)S(1)} %get-tuple-element.76), channel_id=1, source_target_pairs={{0,14},{2,12},{4,10},{6,8},{8,6},{10,4},{12,2},{14,0},{1,15},{3,13... | collective-permute-start | bytes 221192 | tf_op jit(solution)/shard_map/ppermute | solution.py:519
  90.1 26.3 %copy-start.6 = (bf16[1,64,4096]{2,1,0:T(8,128)(2,1)S(1)}, bf16[1,64,4096]{2,1,0:T(8,128)(2,1)}, u32[]{:S(2)}) copy-start(bf16[1,64,4096]{2,1,0:T(8,128)(2,1)} %param.21) | copy-start | bytes 1572868
  92.0 6.1 %collective-permute-start.29 = (bf16[72,512]{1,0:T(8,128)(2,1)S(1)}, bf16[72,512]{1,0:T(8,128)(2,1)S(1)}, u32[]{:S(2)}, u32[]{:S(2)}) collective-permute-start(bf16[72,512]{1,0:T(8,128)(2,1)S(1)} %get-tuple-element.70), channel_id=1, source_target_pairs={{0,2},{2,0},{4,6},{6,4},{8,10},{10,8},{12,14},{14,12},{1,3},{3,1},... | collective-permute-start | bytes 221192 | tf_op jit(solution)/shard_map/ppermute | solution.py:519
  95.1 4.7 %collective-permute-start.30 = (bf16[72,512]{1,0:T(8,128)(2,1)S(1)}, bf16[72,512]{1,0:T(8,128)(2,1)S(1)}, u32[]{:S(2)}, u32[]{:S(2)}) collective-permute-start(bf16[72,512]{1,0:T(8,128)(2,1)S(1)} %get-tuple-element.71), channel_id=1, source_target_pairs={{0,4},{2,6},{4,0},{6,2},{8,12},{10,14},{12,8},{14,10},{1,5},{3,7},... | collective-permute-start | bytes 221192 | tf_op jit(solution)/shard_map/ppermute | solution.py:519
  95.4 6.0 %collective-permute-start.31 = (bf16[72,512]{1,0:T(8,128)(2,1)S(1)}, bf16[72,512]{1,0:T(8,128)(2,1)S(1)}, u32[]{:S(2)}, u32[]{:S(2)}) collective-permute-start(bf16[72,512]{1,0:T(8,128)(2,1)S(1)} %get-tuple-element.72), channel_id=1, source_target_pairs={{0,6},{2,4},{4,2},{6,0},{8,14},{10,12},{12,10},{14,8},{1,7},{3,5},... | collective-permute-start | bytes 221192 | tf_op jit(solution)/shard_map/ppermute | solution.py:519
  102.0 4.8 %collective-permute-start.37 = (bf16[80,512]{1,0:T(8,128)(2,1)S(1)}, bf16[80,512]{1,0:T(8,128)(2,1)S(1)}, u32[]{:S(2)}, u32[]{:S(2)}) collective-permute-start(bf16[80,512]{1,0:T(8,128)(2,1)S(1)} %get-tuple-element.78.refs_0_.refs_3_), channel_id=1, source_target_pairs={{0,4},{2,6},{4,0},{6,2},{8,12},{10,14},{12,8},{14,10},{1,5},{3,7},... | collective-permute-start | bytes 245768 | tf_op jit(solution)/shard_map/ppermute | solution.py:519
  103.3 7.3 %collective-permute-start.38 = (bf16[80,512]{1,0:T(8,128)(2,1)S(1)}, bf16[80,512]{1,0:T(8,128)(2,1)S(1)}, u32[]{:S(2)}, u32[]{:S(2)}) collective-permute-start(bf16[80,512]{1,0:T(8,128)(2,1)S(1)} %get-tuple-element.78.refs_0_.refs_3_), channel_id=1, source_target_pairs={{0,8},{2,10},{4,12},{6,14},{8,0},{10,2},{12,4},{14,6},{1,9},{3,11}... | collective-permute-start | bytes 245768 | tf_op jit(solution)/shard_map/ppermute | solution.py:519
  105.5 6.3 %collective-permute-start.39 = (bf16[80,512]{1,0:T(8,128)(2,1)S(1)}, bf16[80,512]{1,0:T(8,128)(2,1)S(1)}, u32[]{:S(2)}, u32[]{:S(2)}) collective-permute-start(bf16[80,512]{1,0:T(8,128)(2,1)S(1)} %get-tuple-element.78.refs_0_.refs_3_), channel_id=1, source_target_pairs={{0,12},{2,14},{4,8},{6,10},{8,4},{10,6},{12,0},{14,2},{1,13},{3,15... | collective-permute-start | bytes 245768 | tf_op jit(solution)/shard_map/ppermute | solution.py:519
  106.4 11.7 %collective-permute-start.36 = (f32[64,512]{1,0:T(8,128)S(1)}, f32[64,512]{1,0:T(8,128)S(1)}, u32[]{:S(2)}, u32[]{:S(2)}) collective-permute-start(f32[64,512]{1,0:T(8,128)S(1)} %get-tuple-element.77.refs_0_), channel_id=1, source_target_pairs={{0,1},{1,0},{2,3},{3,2},{4,5},{5,4},{6,7},{7,6},{8,9},{9,8},{10,11... | collective-permute-start | bytes 393224 | tf_op jit(solution)/shard_map/ppermute | solution.py:516
  112.8 8.4 %collective-permute-start.42 = (f32[64,64]{1,0:T(8,128)S(1)}, f32[64,64]{1,0:T(8,128)S(1)}, u32[]{:S(2)}, u32[]{:S(2)}) collective-permute-start(f32[64,64]{1,0:T(8,128)S(1)} %get-tuple-element.84), channel_id=1, source_target_pairs={{0,2},{2,0},{4,6},{6,4},{8,10},{10,8},{12,14},{14,12},{1,3},{3,1},... | collective-permute-start | bytes 49160 | tf_op jit(solution)/shard_map/ppermute | solution.py:519
  113.6 7.6 %collective-permute-start.43 = (f32[64,64]{1,0:T(8,128)S(1)}, f32[64,64]{1,0:T(8,128)S(1)}, u32[]{:S(2)}, u32[]{:S(2)}) collective-permute-start(f32[64,64]{1,0:T(8,128)S(1)} %get-tuple-element.85), channel_id=1, source_target_pairs={{0,3},{1,2},{2,1},{3,0},{4,7},{5,6},{6,5},{7,4},{8,11},{9,10},{10,... | collective-permute-start | bytes 49160 | tf_op jit(solution)/shard_map/ppermute | solution.py:622
  113.6 7.6 %collective-permute-start.44 = (f32[64,64]{1,0:T(8,128)S(1)}, f32[64,64]{1,0:T(8,128)S(1)}, u32[]{:S(2)}, u32[]{:S(2)}) collective-permute-start(f32[64,64]{1,0:T(8,128)S(1)} %get-tuple-element.86), channel_id=1, source_target_pairs={{0,1},{1,0},{2,3},{3,2},{4,5},{5,4},{6,7},{7,6},{8,9},{9,8},{10,11... | collective-permute-start | bytes 49160 | tf_op jit(solution)/shard_map/ppermute | solution.py:516
  115.6 4.3 %collective-permute-start.40 = (f32[32,512]{1,0:T(8,128)S(1)}, f32[32,512]{1,0:T(8,128)S(1)}, u32[]{:S(2)}, u32[]{:S(2)}) collective-permute-start(f32[32,512]{1,0:T(8,128)S(1)} %shard_map.149.refs_2_), channel_id=1, source_target_pairs={{0,2},{2,0},{4,6},{6,4},{8,10},{10,8},{12,14},{14,12},{1,3},{3,1},... | collective-permute-start | bytes 196616 | tf_op jit(solution)/shard_map/ppermute | solution.py:519
  (8 other events, 113.6 us)
